TPU v7x, 32 devices: a whole 2x2x4 slice. The times are simulated.
32 devices in a mesh: seq: 2 (over x), mp: 16 (over z, y, core).
Axes of the slice: x: 2, y: 2, z: 4, core: 2. Of those that a mesh axis runs over, the one named last changes fastest.
Arguments:
- tokens: bfloat16 [4096, 2048], P(('seq', 'mp')), may hold values from -6 to 6
- lengths: int32 [2, 3], P('seq'), may hold values from 1 to 1536, 2048 in all within a row
- norm_gains: float32 [2, 2048], replicated, may hold values from 0.5 to 1.5
- norm_biases: float32 [2, 2048], replicated, may hold values from -2 to 2
- w_query: bfloat16 [2048, 2048], P(None, 'mp'), may hold values from -0.125 to 0.125
- w_key: bfloat16 [2048, 2048], P(None, 'mp'), may hold values from -0.125 to 0.125
- w_value: bfloat16 [2048, 4096], P(None, 'mp'), may hold values from -0.125 to 0.125
- w_gate: bfloat16 [2048, 4096], P(None, 'mp'), may hold values from -0.125 to 0.125
- w_out: bfloat16 [4096, 2048], P('mp'), may hold values from -0.125 to 0.125
- w_up: bfloat16 [2048, 4096], P(None, 'mp'), may hold values from -0.125 to 0.125
- w_down: bfloat16 [4096, 2048], P('mp'), may hold values from -0.125 to 0.125
- out_grad: bfloat16 [4096, 2048], P(('seq', 'mp')), may hold values from -6 to 6
Outputs:
- layer_out: float32 [4096, 2048], P(('seq', 'mp'))
- tokens_grad: float32 [4096, 2048], P(('seq', 'mp'))
- query_grad: float32 [2048, 2048], P(None, 'mp')
- key_grad: float32 [2048, 2048], P(None, 'mp')
- value_grad: float32 [2048, 4096], P(None, 'mp')
- gate_grad: float32 [2048, 4096], P(None, 'mp')
- out_weight_grad: float32 [4096, 2048], P('mp')
- up_grad: float32 [2048, 4096], P(None, 'mp')
- down_grad: float32 [4096, 2048], P('mp')
- gains_grad: float32 [2, 2048], P(None, 'mp')
- biases_grad: float32 [2, 2048], P(None, 'mp')
Inputs may be any that keep to these rules, and one draw needn't show every extreme that they name: Each row of lengths lists the 3 sequences of one group in order; they sum to 2048 and the longest is exactly 1536.
All inputs are finite; a program needn't handle non-finite values.
Results may differ from a plain program's by a relative error of at most 0.017.
Values may be sent and summed in bfloat16 or wider, within the bound.
No kernel may reach another device: no remote copies, remote signals or barrier semaphores. Data moves between devices by JAX's collectives and lax.ppermute only.
A program may use at most 576 MiB of HBM per device.

v0:
```python
import jax
import jax.numpy as jnp
from jax import lax
from jax.sharding import PartitionSpec as P

HEADS = 8
KEY = 256
VAL = 512
SPAN = 512


highest = lax.Precision.HIGHEST
epsilon = 1e-05
group_epsilon = 0.25


def shifted(value, axis, by):
    peers = lax.axis_size(axis)
    return lax.ppermute(value, axis, [(i, (i + by) % peers) for i in range(peers)])


def contract(left_side, right_side, left_dim, right_dim):
    return lax.dot_general(
        left_side,
        right_side,
        (((left_dim,), (right_dim,)), ((), ())),
        preferred_element_type=jnp.float32,
    )


def normalize(values, norm_gain, norm_bias):
    average = jnp.mean(values, axis=-1, keepdims=True)
    centered = values - average
    variance = jnp.mean(centered * centered, axis=-1, keepdims=True)
    inverse = lax.rsqrt(variance + epsilon)
    unit_rows = centered * inverse
    return (unit_rows * norm_gain + norm_bias, unit_rows, inverse)


def normalize_back(grad_normed, unit_rows, inverse, norm_gain):
    scaled = grad_normed * norm_gain
    plain_mean = jnp.mean(scaled, axis=-1, keepdims=True)
    cross_mean = jnp.mean(scaled * unit_rows, axis=-1, keepdims=True)
    return inverse * (scaled - plain_mean - unit_rows * cross_mean)


def sequence_info(lengths_row, group_rows):
    sequence_ends = jnp.cumsum(lengths_row, dtype=jnp.int32)
    sequence_starts = sequence_ends - lengths_row
    row_ids = jnp.arange(group_rows, dtype=jnp.int32)
    member = (row_ids[:, None] >= sequence_starts[None, :]) & (
        row_ids[:, None] < sequence_ends[None, :]
    )
    labels = jnp.arange(lengths_row.shape[0], dtype=jnp.int32)
    zero_int = jnp.zeros((), jnp.int32)
    segment = jnp.sum(jnp.where(member, labels[None, :], zero_int), axis=1, dtype=jnp.int32)
    begins = jnp.sum(jnp.where(member, sequence_starts[None, :], zero_int), axis=1, dtype=jnp.int32)
    position = row_ids - begins
    return (segment, position)


def rotate(values, position, direction):
    half_width = values.shape[-1] // 2
    frequencies = 10000.0 ** (-jnp.arange(half_width).astype(jnp.float32) / half_width)
    angles = position.astype(jnp.float32)[:, None] * frequencies[None, :]
    cosine = jnp.cos(angles)
    sine_part = direction * jnp.sin(angles)
    paired = values.reshape(values.shape[0], half_width, 2)
    even_part = paired[:, :, 0]
    odd_part = paired[:, :, 1]
    turned = jnp.stack(
        [even_part * cosine - odd_part * sine_part, even_part * sine_part + odd_part * cosine],
        axis=-1,
    )
    return turned.reshape(values.shape)


def span_masks(segment_part, previous, log_decay):
    offsets = jnp.arange(SPAN, dtype=jnp.int32)
    distance = offsets[:, None] - offsets[None, :]
    same_sequence = (distance >= 0) & (segment_part[:, None] == segment_part[None, :])
    safe_distance = jnp.where(same_sequence, distance, jnp.zeros_like(distance)).astype(jnp.float32)
    decayed = jnp.exp(safe_distance * log_decay)
    weights = jnp.where(same_sequence, decayed, jnp.zeros_like(decayed))
    carry_decay = jnp.exp((offsets + 1).astype(jnp.float32) * log_decay)
    carried = jnp.where(segment_part == previous, carry_decay, jnp.zeros_like(carry_decay))
    last_segment = segment_part[-1]
    block_decay = jnp.exp(jnp.float32(SPAN) * log_decay)
    keep_factor = jnp.where(previous == last_segment, block_decay, jnp.zeros_like(block_decay))
    fresh_decay = jnp.exp((SPAN - 1 - offsets).astype(jnp.float32) * log_decay)
    fresh_weights = jnp.where(
        segment_part == last_segment, fresh_decay, jnp.zeros_like(fresh_decay)
    )
    return (weights, carried, keep_factor, fresh_weights, last_segment)


def retain_forward(queries, key_rows, value_rows, segment, log_decay):
    group_rows, columns = value_rows.shape
    blocks = group_rows // SPAN

    def advance(carry_pair, inputs):
        carry_state, previous = carry_pair
        query_part, key_part, value_part, segment_part = inputs
        weights, carried, keep_factor, fresh_weights, last_segment = span_masks(
            segment_part, previous, log_decay
        )
        scores = contract(query_part, key_part, 1, 1)
        intra_weights = (scores * weights).astype(jnp.bfloat16)
        inner_part = jnp.dot(intra_weights, value_part, preferred_element_type=jnp.float32)
        outer_part = jnp.dot(
            query_part.astype(jnp.float32) * carried[:, None], carry_state, precision=highest
        )
        update = jnp.dot(
            (key_part.astype(jnp.float32) * fresh_weights[:, None]).T,
            value_part.astype(jnp.float32),
            precision=highest,
        )
        return (
            (keep_factor * carry_state + update, last_segment),
            (inner_part + outer_part, carry_state, previous),
        )

    start_pair = (jnp.zeros((queries.shape[1], columns), jnp.float32), jnp.full((), -1, jnp.int32))
    inputs = (
        queries.reshape(blocks, SPAN, -1),
        key_rows.reshape(blocks, SPAN, -1),
        value_rows.reshape(blocks, SPAN, columns),
        segment.reshape(blocks, SPAN),
    )
    unused, (outputs, states, previous_ids) = lax.scan(advance, start_pair, inputs)
    return (outputs.reshape(group_rows, columns), states, previous_ids)


def retain_backward(
    queries, key_rows, value_rows, segment, log_decay, states, previous_ids, grad_retained
):
    group_rows, columns = value_rows.shape
    blocks = group_rows // SPAN

    def retreat(grad_state, inputs):
        query_part, key_part, value_part, segment_part, carry_state, previous, grad_part = inputs
        weights, carried, keep_factor, fresh_weights, last_segment = span_masks(
            segment_part, previous, log_decay
        )
        scores = contract(query_part, key_part, 1, 1)
        intra_weights = (scores * weights).astype(jnp.bfloat16)
        grad_value = contract(intra_weights, grad_part, 0, 0)
        grad_intra = contract(grad_part, value_part, 1, 1)
        grad_scores = (grad_intra * weights).astype(jnp.bfloat16)
        grad_query = jnp.dot(grad_scores, key_part, preferred_element_type=jnp.float32)
        grad_key = contract(grad_scores, query_part, 0, 0)
        grad_float = grad_part.astype(jnp.float32)
        grad_query = grad_query + carried[:, None] * jnp.dot(
            grad_float, carry_state.T, precision=highest
        )
        grad_key = grad_key + fresh_weights[:, None] * jnp.dot(
            value_part.astype(jnp.float32), grad_state.T, precision=highest
        )
        grad_value = grad_value + jnp.dot(
            key_part.astype(jnp.float32) * fresh_weights[:, None], grad_state, precision=highest
        )
        grad_before = keep_factor * grad_state + jnp.dot(
            (query_part.astype(jnp.float32) * carried[:, None]).T, grad_float, precision=highest
        )
        return (grad_before, (grad_query, grad_key, grad_value))

    inputs = (
        queries.reshape(blocks, SPAN, -1),
        key_rows.reshape(blocks, SPAN, -1),
        value_rows.reshape(blocks, SPAN, columns),
        segment.reshape(blocks, SPAN),
        states,
        previous_ids,
        grad_retained.reshape(blocks, SPAN, columns),
    )
    start_grad = jnp.zeros((queries.shape[1], columns), jnp.float32)
    unused, (grad_query, grad_key, grad_value) = lax.scan(retreat, start_grad, inputs, reverse=True)
    return (
        grad_query.reshape(group_rows, -1),
        grad_key.reshape(group_rows, -1),
        grad_value.reshape(group_rows, columns),
    )


def gelu_slope(hidden):
    cumulative = 0.5 * (1.0 + lax.erf(hidden * 0.7071067811865476))
    density = jnp.exp(-0.5 * hidden * hidden) * 0.3989422804014327
    return cumulative + hidden * density


def local(
    tokens,
    lengths,
    norm_gains,
    norm_biases,
    w_query,
    w_key,
    w_value,
    w_gate,
    w_out,
    w_up,
    w_down,
    out_grad,
):
    mp_size = lax.axis_size("mp")
    mp_index = lax.axis_index("mp")
    per_head = mp_size // HEADS
    head_index = mp_index // per_head
    local_spot = mp_index % per_head
    local_rows = tokens.shape[0]
    group_rows = local_rows * mp_size
    key_scale = KEY ** (-0.5)
    offsets_list = list(range(1, per_head)) + list(range(1 - per_head, 0))

    def gather_rows(row_block):
        return lax.all_gather(row_block, "mp", axis=0, tiled=True)

    def sum_rows(term_maker):
        return lax.psum_scatter(
            term_maker(jnp.int32(0), local_rows * lax.axis_size("mp")),
            "mp",
            scatter_dimension=0,
            tiled=True,
        )

    def head_sums(plain_sum, cross_sum):
        sum_pair = jnp.stack([plain_sum, cross_sum])
        total = sum_pair
        for offset in offsets_list:
            arrived = shifted(sum_pair.astype(jnp.bfloat16), "mp", offset).astype(sum_pair.dtype)
            spot = local_spot - offset
            valid = (spot >= 0) & (spot < per_head)
            total = total + jnp.where(valid, arrived, jnp.zeros_like(arrived))
        return (total[0], total[1])

    segment, position = sequence_info(lengths[0], group_rows)
    log_decay = jnp.log(1.0 - 2.0 ** (-5.0 - head_index.astype(jnp.float32)))
    residual = tokens.astype(jnp.float32)
    normed_one, unit_one, inverse_one = normalize(residual, norm_gains[0], norm_biases[0])
    rows_one = gather_rows(normed_one.astype(jnp.bfloat16))
    shard_pair = jnp.stack([w_query, w_key])
    width = shard_pair.shape[2]
    assembled = jnp.zeros((2, shard_pair.shape[1], per_head * width), shard_pair.dtype)
    assembled = lax.dynamic_update_slice(assembled, shard_pair, (0, 0, local_spot * width))
    for offset in offsets_list:
        arrived = shifted(shard_pair, "mp", offset)
        spot = local_spot - offset
        valid = (spot >= 0) & (spot < per_head)
        placed = lax.dynamic_update_slice(
            assembled, arrived, (0, 0, jnp.clip(spot, 0, per_head - 1) * width)
        )
        assembled = jnp.where(valid, placed, assembled)
    query_head = assembled[0]
    key_head = assembled[1]
    queries = rotate(
        jnp.dot(rows_one, query_head, preferred_element_type=jnp.float32), position, 1.0
    ).astype(jnp.bfloat16)
    key_rows = (
        rotate(jnp.dot(rows_one, key_head, preferred_element_type=jnp.float32), position, 1.0)
        * key_scale
    ).astype(jnp.bfloat16)
    value_rows = jnp.dot(rows_one, w_value, preferred_element_type=jnp.float32).astype(jnp.bfloat16)
    gate_pre = jnp.dot(rows_one, w_gate, preferred_element_type=jnp.float32)
    retained, states, previous_ids = retain_forward(
        queries, key_rows, value_rows, segment, log_decay
    )
    totals, squares = head_sums(jnp.sum(retained, axis=1), jnp.sum(retained * retained, axis=1))
    average = totals / VAL
    inverse_group = lax.rsqrt(squares / VAL - average * average + group_epsilon)
    grouped = (retained - average[:, None]) * inverse_group[:, None]
    swish = jax.nn.silu(gate_pre)
    gated = (swish * grouped).astype(jnp.bfloat16)

    def project_out(first_row, row_count):
        return jnp.dot(gated, w_out, preferred_element_type=jnp.float32)

    middle = residual + sum_rows(project_out)
    normed_two, unit_two, inverse_two = normalize(middle, norm_gains[1], norm_biases[1])
    input_two = normed_two.astype(jnp.bfloat16)
    rows_two = gather_rows(input_two)
    hidden = jnp.dot(rows_two, w_up, preferred_element_type=jnp.float32)
    active = jax.nn.gelu(hidden, approximate=False).astype(jnp.bfloat16)

    def project_down(first_row, row_count):
        return jnp.dot(active, w_down, preferred_element_type=jnp.float32)

    layer_out = middle + sum_rows(project_down)
    grad_rows = gather_rows(out_grad)
    grad_active = contract(grad_rows, w_down, 1, 1)
    down_grad = contract(active, grad_rows, 0, 0)
    grad_hidden = (grad_active * gelu_slope(hidden)).astype(jnp.bfloat16)
    up_grad = contract(rows_two, grad_hidden, 0, 0)

    def back_up(first_row, row_count):
        return contract(grad_hidden, w_up, 1, 1)

    grad_normed_two = sum_rows(back_up)
    grad_middle = out_grad.astype(jnp.float32) + normalize_back(
        grad_normed_two, unit_two, inverse_two, norm_gains[1]
    )
    gain_two = jnp.sum(grad_normed_two * unit_two, axis=0)
    bias_two = jnp.sum(grad_normed_two, axis=0)
    grad_branch = grad_middle.astype(jnp.bfloat16)
    grad_rows_one = gather_rows(grad_branch)
    grad_gated = contract(grad_rows_one, w_out, 1, 1)
    out_weight_grad = contract(gated, grad_rows_one, 0, 0)
    sigmoid = jax.nn.sigmoid(gate_pre)
    grad_gate = (grad_gated * grouped * (sigmoid * (1.0 + gate_pre * (1.0 - sigmoid)))).astype(
        jnp.bfloat16
    )
    grad_grouped = grad_gated * swish
    plain_sum, cross_sum = head_sums(
        jnp.sum(grad_grouped, axis=1), jnp.sum(grad_grouped * grouped, axis=1)
    )
    grad_retained = (
        inverse_group[:, None]
        * (grad_grouped - plain_sum[:, None] / VAL - grouped * cross_sum[:, None] / VAL)
    ).astype(jnp.bfloat16)
    grad_query, grad_key, grad_value = retain_backward(
        queries, key_rows, value_rows, segment, log_decay, states, previous_ids, grad_retained
    )
    grad_query = rotate(grad_query, position, -1.0).astype(jnp.bfloat16)
    grad_key = (rotate(grad_key, position, -1.0) * key_scale).astype(jnp.bfloat16)
    grad_value = grad_value.astype(jnp.bfloat16)
    value_grad = contract(rows_one, grad_value, 0, 0)
    gate_grad = contract(rows_one, grad_gate, 0, 0)
    query_part = contract(rows_one, grad_query, 0, 0)
    key_part = contract(rows_one, grad_key, 0, 0)

    def back_in(first_row, row_count):
        return (
            contract(grad_query, query_head, 1, 1)
            + contract(grad_key, key_head, 1, 1)
            + contract(grad_value, w_value, 1, 1)
            + contract(grad_gate, w_gate, 1, 1)
        )

    grad_normed_one = sum_rows(back_in)
    tokens_grad = grad_middle + normalize_back(
        grad_normed_one, unit_one, inverse_one, norm_gains[0]
    )
    gain_one = jnp.sum(grad_normed_one * unit_one, axis=0)
    bias_one = jnp.sum(grad_normed_one, axis=0)
    grad_pair = jnp.stack([query_part, key_part])
    width = grad_pair.shape[2] // per_head
    total = lax.dynamic_slice_in_dim(grad_pair, local_spot * width, width, 2)
    for offset in offsets_list:
        target = local_spot + offset
        valid = (target >= 0) & (target < per_head)
        piece = lax.dynamic_slice_in_dim(
            grad_pair, jnp.clip(target, 0, per_head - 1) * width, width, 2
        )
        piece = jnp.where(valid, piece, jnp.zeros_like(piece))
        total = total + shifted(piece.astype(jnp.bfloat16), "mp", offset).astype(piece.dtype)
    gains_part = jnp.stack([gain_one, gain_two])
    biases_part = jnp.stack([bias_one, bias_two])
    gains_shard, biases_shard = (
        lax.psum_scatter(gains_part, "mp", scatter_dimension=1, tiled=True),
        lax.psum_scatter(biases_part, "mp", scatter_dimension=1, tiled=True),
    )
    summed = (
        lax.psum(total[0].astype(jnp.bfloat16), "seq").astype(jnp.float32),
        lax.psum(total[1].astype(jnp.bfloat16), "seq").astype(jnp.float32),
        lax.psum(value_grad.astype(jnp.bfloat16), "seq").astype(jnp.float32),
        lax.psum(gate_grad.astype(jnp.bfloat16), "seq").astype(jnp.float32),
        lax.psum(out_weight_grad.astype(jnp.bfloat16), "seq").astype(jnp.float32),
        lax.psum(up_grad.astype(jnp.bfloat16), "seq").astype(jnp.float32),
        lax.psum(down_grad.astype(jnp.bfloat16), "seq").astype(jnp.float32),
        lax.psum(gains_shard.astype(jnp.bfloat16), "seq").astype(jnp.float32),
        lax.psum(biases_shard.astype(jnp.bfloat16), "seq").astype(jnp.float32),
    )
    return (
        layer_out,
        tokens_grad,
        summed[0],
        summed[1],
        summed[2],
        summed[3],
        summed[4],
        summed[5],
        summed[6],
        summed[7],
        summed[8],
    )


def solution(mesh):
    return jax.shard_map(
        local,
        mesh=mesh,
        in_specs=(
            P(("seq", "mp"), None),
            P("seq", None),
            P(),
            P(),
            P(None, "mp"),
            P(None, "mp"),
            P(None, "mp"),
            P(None, "mp"),
            P("mp", None),
            P(None, "mp"),
            P("mp", None),
            P(("seq", "mp"), None),
        ),
        out_specs=(
            P(("seq", "mp"), None),
            P(("seq", "mp"), None),
            P(None, "mp"),
            P(None, "mp"),
            P(None, "mp"),
            P(None, "mp"),
            P("mp", None),
            P(None, "mp"),
            P("mp", None),
            P(None, "mp"),
            P(None, "mp"),
        ),
        check_vma=False,
    )
```

profile of v0, /device:TPU:0, one launch (start us, length us, event | category | flops | bytes accessed | tf_op | source)
XLA Modules:
  0.0 1700.9 jit_solution(8317872682672073393)
XLA Ops:
  16.9 5.0 collective-permute-start.1
  22.4 20.6 %collective-permute-done = bf16[2,2048,128]{2,1,0:T(8,128)(2,1)} collective-permute-done((bf16[2,2048,128]{2,1,0:T(8,128)(2,1)}, bf16[2,2048,128]{2,1,0:T(8,128)(2,1)}, u32[]{:S(2)}, u32[]{:S(2)}) %collective-permute-start) | collective-permute-done | bytes 1048608 | tf_op jit(solution)/shard_map/ppermute | solution.py:19
  50.4 2.6 dot_general.178
  55.2 44.5 %all-gather.5.cloned.1.call-done = bf16[2048,2048]{1,0:T(8,128)(2,1)} async-done(((bf16[128,2048]{1,0:T(8,128)(2,1)}), bf16[2048,2048]{1,0:T(8,128)(2,1)}) %all-gather.5.cloned.1.call-update) | async-done | bytes 8388624 | tf_op jit(solution)/shard_map/all_gather | solution.py:216
  99.8 6.0 fusion.126
  105.8 2.7 fusion.128
  108.5 5.8 fusion.197
  118.5 2.7 fusion.148
  121.2 3.7 copy.61
  129.8 6.9 convolution_convert_fusion.5
  136.7 33.2 %while.44 = (s32[]{:T(128)}, f32[256,256]{1,0:T(8,128)S(1)}, s32[]{:T(128)}, f32[4,512,256]{2,1,0:T(8,128)}, f32[4,256,256]{2,1,0:T(8,128)}, /*index=5*/s32[4]{0...) while((s32[]{:T(128)}, f32[256,256]{1,0:T(8,128)S(1)}, ...), condition=%wide.region_6.7_spmd.clone.clone, body=%wide.region_5.6_spmd.clone.sunk.clone | while | flops 1077351424 | bytes 4479714 | solution.py:130
  175.3 4.4 collective-permute-done.2
  179.8 7.7 multiply_convert_fusion.2
  188.5 8.1 fusion.221
  196.7 175.8 %reduce-scatter.11.cloned.1.call-done = f32[128,2048]{1,0:T(8,128)} async-done(((f32[2048,2048]{1,0:T(8,128)}), f32[128,2048]{1,0:T(8,128)}) %reduce-scatter.11.cloned.1.call-update) | async-done | bytes 1048592 | tf_op jit(solution)/shard_map/reduce_scatter | solution.py:219
  376.0 73.5 %all-gather.7.cloned.1.call-done = bf16[2048,2048]{1,0:T(8,128)(2,1)} async-done(((bf16[128,2048]{1,0:T(8,128)(2,1)}), bf16[2048,2048]{1,0:T(8,128)(2,1)}) %all-gather.7.cloned.1.call-update) | async-done | bytes 8388624 | tf_op jit(solution)/shard_map/all_gather | solution.py:216
  449.5 10.5 fusion.133
  460.1 64.7 %all-gather.9.cloned.1.call-done = bf16[2048,2048]{1,0:T(8,128)(2,1)} async-done(((bf16[128,2048]{1,0:T(8,128)(2,1)}), bf16[2048,2048]{1,0:T(8,128)(2,1)}) %all-gather.9.cloned.1.call-update) | async-done | bytes 8388624 | tf_op jit(solution)/shard_map/all_gather | solution.py:216
  524.7 7.4 fusion.130
  533.1 8.1 fusion.223
  541.2 12.4 fusion.222
  553.9 164.3 %reduce-scatter.15.cloned.1.call-done = f32[128,2048]{1,0:T(8,128)} async-done(((f32[2048,2048]{1,0:T(8,128)}), f32[128,2048]{1,0:T(8,128)}) %reduce-scatter.15.cloned.1.call-update) | async-done | bytes 1048592 | tf_op jit(solution)/shard_map/reduce_scatter | solution.py:219
  720.4 179.3 %reduce-scatter.13.cloned.1.call-done = f32[128,2048]{1,0:T(8,128)} async-done(((f32[2048,2048]{1,0:T(8,128)}), f32[128,2048]{1,0:T(8,128)}) %reduce-scatter.13.cloned.1.call-update) | async-done | bytes 1048592 | tf_op jit(solution)/shard_map/reduce_scatter | solution.py:219
  899.7 3.8 fusion.215
  904.6 7.1 convolution_convert_fusion
  911.7 6.9 convolution_convert_fusion.1
  918.6 59.0 %all-gather.11.cloned.1.call-done = bf16[2048,2048]{1,0:T(8,128)(2,1)} async-done(((bf16[128,2048]{1,0:T(8,128)(2,1)}), bf16[2048,2048]{1,0:T(8,128)(2,1)}) %all-gather.11.cloned.1.call-update) | async-done | bytes 8388624 | tf_op jit(solution)/shard_map/all_gather | solution.py:216
  977.6 8.3 fusion.212
  987.5 7.0 convolution_convert_fusion.3
  994.7 3.0 multiply_convert_fusion.1
  1000.8 154.3 %while.45 = (s32[]{:T(128)}, f32[256,256]{1,0:T(8,128)S(1)}, f32[4,512,256]{1,0,2:T(4,128)}, f32[4,512,256]{1,0,2:T(4,128)}, bf16[4,512,256]{2,1,0:T(8,128)(2,1)...) while((s32[]{:T(128)}, f32[256,256]{1,0:T(8,128)S(1)}, ...), condition=%wide.region_19.20_spmd.clone.clone, body=%wide.region_18.19_spmd.clone.sunk.clone | while | flops 2288456704 | bytes 14976262 | solution.py:177
  1014.8 2.5 fusion.362
  1017.3 11.0 dynamic_update_slice.78
  1028.3 11.0 dynamic_update_slice.77
  1053.3 2.5 fusion.362
  1055.9 11.0 dynamic_update_slice.78
  1066.9 11.0 dynamic_update_slice.77
  1094.5 11.0 dynamic_update_slice.78
  1105.5 11.0 dynamic_update_slice.77
  1133.1 11.0 dynamic_update_slice.78
  1144.1 11.0 dynamic_update_slice.77
  1155.1 3.4 reshape_reshape.7
  1158.5 2.6 fusion.218
  1164.2 4.6 fusion.192
  1169.9 2.7 copy.76
  1173.9 3.3 reshape_reshape.6
  1177.2 4.4 fusion.217
  1183.1 4.7 fusion.190
  1189.4 6.4 convolution_bitcast_fusion
  1195.8 6.2 convolution_bitcast_fusion.1
  1203.0 4.0 collective-permute-start.7
  1207.0 3.3 convolution_convert_fusion.2
  1210.4 3.6 convolution_convert_fusion.4
  1214.0 5.5 collective-permute-done.6
  1221.2 4.1 fusion.225
  1225.3 8.7 fusion.201
  1234.1 8.1 fusion.224
  1242.2 19.1 %add_add_fusion = f32[2048,2048]{1,0:T(8,128)} fusion(f32[2048,2048]{1,0:T(8,128)S(1)} %fusion.225, f32[2048,2048]{1,0:T(8,128)} %fusion.224, f32[2048,2048]{1,0:T(8,128)} %fusion.201, bf16[2048,256]{0,1:T(8,128)(2,1)S(1)} %copy-done.11, bf16[2,2048,256]{2,1,0:T(8,128)(2,1)S(1)} %copy-done.3), kind=kOutput, calls=%fused_computation.131 | convolution fusion | flops 2160066560 | bytes 69206016 | tf_op jit(solution)/shard_map/dot_general | solution.py:23
  1261.3 122.0 %all-reduce.4.cloned.1.call-done = (bf16[2048,128]{1,0:T(8,128)(2,1)}, bf16[2048,128]{1,0:T(8,128)(2,1)}, bf16[2048,256]{1,0:T(8,128)(2,1)}, bf16[2048,256]{1,0:...) async-done(((bf16[2048,128]{1,0:T(8,128)(2,1)}, bf16[2048,128]{1,0:T(8,128)(2,1)}, bf16[2048,256]{1,0:T(8,128)(2,1)}, ...) | async-done | bytes 6291472 | tf_op jit(solution)/shard_map/psum | solution.py:362
  1395.5 171.1 %reduce-scatter.17.cloned.1.call-done = f32[128,2048]{1,0:T(8,128)} async-done(((f32[2048,2048]{1,0:T(8,128)}), f32[128,2048]{1,0:T(8,128)}) %reduce-scatter.17.cloned.1.call-update) | async-done | bytes 1048592 | tf_op jit(solution)/shard_map/reduce_scatter | solution.py:219
  1571.2 2.7 fusion.187
  1574.0 53.0 %reduce-scatter.21.cloned.1.call-done = f32[128,2]{1,0:T(8,128)} async-done(((f32[2048,2]{1,0:T(8,128)}), f32[128,2]{1,0:T(8,128)}) %reduce-scatter.21.cloned.1.call-update) | async-done | bytes 1040
  1627.9 59.1 %reduce-scatter.19.cloned.1.call-done = f32[128,2]{1,0:T(8,128)} async-done(((f32[2048,2]{1,0:T(8,128)}), f32[128,2]{1,0:T(8,128)}) %reduce-scatter.19.cloned.1.call-update) | async-done | bytes 1040
  1687.9 4.9 all-reduce
  (291 shorter events, 161.8 us)
Async XLA Ops:
  7.2 181.4 %copy-start = (bf16[256,2048]{1,0:T(8,128)(2,1)S(1)}, bf16[256,2048]{1,0:T(8,128)(2,1)}, u32[]{:S(2)}) copy-start(bf16[256,2048]{1,0:T(8,128)(2,1)} %param.24) | copy-start | bytes 3145732
  7.2 92.6 %all-gather.5.cloned.1.call-start = ((), (), s32[]{:S(2)}) async-start(), calls=%async_computation.6 | async-start | bytes 8912896 | tf_op jit(solution)/shard_map/all_gather | solution.py:216
  8.5 3.0 copy-start.34
  9.9 1.7 copy-start.36
  10.7 0.8 copy-start.30
  13.8 358.7 %reduce-scatter.11.cloned.1.call-start = ((), (), s32[]{:S(2)}) async-start(), calls=%async_computation.7 | async-start | bytes 17825792 | tf_op jit(solution)/shard_map/reduce_scatter | solution.py:219
  14.0 7.9 copy-start.39
  16.5 26.5 %collective-permute-start = (bf16[2,2048,128]{2,1,0:T(8,128)(2,1)}, bf16[2,2048,128]{2,1,0:T(8,128)(2,1)}, u32[]{:S(2)}, u32[]{:S(2)}) collective-permute-start(bf16[2,2048,128]{2,1,0:T(8,128)(2,1)} %get-tuple-element.688), channel_id=1, source_target_pairs={{0,1},{1,2},{2,3},{3,4},{4,5},{5,6},{6,7},{7,8},{8,9},{9,10},{10,1... | collective-permute-start | bytes 3145736 | tf_op jit(solution)/shard_map/ppermute | solution.py:19
  16.9 27.6 %collective-permute-start.1 = (bf16[2,2048,128]{2,1,0:T(8,128)(2,1)}, bf16[2,2048,128]{2,1,0:T(8,128)(2,1)}, u32[]{:S(2)}, u32[]{:S(2)}) collective-permute-start(bf16[2,2048,128]{2,1,0:T(8,128)(2,1)} %get-tuple-element.688), channel_id=1, source_target_pairs={{0,15},{1,0},{2,1},{3,2},{4,3},{5,4},{6,5},{7,6},{8,7},{9,8},{10,9... | collective-permute-start | bytes 3145736 | tf_op jit(solution)/shard_map/ppermute | solution.py:19
  46.2 2.0 copy-start.2
  50.4 2.6 copy-start.17
  53.7 46.1 %copy-start.28 = (bf16[128,2,2048]{2,1,0:T(2,128)(2,1)S(1)}, bf16[128,2,2048]{2,1,0:T(2,128)(2,1)}, u32[]{:S(2)}) copy-start(bf16[128,2,2048]{2,1,0:T(2,128)(2,1)} %dot_general.178) | copy-start | bytes 3145732
  55.2 50.5 %copy-start.29 = (bf16[128,2,2048]{2,1,0:T(2,128)(2,1)S(1)}, bf16[128,2,2048]{2,1,0:T(2,128)(2,1)}, u32[]{:S(2)}) copy-start(bf16[128,2,2048]{2,1,0:T(2,128)(2,1)} %dot_general.174) | copy-start | bytes 3145732
  99.8 6.0 copy-start.38
  170.0 9.8 copy-start.5
  172.4 2.9 collective-permute-start.3
  174.0 5.8 collective-permute-start.2
  187.5 1.0 copy-start.8
  196.7 252.8 %all-gather.7.cloned.1.call-start = ((), (), s32[]{:S(2)}) async-start(), calls=%async_computation.8 | async-start | bytes 8912896 | tf_op jit(solution)/shard_map/all_gather | solution.py:216
  375.4 149.3 %all-gather.9.cloned.1.call-start = ((), (), s32[]{:S(2)}) async-start(), calls=%async_computation.10 | async-start | bytes 8912896 | tf_op jit(solution)/shard_map/all_gather | solution.py:216
  376.0 342.1 %reduce-scatter.15.cloned.1.call-start = ((), (), s32[]{:S(2)}) async-start(), calls=%async_computation.11 | async-start | bytes 17825792 | tf_op jit(solution)/shard_map/reduce_scatter | solution.py:219
  524.7 8.4 copy-start.18
  532.1 1.0 copy-start.21
  541.2 358.5 %reduce-scatter.13.cloned.1.call-start = ((), (), s32[]{:S(2)}) async-start(), calls=%async_computation.9 | async-start | bytes 17825792 | tf_op jit(solution)/shard_map/reduce_scatter | solution.py:219
  553.6 424.0 %all-gather.11.cloned.1.call-start = ((), (), s32[]{:S(2)}) async-start(), calls=%async_computation.12 | async-start | bytes 8912896 | tf_op jit(solution)/shard_map/all_gather | solution.py:216
  903.6 479.8 %all-reduce.4.cloned.1.call-start = ((), (), s32[]{:S(2)}) async-start(), calls=%async_computation.16 | async-start | bytes 12582912 | tf_op jit(solution)/shard_map/psum | solution.py:362
  904.6 7.1 copy-start.22
  985.9 8.6 copy-start.20
  986.0 8.6 collective-permute-start.5
  987.5 7.0 collective-permute-start.4
  987.5 7.1 copy-start.6
  1169.9 4.0 copy-start.7
  1187.9 1.5 copy-start.12
  1189.3 6.5 copy-start.10
  1189.3 17.7 %slice-start = ((s8[8388608]{0:T(1024)(128)(4,1)}), s8[4194304]{0:T(1024)(128)(4,1)S(1)}, s32[]{:S(2)}) async-start(s8[8388608]{0:T(1024)(128)(4,1)} %bitcast.296), calls=%async_computation.17 | async-start | bytes 8388608
  1195.8 11.2 slice-start.1
  1202.0 5.0 copy-start.9
  1202.4 17.1 %collective-permute-start.6 = (bf16[2,2048,128]{2,1,0:T(8,128)(2,1)S(1)}, bf16[2,2048,128]{2,1,0:T(8,128)(2,1)S(1)}, u32[]{:S(2)}, u32[]{:S(2)}) collective-permute-start(bf16[2,2048,128]{2,1,0:T(8,128)(2,1)S(1)} %get-tuple-element.669), channel_id=1, source_target_pairs={{0,1},{1,2},{2,3},{3,4},{4,5},{5,6},{6,7},{7,8},{8,9},{9,10},{10,1... | collective-permute-start | bytes 3145736 | tf_op jit(solution)/shard_map/ppermute | solution.py:19
  1203.0 7.4 slice-start.2
  1203.0 7.4 copy-start.15
  1203.0 7.4 slice-start.3
  1203.0 16.5 collective-permute-start.7
  1220.9 4.4 copy-start.3
  1220.9 4.4 copy-start.13
  1220.9 345.7 %reduce-scatter.17.cloned.1.call-start = ((), (), s32[]{:S(2)}) async-start(), calls=%async_computation.13 | async-start | bytes 17825792 | tf_op jit(solution)/shard_map/reduce_scatter | solution.py:219
  1225.3 8.8 copy-start.16
  1225.3 8.8 copy-start.19
  1234.1 8.1 copy-start.11
  1261.3 365.7 %reduce-scatter.21.cloned.1.call-start = ((), (), s32[]{:S(2)}) async-start(), calls=%async_computation.15 | async-start | bytes 1114112
  1383.3 4.3 copy-start.27
  1385.5 3.7 copy-start.26
  1389.1 1.6 copy-start.25
  1390.6 1.6 copy-start.24
  1392.3 1.7 copy-start.23
  1393.8 172.8 %copy-start.4 = (bf16[128,2048]{1,0:T(8,128)(2,1)S(1)}, bf16[128,2048]{1,0:T(8,128)(2,1)}, u32[]{:S(2)}) copy-start(bf16[128,2048]{1,0:T(8,128)(2,1)} %param.16) | copy-start | bytes 1572868
  1393.8 172.8 %copy-start.31 = (f32[1,2048]{1,0:T(1,128)S(1)}, f32[1,2048]{1,0:T(1,128)}, u32[]{:S(2)}) copy-start(f32[1,2048]{1,0:T(1,128)} %copy-done.30) | copy-start | bytes 24580
  1393.8 172.8 %copy-start.35 = (f32[128]{0:T(128)S(1)}, f32[128]{0:T(128)}, u32[]{:S(2)}) copy-start(f32[128]{0:T(128)} %copy-done.34) | copy-start | bytes 1540
  1393.8 172.8 %copy-start.37 = (f32[128]{0:T(128)S(1)}, f32[128]{0:T(128)}, u32[]{:S(2)}) copy-start(f32[128]{0:T(128)} %copy-done.36) | copy-start | bytes 1540
  1394.0 174.4 %copy-start.33 = (f32[2048]{0:T(1024)S(1)}, f32[2048]{0:T(1024)}, u32[]{:S(2)}) copy-start(f32[2048]{0:T(1024)} %get-tuple-element.595) | copy-start | bytes 24580
  1395.5 174.3 %copy-start.32 = (f32[2048]{0:T(1024)S(1)}, f32[2048]{0:T(1024)}, u32[]{:S(2)}) copy-start(f32[2048]{0:T(1024)} %get-tuple-element.584) | copy-start | bytes 24580
  1568.3 2.9 copy-start.14
  1569.7 117.3 %reduce-scatter.19.cloned.1.call-start = ((), (), s32[]{:S(2)}) async-start(), calls=%async_computation.14 | async-start | bytes 1114112
  1571.2 122.8 %copy-start.1 = (bf16[256,2048]{1,0:T(8,128)(2,1)S(1)}, bf16[256,2048]{1,0:T(8,128)(2,1)}, u32[]{:S(2)}) copy-start(bf16[256,2048]{1,0:T(8,128)(2,1)} %param.24) | copy-start | bytes 3145732
Sparse Core Ops, SparseCore 0:
  13.9 85.7 all-gather.4
  196.8 175.6 reduce-scatter.10
  375.5 73.9 all-gather.6
  451.5 73.1 all-gather.8
  541.3 176.7 reduce-scatter.14
  722.1 177.5 reduce-scatter.12
  903.7 73.8 all-gather.10
  1221.0 162.2 all-reduce.3
  1388.0 178.5 reduce-scatter.16
  1570.5 56.4 reduce-scatter.20
  1630.6 56.3 reduce-scatter.18
where the time goes:
time: 1710 us; the launch traced here: 1700 us
  waiting for transfers between devices  1200 us (70%)
  matrix products  225 us (13%)
  local copies, waits for them, and re-layouts  157 us (9%)
  other arithmetic  73.4 us (4%)
    reduce_scatter x4, waiting for transfers between devices, sum_rows(): lax.psum_scatter(term_maker(jnp.int32(0), local_rows * lax.axis_size('mp'...  690 us
    all_gather x4, waiting for transfers between devices, gather_rows(): return lax.all_gather(row_block, 'mp', axis=0, tiled=True)  242 us
    psum x1, waiting for transfers between devices, local(): lax.psum(total[0].astype(jnp.bfloat16), 'seq').astype(jnp.float32)  122 us
    dot_general x26, matrix products, contract(): lax.dot_general(left_side, right_side, (((left_dim,), (right_dim,)), ((),...  122 us
    unnamed x13, waiting for transfers between devices  113 us
    dynamic_update_slice x20, local copies, waits for them, and re-layouts, retain_forward(): lax.scan(advance, start_pair, inputs)  91.8 us
  transfers between devices with their start and end apart: 19, of which 16 were waited for; matrix products, arithmetic and copies ran while one was open for 7% of the time, Pallas kernels for 0%

commit v1 on v0

v1 whole, which is shorter than its diff:
```python
import jax
import jax.numpy as jnp
import numpy as np
from jax import lax
from jax.sharding import PartitionSpec as P

HEADS = 8
KEY = 256
VAL = 512

epsilon = 1e-05
group_epsilon = 0.25

RING = tuple(range(0, HEADS, 2)) + tuple(range(HEADS - 1, 0, -2))
ARRIVAL = ((0,), (-1, 1), (-2, 2), (-3, 3), (4,))
OFFSETS = tuple(offset for batch in ARRIVAL for offset in batch)


def contract(left_side, right_side, left_dim, right_dim):
    return lax.dot_general(
        left_side,
        right_side,
        (((left_dim,), (right_dim,)), ((), ())),
        preferred_element_type=jnp.float32,
    )


def row_stats(values):
    average = jnp.mean(values, axis=-1, keepdims=True)
    centered = values - average
    variance = jnp.mean(centered * centered, axis=-1, keepdims=True)
    return average, lax.rsqrt(variance + epsilon)


def normalize_back(grad_normed, unit_rows, inverse, norm_gain):
    scaled = grad_normed * norm_gain
    plain_mean = jnp.mean(scaled, axis=-1, keepdims=True)
    cross_mean = jnp.mean(scaled * unit_rows, axis=-1, keepdims=True)
    return inverse * (scaled - plain_mean - unit_rows * cross_mean)


def gelu_slope(hidden):
    cumulative = 0.5 * (1.0 + lax.erf(hidden * 0.7071067811865476))
    density = jnp.exp(-0.5 * hidden * hidden) * 0.3989422804014327
    return cumulative + hidden * density


def turn(values, cosine, sine):
    half = values.shape[-1] // 2
    even, odd = values[:, :half], values[:, half:]
    return jnp.concatenate([even * cosine - odd * sine, even * sine + odd * cosine], axis=1)


def local(
    tokens,
    lengths,
    norm_gains,
    norm_biases,
    w_query,
    w_key,
    w_value,
    w_gate,
    w_out,
    w_up,
    w_down,
    out_grad,
):
    bf16, f32 = jnp.bfloat16, jnp.float32
    mp_size = lax.axis_size("mp")
    seq_size = lax.axis_size("seq")
    ranks = mp_size // HEADS
    mp_index = lax.axis_index("mp")
    head = mp_index // ranks
    rank = mp_index % ranks
    chunk = tokens.shape[0]
    width = tokens.shape[1]
    half = width // 2
    own_rows = chunk * HEADS
    key_scale = KEY ** (-0.5)

    def ring_shift(value, step):
        pairs = [
            (RING[k] * ranks + r, RING[(k + step) % HEADS] * ranks + r)
            for k in range(HEADS)
            for r in range(ranks)
        ]
        return lax.ppermute(value, "mp", pairs)

    def rank_shift(value, by):
        pairs = [(h * ranks + r, h * ranks + (r + by) % ranks) for h in range(HEADS) for r in range(ranks)]
        return lax.ppermute(value, "mp", pairs)

    def gather_ring(block):
        forth, back = block, block
        batches = [block]
        for _ in range(3):
            forth, back = ring_shift(forth, 1), ring_shift(back, -1)
            batches.append(jnp.concatenate([forth, back], axis=0))
        left = ring_shift(forth[:, :half], 1)
        right = ring_shift(back[:, half:], -1)
        batches.append(jnp.concatenate([left, right], axis=1))
        return batches

    def scatter_ring(parts):
        far = parts[4].astype(bf16)
        forth = ring_shift(far[:, :half], 1).astype(f32)
        back = ring_shift(far[:, half:], -1).astype(f32)
        for at in (3, 2, 1):
            back_part, forth_part = parts[at][:chunk], parts[at][chunk:]
            if at == 3:
                forth = jnp.concatenate([forth_part[:, :half] + forth, forth_part[:, half:]], axis=1)
                back = jnp.concatenate([back_part[:, :half], back_part[:, half:] + back], axis=1)
            else:
                forth = forth_part + forth
                back = back_part + back
            forth = ring_shift(forth.astype(bf16), 1).astype(f32)
            back = ring_shift(back.astype(bf16), -1).astype(f32)
        return parts[0] + forth + back

    def assemble(shard, axis):
        pieces = [shard] + [rank_shift(shard, t) for t in range(1, ranks)]
        ordered = []
        for spot in range(ranks):
            value = pieces[0]
            for t in range(1, ranks):
                value = jnp.where((rank - t + ranks) % ranks == spot, pieces[t], value)
            ordered.append(value)
        return jnp.concatenate(ordered, axis=axis)

    def place(buffer, piece, first):
        return lax.dynamic_update_slice(buffer, piece, (first, 0))

    first_row = []
    at = 0
    for batch in ARRIVAL:
        first_row.append(at)
        at += chunk * len(batch)

    def batch_of(array, at):
        return array[first_row[at] : first_row[at] + chunk * len(ARRIVAL[at])]

    table = np.zeros((HEADS, HEADS), np.int32)
    for k, h in enumerate(RING):
        for j, offset in enumerate(OFFSETS):
            table[h, j] = RING[(k + offset) % HEADS]
    sources = lax.dynamic_slice_in_dim(jnp.asarray(table), head, 1, 0)[0]
    inner = jnp.arange(chunk, dtype=jnp.int32)
    row_ids = jnp.concatenate(
        [
            (((sources * ranks + (rank - t + ranks) % ranks) * chunk)[:, None] + inner[None, :]).reshape(-1)
            for t in range(ranks)
        ]
    )
    ends = jnp.cumsum(lengths[0], dtype=jnp.int32)
    starts = ends - lengths[0]
    member = (row_ids[:, None] >= starts[None, :]) & (row_ids[:, None] < ends[None, :])
    begins = jnp.sum(jnp.where(member, starts[None, :], 0), axis=1, dtype=jnp.int32)
    position = (row_ids - begins)[:own_rows]
    frequencies = 10000.0 ** (-jnp.arange(KEY // 2).astype(f32) / (KEY // 2))
    angles = position.astype(f32)[:, None] * frequencies[None, :]
    cosine, sine = jnp.cos(angles), jnp.sin(angles)
    log_decay = jnp.log(1.0 - 2.0 ** (-5.0 - head.astype(f32)))

    def decay_of(distance, allowed):
        allowed = allowed & (distance >= 0)
        safe = jnp.where(allowed, distance, 0).astype(f32)
        return jnp.where(allowed, jnp.exp(safe * log_decay), 0.0)

    def query_decay(at):
        ids, first = batch_of(row_ids, at), batch_of(begins, at)
        return decay_of(ids[:, None] - row_ids[None, :], row_ids[None, :] >= first[:, None])

    def key_decay(at):
        ids = batch_of(row_ids, at)
        return decay_of(row_ids[None, :] - ids[:, None], ids[:, None] >= begins[None, :])

    with jax.named_scope("gather_tokens"):
        token_batches = gather_ring(tokens)
    with jax.named_scope("head_weights"):
        split = np.zeros((KEY, KEY), np.float32)
        for i in range(KEY // 2):
            split[2 * i, i] = 1.0
            split[2 * i + 1, KEY // 2 + i] = 1.0
        split = jnp.asarray(split, bf16)

        def separate(weight):
            return jnp.dot(weight, split, preferred_element_type=f32).astype(bf16)

        def interleave(grads):
            return contract(grads, split, 1, 1).astype(bf16)

        in_weights = jnp.concatenate(
            [
                separate(assemble(w_query, 1)),
                separate(assemble(w_key, 1)),
                assemble(w_value, 1),
                assemble(w_gate, 1),
            ],
            axis=1,
        )
        out_weight = assemble(w_out, 0)
        up_weight = assemble(w_up, 1)
        down_weight = assemble(w_down, 0)

    all_qkv = jnp.zeros((ranks * own_rows, 2 * KEY + VAL), bf16)
    rows_one = jnp.zeros((own_rows, width), bf16)
    gate_pre, stats_one = [], []
    with jax.named_scope("project_in"):
        for at in range(5):
            raw = token_batches[at].astype(f32)
            average, inverse = row_stats(raw)
            stats_one.append((average, inverse))
            normed = ((raw - average) * inverse * norm_gains[0] + norm_biases[0]).astype(bf16)
            rows_one = place(rows_one, normed, first_row[at])
            out = jnp.dot(normed, in_weights, preferred_element_type=f32)
            c, s = batch_of(cosine, at), batch_of(sine, at)
            qkv = jnp.concatenate(
                [
                    turn(out[:, :KEY], c, s),
                    turn(out[:, KEY : 2 * KEY], c, s) * key_scale,
                    out[:, 2 * KEY : 2 * KEY + VAL],
                ],
                axis=1,
            ).astype(bf16)
            gate_pre.append(out[:, 2 * KEY + VAL :])
            all_qkv = place(all_qkv, qkv, first_row[at])
            for t in range(1, ranks):
                all_qkv = place(all_qkv, rank_shift(qkv, t), t * own_rows + first_row[at])
    all_q, all_k, all_v = all_qkv[:, :KEY], all_qkv[:, KEY : 2 * KEY], all_qkv[:, 2 * KEY :]

    with jax.named_scope("gather_out_grad"):
        grad_batches = gather_ring(lax.optimization_barrier((out_grad, token_batches[4]))[0])

    grouped, inverse_group, swish = [None] * 5, [None] * 5, [None] * 5
    parts = [None] * 5
    gated_rows = [None] * 5
    with jax.named_scope("retention"):
        for at in (4, 3, 2, 1, 0):
            scores = contract(batch_of(all_q, at), all_k, 1, 1)
            intra = (scores * query_decay(at)).astype(bf16)
            retained = jnp.dot(intra, all_v, preferred_element_type=f32)
            average = jnp.mean(retained, axis=1, keepdims=True)
            square = jnp.mean(retained * retained, axis=1, keepdims=True)
            inverse_group[at] = lax.rsqrt(square - average * average + group_epsilon)
            grouped[at] = (retained - average) * inverse_group[at]
            swish[at] = jax.nn.silu(gate_pre[at])
            gated_rows[at] = (swish[at] * grouped[at]).astype(bf16)
            parts[at] = jnp.dot(gated_rows[at], out_weight, preferred_element_type=f32)
    with jax.named_scope("scatter_branch"):
        middle = tokens.astype(f32) + scatter_ring(parts)

    with jax.named_scope("norm_two"):
        average, inverse_two = row_stats(middle)
        unit_two = (middle - average) * inverse_two
        normed_two = (unit_two * norm_gains[1] + norm_biases[1]).astype(bf16)
    with jax.named_scope("gather_two"):
        two_batches = gather_ring(normed_two)
    down_parts, up_parts = [None] * 5, [None] * 5
    active_rows, grad_hidden_rows = [None] * 5, [None] * 5
    with jax.named_scope("feed_forward"):
        for at in range(5):
            hidden = jnp.dot(two_batches[at], up_weight, preferred_element_type=f32)
            active_rows[at] = jax.nn.gelu(hidden, approximate=False).astype(bf16)
            grad_active = contract(grad_batches[at], down_weight, 1, 1)
            grad_hidden_rows[at] = (grad_active * gelu_slope(hidden)).astype(bf16)
            up_parts[at] = contract(grad_hidden_rows[at], up_weight, 1, 1)
            down_parts[at] = jnp.dot(active_rows[at], down_weight, preferred_element_type=f32)
    with jax.named_scope("scatter_up"):
        grad_normed_two = scatter_ring(up_parts)
    with jax.named_scope("norm_two_back"):
        grad_middle = out_grad.astype(f32) + normalize_back(
            grad_normed_two, unit_two, inverse_two, norm_gains[1]
        )
        grad_branch = grad_middle.astype(bf16)
        gain_two = jnp.sum(grad_normed_two * unit_two, axis=0)
        bias_two = jnp.sum(grad_normed_two, axis=0)
    with jax.named_scope("gather_branch"):
        branch_batches = gather_ring(grad_branch)
    with jax.named_scope("scatter_down"):
        gate = lax.optimization_barrier((down_parts[4], grad_branch))[0]
        layer_out = middle + scatter_ring(down_parts[:4] + [gate])

    all_grad = jnp.zeros((ranks * own_rows, VAL), bf16)
    grad_gate, grad_query = [None] * 5, [None] * 5
    with jax.named_scope("retention_back_rows"):
        for at in range(5):
            grad_gated = contract(branch_batches[at], out_weight, 1, 1)
            pre = gate_pre[at]
            sigmoid = jax.nn.sigmoid(pre)
            grad_gate[at] = (
                grad_gated * grouped[at] * (sigmoid * (1.0 + pre * (1.0 - sigmoid)))
            ).astype(bf16)
            grad_grouped = grad_gated * swish[at]
            plain = jnp.mean(grad_grouped, axis=1, keepdims=True)
            cross = jnp.mean(grad_grouped * grouped[at], axis=1, keepdims=True)
            grad_retained = (
                inverse_group[at] * (grad_grouped - plain - grouped[at] * cross)
            ).astype(bf16)
            all_grad = place(all_grad, grad_retained, first_row[at])
            for t in range(1, ranks):
                all_grad = place(all_grad, rank_shift(grad_retained, t), t * own_rows + first_row[at])
            grad_scores = (contract(grad_retained, all_v, 1, 1) * query_decay(at)).astype(bf16)
            turned = jnp.dot(grad_scores, all_k, preferred_element_type=f32)
            grad_query[at] = turn(turned, batch_of(cosine, at), -batch_of(sine, at)).astype(bf16)
    in_parts = [None] * 5
    grad_key, grad_value = [None] * 5, [None] * 5
    gain_one, bias_one = jnp.zeros((width,), f32), jnp.zeros((width,), f32)
    with jax.named_scope("retention_back_columns"):
        for at in (4, 3, 2, 1, 0):
            weights = key_decay(at)
            intra = (contract(batch_of(all_k, at), all_q, 1, 1) * weights).astype(bf16)
            grad_value[at] = jnp.dot(intra, all_grad, preferred_element_type=f32).astype(bf16)
            grad_scores = (contract(batch_of(all_v, at), all_grad, 1, 1) * weights).astype(bf16)
            turned = jnp.dot(grad_scores, all_q, preferred_element_type=f32)
            grad_key[at] = (
                turn(turned, batch_of(cosine, at), -batch_of(sine, at)) * key_scale
            ).astype(bf16)
            grads = jnp.concatenate([grad_query[at], grad_key[at], grad_value[at], grad_gate[at]], axis=1)
            in_parts[at] = contract(grads, in_weights, 1, 1)
            average, inverse = stats_one[at]
            unit = (token_batches[at].astype(f32) - average) * inverse
            gain_one = gain_one + jnp.sum(in_parts[at] * unit, axis=0)
            bias_one = bias_one + jnp.sum(in_parts[at], axis=0)
    with jax.named_scope("scatter_in"):
        grad_normed_one = scatter_ring(in_parts)
    with jax.named_scope("norm_one_back"):
        average, inverse = stats_one[0]
        unit_one = (tokens.astype(f32) - average) * inverse
        tokens_grad = grad_middle + normalize_back(
            grad_normed_one, unit_one, inverse, norm_gains[0]
        )

    with jax.named_scope("norm_grads"):
        norm_sums = jnp.stack([gain_one, gain_two, bias_one, bias_two])
        total = norm_sums
        for t in range(1, ranks):
            total = total + rank_shift(norm_sums, t)
        for bit in (1, 2, 4):
            pairs = [(h * ranks + r, (h ^ bit) * ranks + r) for h in range(HEADS) for r in range(ranks)]
            total = total + lax.ppermute(total, "mp", pairs)
        columns = width // mp_size
        mine = lax.dynamic_slice_in_dim(total, mp_index * columns, columns, 1)

        def sum_groups(value):
            result = value
            for t in range(1, seq_size):
                pairs = [(i, (i + t) % seq_size) for i in range(seq_size)]
                result = result + lax.ppermute(value, "seq", pairs)
            return result

        mine = sum_groups(mine)

    def weight_shard(left, right, sharded_left):
        source = left if sharded_left else right
        size = source.shape[1] // ranks

        def shard(spot):
            cut = lax.dynamic_slice_in_dim(source, spot * size, size, 1)
            return contract(cut, right, 0, 0) if sharded_left else contract(left, cut, 0, 0)

        result = shard(rank)
        for t in range(1, ranks):
            result = result + rank_shift(shard((rank + t) % ranks).astype(bf16), t).astype(f32)
        return sum_groups(result.astype(bf16)).astype(f32)

    def rows(batches):
        return jnp.concatenate(batches, axis=0)

    with jax.named_scope("down_grad"):
        out_grad_rows = rows(grad_batches)
        down_grad = weight_shard(rows(active_rows), out_grad_rows, True)
    with jax.named_scope("up_grad"):
        up_grad = weight_shard(rows(two_batches), rows(grad_hidden_rows), False)
    with jax.named_scope("out_weight_grad"):
        out_weight_grad = weight_shard(rows(gated_rows), rows(branch_batches), True)
    with jax.named_scope("gate_grad"):
        gate_grad = weight_shard(rows_one, rows(grad_gate), False)
    with jax.named_scope("query_grad"):
        query_grad = weight_shard(rows_one, interleave(rows(grad_query)), False)
    with jax.named_scope("value_grad"):
        value_grad = weight_shard(rows_one, rows(grad_value), False)
    with jax.named_scope("key_grad"):
        key_grad = weight_shard(rows_one, interleave(rows(grad_key)), False)
    return (
        layer_out,
        tokens_grad,
        query_grad,
        key_grad,
        value_grad,
        gate_grad,
        out_weight_grad,
        up_grad,
        down_grad,
        mine[:2],
        mine[2:],
    )


def solution(mesh):
    return jax.shard_map(
        local,
        mesh=mesh,
        in_specs=(
            P(("seq", "mp"), None),
            P("seq", None),
            P(),
            P(),
            P(None, "mp"),
            P(None, "mp"),
            P(None, "mp"),
            P(None, "mp"),
            P("mp", None),
            P(None, "mp"),
            P("mp", None),
            P(("seq", "mp"), None),
        ),
        out_specs=(
            P(("seq", "mp"), None),
            P(("seq", "mp"), None),
            P(None, "mp"),
            P(None, "mp"),
            P(None, "mp"),
            P(None, "mp"),
            P("mp", None),
            P(None, "mp"),
            P("mp", None),
            P(None, "mp"),
            P(None, "mp"),
        ),
        check_vma=False,
    )
```

time: 1710 us -> 601 us (0.35)
  waiting for transfers between devices: 1200 us -> 177 us
  local copies, waits for them, and re-layouts: 157 us -> 51.9 us
  starting transfers between devices: 14 us -> 84.3 us
  matrix products: 225 us -> 194 us
    reduce_scatter x4 -> x0, waiting for transfers between devices: 690 us -> none  [sum_rows(): lax.psum_scatter(term_maker(jnp.int32(0), local_rows * lax.axis_size('mp'...]
    all_gather x4 -> x0, waiting for transfers between devices: 242 us -> none  [gather_rows(): return lax.all_gather(row_block, 'mp', axis=0, tiled=True)]
    ppermute x8 -> x100, waiting for transfers between devices: 32.9 us -> 177 us  [the longest x64 113 us: ring_shift(): return lax.ppermute(value, 'mp', pairs)]
    psum x1 -> x0, waiting for transfers between devices: 122 us -> none  [local(): lax.psum(total[0].astype(jnp.bfloat16), 'seq').astype(jnp.float32)]
    unnamed x13 -> x0, waiting for transfers between devices: 113 us -> none
    dynamic_update_slice x20 -> x13, local copies, waits for them, and re-layouts: 91.8 us -> 16 us  [place(): return lax.dynamic_update_slice(buffer, piece, (first, 0))]
    ppermute x8 -> x100, starting transfers between devices: 13.1 us -> 84.3 us  [the longest x64 70 us: ring_shift(): return lax.ppermute(value, 'mp', pairs)]
    dot_general x26 -> x36, matrix products: 122 us -> 82.3 us  [contract(): lax.dot_general(left_side, right_side, (((left_dim,), (right_dim,)), ((),...]
  transfers between devices with their start and end apart: 19 -> 100, of which waited for: 16 -> 41; matrix products, arithmetic and copies ran while one was open for 7% -> 52% of each run, Pallas kernels for 0% -> 0%
where the time goes in v1:
time: 601 us; the launch traced here: 591 us
  matrix products  194 us (32%)
  waiting for transfers between devices  177 us (29%)
  starting transfers between devices  84.3 us (14%)
  other arithmetic  78.2 us (13%)
  local copies, waits for them, and re-layouts  51.9 us (9%)
    ppermute x64, waiting for transfers between devices, ring_shift(): return lax.ppermute(value, 'mp', pairs)  113 us
    dot_general x36, matrix products, contract(): lax.dot_general(left_side, right_side, (((left_dim,), (right_dim,)), ((),...  82.3 us
    ppermute x64, starting transfers between devices, ring_shift(): return lax.ppermute(value, 'mp', pairs)  70 us
    ppermute x8, waiting for transfers between devices, sum_groups(): result = result + lax.ppermute(value, 'seq', pairs)  54.4 us
    unnamed x360, local copies, waits for them, and re-layouts  27.2 us
    unnamed x27, other arithmetic  23.3 us
    dot_general x5, matrix products, local(): jnp.dot(intra, all_grad, preferred_element_type=f32).astype(bf16)  19.7 us
    dot_general x5, matrix products, local(): retained = jnp.dot(intra, all_v, preferred_element_type=f32)  18.6 us
  transfers between devices with their start and end apart: 100, of which 41 were waited for; matrix products, arithmetic and copies ran while one was open for 52% of the time, Pallas kernels for 0%

profile of v1, /device:TPU:0, one launch (start us, length us, event | category | flops | bytes accessed | tf_op | source)
XLA Modules:
  0.0 590.6 jit_solution(4837069392736736320)
XLA Ops:
  0.7 3.0 collective-permute-start.6
  26.9 2.7 constant_dynamic-update-slice_fusion.92
  29.6 3.9 collective-permute-done.9
  46.2 3.0 broadcast_select_fusion.5
  50.3 3.5 fusion.643
  67.5 4.4 collective-permute-done.14
  89.3 2.9 fusion.668
  97.1 2.9 fusion.667
  100.0 4.2 fusion.662
  104.3 4.3 fusion.663
  108.6 4.3 fusion.664
  128.6 7.7 %collective-permute-done.23 = bf16[128,2048]{1,0:T(8,128)(2,1)S(1)} collective-permute-done((bf16[128,2048]{1,0:T(8,128)(2,1)S(1)}, bf16[128,2048]{1,0:T(8,128)(2,1)S(1)}, u32[]{:S(2)}, u32[]{:S(2)}) %collective-permute-start.23) | collective-permute-done | bytes 524320 | tf_op jit(solution)/shard_map/scatter_branch/ppermute | solution.py:87
  143.3 4.3 collective-permute-done.41
  149.8 10.7 %collective-permute-done.20 = bf16[128,2048]{1,0:T(8,128)(2,1)S(1)} collective-permute-done((bf16[128,2048]{1,0:T(8,128)(2,1)S(1)}, bf16[128,2048]{1,0:T(8,128)(2,1)S(1)}, u32[]{:S(2)}, u32[]{:S(2)}) %collective-permute-start.20) | collective-permute-done | bytes 524320 | tf_op jit(solution)/shard_map/scatter_branch/ppermute | solution.py:87
  163.1 2.9 collective-permute-done.42
  166.2 8.9 %collective-permute-done.21 = bf16[128,2048]{1,0:T(8,128)(2,1)S(1)} collective-permute-done((bf16[128,2048]{1,0:T(8,128)(2,1)S(1)}, bf16[128,2048]{1,0:T(8,128)(2,1)S(1)}, u32[]{:S(2)}, u32[]{:S(2)}) %collective-permute-start.21) | collective-permute-done | bytes 524320 | tf_op jit(solution)/shard_map/scatter_branch/ppermute | solution.py:87
  180.9 7.4 %collective-permute-done.29 = bf16[128,2048]{1,0:T(8,128)(2,1)S(1)} collective-permute-done((bf16[128,2048]{1,0:T(8,128)(2,1)S(1)}, bf16[128,2048]{1,0:T(8,128)(2,1)S(1)}, u32[]{:S(2)}, u32[]{:S(2)}) %collective-permute-start.29) | collective-permute-done | bytes 524320 | tf_op jit(solution)/shard_map/gather_two/ppermute | solution.py:87
  197.9 5.6 collective-permute-done.31
  212.4 7.1 %collective-permute-done.33 = bf16[128,2048]{1,0:T(8,128)(2,1)S(1)} collective-permute-done((bf16[128,2048]{1,0:T(8,128)(2,1)S(1)}, bf16[128,2048]{1,0:T(8,128)(2,1)S(1)}, u32[]{:S(2)}, u32[]{:S(2)}) %collective-permute-start.33) | collective-permute-done | bytes 524320 | tf_op jit(solution)/shard_map/gather_two/ppermute | solution.py:87
  233.7 7.1 %collective-permute-done.44 = bf16[128,1024]{1,0:T(8,128)(2,1)S(1)} collective-permute-done((bf16[128,1024]{1,0:T(8,128)(2,1)S(1)}, bf16[128,1024]{1,0:T(8,128)(2,1)S(1)}, u32[]{:S(2)}, u32[]{:S(2)}) %collective-permute-start.44) | collective-permute-done | bytes 262176 | tf_op jit(solution)/shard_map/scatter_up/ppermute | solution.py:87
  244.8 6.5 %collective-permute-done.49 = bf16[128,2048]{1,0:T(8,128)(2,1)S(1)} collective-permute-done((bf16[128,2048]{1,0:T(8,128)(2,1)S(1)}, bf16[128,2048]{1,0:T(8,128)(2,1)S(1)}, u32[]{:S(2)}, u32[]{:S(2)}) %collective-permute-start.49) | collective-permute-done | bytes 524320 | tf_op jit(solution)/shard_map/scatter_up/ppermute | solution.py:87
  258.6 5.3 collective-permute-done.46
  275.3 2.9 collective-permute-done.51
  283.0 2.6 constant_dynamic-update-slice_fusion.46
  286.6 3.6 fusion.97
  297.3 3.0 add_convert_fusion.2
  300.3 10.9 %collective-permute-done.92 = bf16[2048,256]{1,0:T(8,128)(2,1)} collective-permute-done((bf16[2048,256]{1,0:T(8,128)(2,1)}, bf16[2048,256]{1,0:T(8,128)(2,1)}, u32[]{:S(2)}, u32[]{:S(2)}) %collective-permute-start.92) | collective-permute-done | bytes 1048608 | tf_op jit(solution)/shard_map/up_grad/ppermute | solution.py:348
  311.3 3.1 add_convert_fusion.3
  327.7 3.1 fusion.112
  330.9 3.2 fusion.172
  348.9 3.9 fusion.110
  352.8 3.3 fusion.173
  365.7 3.9 fusion.108
  385.2 3.6 fusion.95
  396.5 4.5 convolution_convert_fusion.2
  401.3 4.6 convolution_convert_fusion.3
  406.7 4.5 convolution_convert_fusion.6
  411.5 3.2 fusion.27
  415.4 3.0 fusion.94
  418.5 3.0 fusion.96
  421.5 3.1 fusion.107
  424.6 3.1 fusion.109
  427.8 4.0 fusion.111
  432.5 3.5 constant_dynamic-update-slice_fusion.41
  439.6 4.4 convolution_convert_fusion.5
  444.0 4.2 constant_dynamic-update-slice_fusion.40
  448.2 4.2 constant_dynamic-update-slice_fusion.39
  452.3 4.2 constant_dynamic-update-slice_fusion.38
  457.5 3.6 constant_dynamic-update-slice_fusion.37
  462.1 4.1 fusion.128
  468.6 3.7 convolution_convert_fusion.4
  474.7 3.3 fusion.46
  483.4 3.6 add_convert_fusion.8
  487.2 3.5 add_convert_fusion.7
  490.7 5.1 collective-permute-done.78
  500.1 3.9 add_convert_fusion
  505.0 3.8 fusion.6
  516.7 3.6 add_convert_fusion.1
  520.3 4.8 collective-permute-done.76
  526.6 2.7 fusion.658
  531.1 3.6 collective-permute-done.96
  535.9 2.8 collective-permute-done.97
  545.8 21.0 %collective-permute-done.88 = bf16[2048,256]{1,0:T(8,128)(2,1)S(1)} collective-permute-done((bf16[2048,256]{1,0:T(8,128)(2,1)S(1)}, bf16[2048,256]{1,0:T(8,128)(2,1)S(1)}, u32[]{:S(2)}, u32[]{:S(2)}) %collective-permute-start.88) | collective-permute-done | bytes 1048608 | tf_op jit(solution)/shard_map/gate_grad/ppermute | solution.py:348
  568.2 19.9 %collective-permute-done.99 = f32[4,128]{1,0:T(4,128)S(1)} collective-permute-done((f32[4,128]{1,0:T(4,128)S(1)}, f32[4,128]{1,0:T(4,128)S(1)}, u32[]{:S(2)}, u32[]{:S(2)}) %collective-permute-start.99) | collective-permute-done | bytes 2080 | tf_op jit(solution)/shard_map/norm_grads/ppermute | solution.py:348
  (772 shorter events, 279.9 us)
Async XLA Ops:
  0.7 15.5 %collective-permute-start.6 = (bf16[128,2048]{1,0:T(8,128)(2,1)}, bf16[128,2048]{1,0:T(8,128)(2,1)}, u32[]{:S(2)}, u32[]{:S(2)}) collective-permute-start(bf16[128,2048]{1,0:T(8,128)(2,1)} %param.14), channel_id=1, source_target_pairs={{0,2},{1,3},{4,0},{5,1},{8,4},{9,5},{12,8},{13,9},{14,12},{15,13},... | collective-permute-start | bytes 1572872 | tf_op jit(solution)/shard_map/gather_tokens/ppermute | solution.py:87
  3.7 13.7 %collective-permute-start.5 = (bf16[128,2048]{1,0:T(8,128)(2,1)}, bf16[128,2048]{1,0:T(8,128)(2,1)}, u32[]{:S(2)}, u32[]{:S(2)}) collective-permute-start(bf16[128,2048]{1,0:T(8,128)(2,1)} %param.14), channel_id=1, source_target_pairs={{0,4},{1,5},{4,8},{5,9},{8,12},{9,13},{12,14},{13,15},{14,10},{15,... | collective-permute-start | bytes 1572872 | tf_op jit(solution)/shard_map/gather_tokens/ppermute | solution.py:87
  3.8 18.2 %collective-permute-start = (bf16[2048,128]{1,0:T(8,128)(2,1)}, bf16[2048,128]{1,0:T(8,128)(2,1)}, u32[]{:S(2)}, u32[]{:S(2)}) collective-permute-start(bf16[2048,128]{1,0:T(8,128)(2,1)} %param.18), channel_id=1, source_target_pairs={{0,1},{1,0},{2,3},{3,2},{4,5},{5,4},{6,7},{7,6},{8,9},{9,8},{10,11... | collective-permute-start | bytes 1572872 | tf_op jit(solution)/shard_map/head_weights/ppermute | solution.py:91
  3.8 15.0 %collective-permute-start.1 = (bf16[2048,128]{1,0:T(8,128)(2,1)}, bf16[2048,128]{1,0:T(8,128)(2,1)}, u32[]{:S(2)}, u32[]{:S(2)}) collective-permute-start(bf16[2048,128]{1,0:T(8,128)(2,1)} %param.19), channel_id=1, source_target_pairs={{0,1},{1,0},{2,3},{3,2},{4,5},{5,4},{6,7},{7,6},{8,9},{9,8},{10,11... | collective-permute-start | bytes 1572872 | tf_op jit(solution)/shard_map/head_weights/ppermute | solution.py:91
  6.6 39.0 %collective-permute-start.26 = (bf16[2048,256]{0,1:T(8,128)(2,1)}, bf16[2048,256]{0,1:T(8,128)(2,1)}, u32[]{:S(2)}, u32[]{:S(2)}) collective-permute-start(bf16[2048,256]{0,1:T(8,128)(2,1)} %copy.52), channel_id=1, source_target_pairs={{0,1},{1,0},{2,3},{3,2},{4,5},{5,4},{6,7},{7,6},{8,9},{9,8},{10,11... | collective-permute-start | bytes 3145736 | tf_op jit(solution)/shard_map/head_weights/ppermute | solution.py:91
  16.2 20.2 %collective-permute-start.3 = (bf16[2048,256]{0,1:T(8,128)(2,1)S(1)}, bf16[2048,256]{0,1:T(8,128)(2,1)S(1)}, u32[]{:S(2)}, u32[]{:S(2)}) collective-permute-start(bf16[2048,256]{0,1:T(8,128)(2,1)S(1)} %copy.49), channel_id=1, source_target_pairs={{0,1},{1,0},{2,3},{3,2},{4,5},{5,4},{6,7},{7,6},{8,9},{9,8},{10,11... | collective-permute-start | bytes 3145736 | tf_op jit(solution)/shard_map/head_weights/ppermute | solution.py:91
  17.4 18.2 %collective-permute-start.2 = (bf16[2048,256]{0,1:T(8,128)(2,1)S(1)}, bf16[2048,256]{0,1:T(8,128)(2,1)S(1)}, u32[]{:S(2)}, u32[]{:S(2)}) collective-permute-start(bf16[2048,256]{0,1:T(8,128)(2,1)S(1)} %copy.46), channel_id=1, source_target_pairs={{0,1},{1,0},{2,3},{3,2},{4,5},{5,4},{6,7},{7,6},{8,9},{9,8},{10,11... | collective-permute-start | bytes 3145736 | tf_op jit(solution)/shard_map/head_weights/ppermute | solution.py:91
  18.9 14.6 %collective-permute-start.9 = (bf16[128,2048]{1,0:T(8,128)(2,1)}, bf16[128,2048]{1,0:T(8,128)(2,1)S(1)}, u32[]{:S(2)}, u32[]{:S(2)}) collective-permute-start(bf16[128,2048]{1,0:T(8,128)(2,1)} %collective-permute-done.6), channel_id=1, source_target_pairs={{0,2},{1,3},{4,0},{5,1},{8,4},{9,5},{12,8},{13,9},{14,12},{15,13},... | collective-permute-start | bytes 1572872 | tf_op jit(solution)/shard_map/gather_tokens/ppermute | solution.py:87
  33.5 15.7 %collective-permute-start.17 = (bf16[256,2048]{1,0:T(8,128)(2,1)S(1)}, bf16[256,2048]{1,0:T(8,128)(2,1)S(1)}, u32[]{:S(2)}, u32[]{:S(2)}) collective-permute-start(bf16[256,2048]{1,0:T(8,128)(2,1)S(1)} %copy-done.54), channel_id=1, source_target_pairs={{0,1},{1,0},{2,3},{3,2},{4,5},{5,4},{6,7},{7,6},{8,9},{9,8},{10,11... | collective-permute-start | bytes 3145736 | tf_op jit(solution)/shard_map/head_weights/ppermute | solution.py:91
  35.3 18.5 %collective-permute-start.27 = (bf16[256,2048]{1,0:T(8,128)(2,1)S(1)}, bf16[256,2048]{1,0:T(8,128)(2,1)S(1)}, u32[]{:S(2)}, u32[]{:S(2)}) collective-permute-start(bf16[256,2048]{1,0:T(8,128)(2,1)S(1)} %copy-done.55), channel_id=1, source_target_pairs={{0,1},{1,0},{2,3},{3,2},{4,5},{5,4},{6,7},{7,6},{8,9},{9,8},{10,11... | collective-permute-start | bytes 3145736 | tf_op jit(solution)/shard_map/head_weights/ppermute | solution.py:91
  40.9 18.4 %collective-permute-start.4 = (bf16[128,1024]{1,0:T(8,128)(2,1)S(1)}, bf16[128,1024]{1,0:T(8,128)(2,1)S(1)}, u32[]{:S(2)}, u32[]{:S(2)}) collective-permute-start(bf16[128,1024]{1,0:T(8,128)(2,1)S(1)} %pad_maximum_fusion.17), channel_id=1, source_target_pairs={{0,1},{1,0},{2,3},{3,2},{4,5},{5,4},{6,7},{7,6},{8,9},{9,8},{10,11... | collective-permute-start | bytes 786440 | tf_op jit(solution)/shard_map/project_in/ppermute | solution.py:91
  41.4 19.5 %collective-permute-start.12 = (bf16[128,2048]{1,0:T(8,128)(2,1)S(1)}, bf16[128,2048]{1,0:T(8,128)(2,1)S(1)}, u32[]{:S(2)}, u32[]{:S(2)}) collective-permute-start(bf16[128,2048]{1,0:T(8,128)(2,1)S(1)} %collective-permute-done.9), channel_id=1, source_target_pairs={{0,2},{1,3},{4,0},{5,1},{8,4},{9,5},{12,8},{13,9},{14,12},{15,13},... | collective-permute-start | bytes 1572872 | tf_op jit(solution)/shard_map/gather_tokens/ppermute | solution.py:87
  45.7 17.0 %collective-permute-start.11 = (bf16[128,2048]{1,0:T(8,128)(2,1)S(1)}, bf16[128,2048]{1,0:T(8,128)(2,1)S(1)}, u32[]{:S(2)}, u32[]{:S(2)}) collective-permute-start(bf16[128,2048]{1,0:T(8,128)(2,1)S(1)} %collective-permute-done.8), channel_id=1, source_target_pairs={{0,4},{1,5},{4,8},{5,9},{8,12},{9,13},{12,14},{13,15},{14,10},{15,... | collective-permute-start | bytes 1572872 | tf_op jit(solution)/shard_map/gather_tokens/ppermute | solution.py:87
  71.9 14.2 %collective-permute-start.37 = (bf16[128,2048]{1,0:T(8,128)(2,1)S(1)}, bf16[128,2048]{1,0:T(8,128)(2,1)}, u32[]{:S(2)}, u32[]{:S(2)}) collective-permute-start(bf16[128,2048]{1,0:T(8,128)(2,1)S(1)} %copy-done.43), channel_id=1, source_target_pairs={{0,2},{1,3},{4,0},{5,1},{8,4},{9,5},{12,8},{13,9},{14,12},{15,13},... | collective-permute-start | bytes 1572872 | tf_op jit(solution)/shard_map/gather_out_grad/ppermute | solution.py:87
  73.5 14.2 %collective-permute-start.36 = (bf16[128,2048]{1,0:T(8,128)(2,1)S(1)}, bf16[128,2048]{1,0:T(8,128)(2,1)}, u32[]{:S(2)}, u32[]{:S(2)}) collective-permute-start(bf16[128,2048]{1,0:T(8,128)(2,1)S(1)} %copy-done.43), channel_id=1, source_target_pairs={{0,4},{1,5},{4,8},{5,9},{8,12},{9,13},{12,14},{13,15},{14,10},{15,... | collective-permute-start | bytes 1572872 | tf_op jit(solution)/shard_map/gather_out_grad/ppermute | solution.py:87
  86.1 39.6 %collective-permute-start.39 = (bf16[128,2048]{1,0:T(8,128)(2,1)}, bf16[128,2048]{1,0:T(8,128)(2,1)}, u32[]{:S(2)}, u32[]{:S(2)}) collective-permute-start(bf16[128,2048]{1,0:T(8,128)(2,1)} %collective-permute-done.37), channel_id=1, source_target_pairs={{0,2},{1,3},{4,0},{5,1},{8,4},{9,5},{12,8},{13,9},{14,12},{15,13},... | collective-permute-start | bytes 1572872 | tf_op jit(solution)/shard_map/gather_out_grad/ppermute | solution.py:87
  87.7 39.7 %collective-permute-start.38 = (bf16[128,2048]{1,0:T(8,128)(2,1)}, bf16[128,2048]{1,0:T(8,128)(2,1)}, u32[]{:S(2)}, u32[]{:S(2)}) collective-permute-start(bf16[128,2048]{1,0:T(8,128)(2,1)} %collective-permute-done.36), channel_id=1, source_target_pairs={{0,4},{1,5},{4,8},{5,9},{8,12},{9,13},{12,14},{13,15},{14,10},{15,... | collective-permute-start | bytes 1572872 | tf_op jit(solution)/shard_map/gather_out_grad/ppermute | solution.py:87
  95.0 25.0 %collective-permute-start.18 = (bf16[128,1024]{1,0:T(8,128)(2,1)}, bf16[128,1024]{1,0:T(8,128)(2,1)}, u32[]{:S(2)}, u32[]{:S(2)}) collective-permute-start(bf16[128,1024]{1,0:T(8,128)(2,1)} %get-tuple-element.211), channel_id=1, source_target_pairs={{0,4},{1,5},{4,8},{5,9},{8,12},{9,13},{12,14},{13,15},{14,10},{15,... | collective-permute-start | bytes 786440 | tf_op jit(solution)/shard_map/scatter_branch/ppermute | solution.py:87
  95.5 24.5 %collective-permute-start.22 = (bf16[128,1024]{1,0:T(8,128)(2,1)}, bf16[128,1024]{1,0:T(8,128)(2,1)}, u32[]{:S(2)}, u32[]{:S(2)}) collective-permute-start(bf16[128,1024]{1,0:T(8,128)(2,1)} %get-tuple-element.212), channel_id=1, source_target_pairs={{0,2},{1,3},{4,0},{5,1},{8,4},{9,5},{12,8},{13,9},{14,12},{15,13},... | collective-permute-start | bytes 786440 | tf_op jit(solution)/shard_map/scatter_branch/ppermute | solution.py:87
  121.4 14.9 %collective-permute-start.23 = (bf16[128,2048]{1,0:T(8,128)(2,1)S(1)}, bf16[128,2048]{1,0:T(8,128)(2,1)S(1)}, u32[]{:S(2)}, u32[]{:S(2)}) collective-permute-start(bf16[128,2048]{1,0:T(8,128)(2,1)S(1)} %pad_maximum_fusion.10), channel_id=1, source_target_pairs={{0,2},{1,3},{4,0},{5,1},{8,4},{9,5},{12,8},{13,9},{14,12},{15,13},... | collective-permute-start | bytes 1572872 | tf_op jit(solution)/shard_map/scatter_branch/ppermute | solution.py:87
  123.1 14.9 %collective-permute-start.19 = (bf16[128,2048]{1,0:T(8,128)(2,1)S(1)}, bf16[128,2048]{1,0:T(8,128)(2,1)S(1)}, u32[]{:S(2)}, u32[]{:S(2)}) collective-permute-start(bf16[128,2048]{1,0:T(8,128)(2,1)S(1)} %pad_maximum_fusion.9), channel_id=1, source_target_pairs={{0,4},{1,5},{4,8},{5,9},{8,12},{9,13},{12,14},{13,15},{14,10},{15,... | collective-permute-start | bytes 1572872 | tf_op jit(solution)/shard_map/scatter_branch/ppermute | solution.py:87
  125.8 21.8 %collective-permute-start.41 = (bf16[128,2048]{1,0:T(8,128)(2,1)}, bf16[128,2048]{1,0:T(8,128)(2,1)S(1)}, u32[]{:S(2)}, u32[]{:S(2)}) collective-permute-start(bf16[128,2048]{1,0:T(8,128)(2,1)} %collective-permute-done.39), channel_id=1, source_target_pairs={{0,2},{1,3},{4,0},{5,1},{8,4},{9,5},{12,8},{13,9},{14,12},{15,13},... | collective-permute-start | bytes 1572872 | tf_op jit(solution)/shard_map/gather_out_grad/ppermute | solution.py:87
  127.4 21.8 %collective-permute-start.40 = (bf16[128,2048]{1,0:T(8,128)(2,1)}, bf16[128,2048]{1,0:T(8,128)(2,1)S(1)}, u32[]{:S(2)}, u32[]{:S(2)}) collective-permute-start(bf16[128,2048]{1,0:T(8,128)(2,1)} %collective-permute-done.38), channel_id=1, source_target_pairs={{0,4},{1,5},{4,8},{5,9},{8,12},{9,13},{12,14},{13,15},{14,10},{15,... | collective-permute-start | bytes 1572872 | tf_op jit(solution)/shard_map/gather_out_grad/ppermute | solution.py:87
  138.3 22.2 %collective-permute-start.20 = (bf16[128,2048]{1,0:T(8,128)(2,1)S(1)}, bf16[128,2048]{1,0:T(8,128)(2,1)S(1)}, u32[]{:S(2)}, u32[]{:S(2)}) collective-permute-start(bf16[128,2048]{1,0:T(8,128)(2,1)S(1)} %get-tuple-element.153), channel_id=1, source_target_pairs={{0,4},{1,5},{4,8},{5,9},{8,12},{9,13},{12,14},{13,15},{14,10},{15,... | collective-permute-start | bytes 1572872 | tf_op jit(solution)/shard_map/scatter_branch/ppermute | solution.py:87
  138.8 21.7 %collective-permute-start.24 = (bf16[128,2048]{1,0:T(8,128)(2,1)S(1)}, bf16[128,2048]{1,0:T(8,128)(2,1)S(1)}, u32[]{:S(2)}, u32[]{:S(2)}) collective-permute-start(bf16[128,2048]{1,0:T(8,128)(2,1)S(1)} %get-tuple-element.154), channel_id=1, source_target_pairs={{0,2},{1,3},{4,0},{5,1},{8,4},{9,5},{12,8},{13,9},{14,12},{15,13},... | collective-permute-start | bytes 1572872 | tf_op jit(solution)/shard_map/scatter_branch/ppermute | solution.py:87
  147.6 18.5 %collective-permute-start.43 = (bf16[128,1024]{1,0:T(8,128)(2,1)S(1)}, bf16[128,1024]{1,0:T(8,128)(2,1)S(1)}, u32[]{:S(2)}, u32[]{:S(2)}) collective-permute-start(bf16[128,1024]{1,0:T(8,128)(2,1)S(1)} %slice.784), channel_id=1, source_target_pairs={{0,2},{1,3},{4,0},{5,1},{8,4},{9,5},{12,8},{13,9},{14,12},{15,13},... | collective-permute-start | bytes 786440 | tf_op jit(solution)/shard_map/gather_out_grad/ppermute | solution.py:87
  149.3 16.8 %collective-permute-start.42 = (bf16[128,1024]{1,0:T(8,128)(2,1)S(1)}, bf16[128,1024]{1,0:T(8,128)(2,1)S(1)}, u32[]{:S(2)}, u32[]{:S(2)}) collective-permute-start(bf16[128,1024]{1,0:T(8,128)(2,1)S(1)} %slice.783), channel_id=1, source_target_pairs={{0,4},{1,5},{4,8},{5,9},{8,12},{9,13},{12,14},{13,15},{14,10},{15,... | collective-permute-start | bytes 786440 | tf_op jit(solution)/shard_map/gather_out_grad/ppermute | solution.py:87
  160.8 14.2 %collective-permute-start.21 = (bf16[128,2048]{1,0:T(8,128)(2,1)S(1)}, bf16[128,2048]{1,0:T(8,128)(2,1)S(1)}, u32[]{:S(2)}, u32[]{:S(2)}) collective-permute-start(bf16[128,2048]{1,0:T(8,128)(2,1)S(1)} %get-tuple-element.151), channel_id=1, source_target_pairs={{0,4},{1,5},{4,8},{5,9},{8,12},{9,13},{12,14},{13,15},{14,10},{15,... | collective-permute-start | bytes 1572872 | tf_op jit(solution)/shard_map/scatter_branch/ppermute | solution.py:87
  161.3 13.7 %collective-permute-start.25 = (bf16[128,2048]{1,0:T(8,128)(2,1)S(1)}, bf16[128,2048]{1,0:T(8,128)(2,1)S(1)}, u32[]{:S(2)}, u32[]{:S(2)}) collective-permute-start(bf16[128,2048]{1,0:T(8,128)(2,1)S(1)} %get-tuple-element.152), channel_id=1, source_target_pairs={{0,2},{1,3},{4,0},{5,1},{8,4},{9,5},{12,8},{13,9},{14,12},{15,13},... | collective-permute-start | bytes 1572872 | tf_op jit(solution)/shard_map/scatter_branch/ppermute | solution.py:87
  244.6 23.7 %collective-permute-start.93 = (bf16[256,2048]{1,0:T(8,128)(2,1)S(1)}, bf16[256,2048]{1,0:T(8,128)(2,1)S(1)}, u32[]{:S(2)}, u32[]{:S(2)}) collective-permute-start(bf16[256,2048]{1,0:T(8,128)(2,1)S(1)} %convolution_convert_fusion), channel_id=1, source_target_pairs={{0,1},{1,0},{2,3},{3,2},{4,5},{5,4},{6,7},{7,6},{8,9},{9,8},{10,11... | collective-permute-start | bytes 3145736 | tf_op jit(solution)/shard_map/down_grad/ppermute | solution.py:91
  257.3 14.7 %collective-permute-start.91 = (bf16[2048,256]{1,0:T(8,128)(2,1)S(1)}, bf16[2048,256]{1,0:T(8,128)(2,1)S(1)}, u32[]{:S(2)}, u32[]{:S(2)}) collective-permute-start(bf16[2048,256]{1,0:T(8,128)(2,1)S(1)} %convolution_convert_fusion.1), channel_id=1, source_target_pairs={{0,1},{1,0},{2,3},{3,2},{4,5},{5,4},{6,7},{7,6},{8,9},{9,8},{10,11... | collective-permute-start | bytes 3145736 | tf_op jit(solution)/shard_map/up_grad/ppermute | solution.py:91
  270.6 26.4 %collective-permute-start.94 = (bf16[256,2048]{1,0:T(8,128)(2,1)}, bf16[256,2048]{1,0:T(8,128)(2,1)}, u32[]{:S(2)}, u32[]{:S(2)}) collective-permute-start(bf16[256,2048]{1,0:T(8,128)(2,1)} %fusion.8), channel_id=1, source_target_pairs={{0,16},{16,0},{1,17},{17,1},{2,18},{18,2},{3,19},{19,3},{4,20},{20... | collective-permute-start | bytes 3145736 | tf_op jit(solution)/shard_map/down_grad/ppermute | solution.py:348
  274.4 36.9 %collective-permute-start.92 = (bf16[2048,256]{1,0:T(8,128)(2,1)}, bf16[2048,256]{1,0:T(8,128)(2,1)}, u32[]{:S(2)}, u32[]{:S(2)}) collective-permute-start(bf16[2048,256]{1,0:T(8,128)(2,1)} %fusion.7), channel_id=1, source_target_pairs={{0,16},{16,0},{1,17},{17,1},{2,18},{18,2},{3,19},{19,3},{4,20},{20... | collective-permute-start | bytes 3145736 | tf_op jit(solution)/shard_map/up_grad/ppermute | solution.py:348
  280.9 37.4 %collective-permute-start.62 = (bf16[128,2048]{1,0:T(8,128)(2,1)}, bf16[128,2048]{1,0:T(8,128)(2,1)}, u32[]{:S(2)}, u32[]{:S(2)}) collective-permute-start(bf16[128,2048]{1,0:T(8,128)(2,1)} %get-tuple-element.70), channel_id=1, source_target_pairs={{0,2},{1,3},{4,0},{5,1},{8,4},{9,5},{12,8},{13,9},{14,12},{15,13},... | collective-permute-start | bytes 1572872 | tf_op jit(solution)/shard_map/gather_branch/ppermute | solution.py:87
  281.3 36.9 %collective-permute-start.61 = (bf16[128,2048]{1,0:T(8,128)(2,1)}, bf16[128,2048]{1,0:T(8,128)(2,1)}, u32[]{:S(2)}, u32[]{:S(2)}) collective-permute-start(bf16[128,2048]{1,0:T(8,128)(2,1)} %get-tuple-element.70), channel_id=1, source_target_pairs={{0,4},{1,5},{4,8},{5,9},{8,12},{9,13},{12,14},{13,15},{14,10},{15,... | collective-permute-start | bytes 1572872 | tf_op jit(solution)/shard_map/gather_branch/ppermute | solution.py:87
  291.8 22.6 %collective-permute-start.52 = (bf16[128,1024]{1,0:T(8,128)(2,1)S(1)}, bf16[128,1024]{1,0:T(8,128)(2,1)S(1)}, u32[]{:S(2)}, u32[]{:S(2)}) collective-permute-start(bf16[128,1024]{1,0:T(8,128)(2,1)S(1)} %get-tuple-element.207), channel_id=1, source_target_pairs={{0,4},{1,5},{4,8},{5,9},{8,12},{9,13},{12,14},{13,15},{14,10},{15,... | collective-permute-start | bytes 786440 | tf_op jit(solution)/shard_map/scatter_down/ppermute | solution.py:87
  297.0 17.3 %collective-permute-start.56 = (bf16[128,1024]{1,0:T(8,128)(2,1)S(1)}, bf16[128,1024]{1,0:T(8,128)(2,1)S(1)}, u32[]{:S(2)}, u32[]{:S(2)}) collective-permute-start(bf16[128,1024]{1,0:T(8,128)(2,1)S(1)} %get-tuple-element.208), channel_id=1, source_target_pairs={{0,2},{1,3},{4,0},{5,1},{8,4},{9,5},{12,8},{13,9},{14,12},{15,13},... | collective-permute-start | bytes 786440 | tf_op jit(solution)/shard_map/scatter_down/ppermute | solution.py:87
  315.4 15.5 %collective-permute-start.57 = (bf16[128,2048]{1,0:T(8,128)(2,1)}, bf16[128,2048]{1,0:T(8,128)(2,1)}, u32[]{:S(2)}, u32[]{:S(2)}) collective-permute-start(bf16[128,2048]{1,0:T(8,128)(2,1)} %pad_maximum_fusion.14), channel_id=1, source_target_pairs={{0,2},{1,3},{4,0},{5,1},{8,4},{9,5},{12,8},{13,9},{14,12},{15,13},... | collective-permute-start | bytes 1572872 | tf_op jit(solution)/shard_map/scatter_down/ppermute | solution.py:87
  321.8 14.4 %collective-permute-start.63 = (bf16[256,512]{1,0:T(8,128)(2,1)}, bf16[256,512]{1,0:T(8,128)(2,1)}, u32[]{:S(2)}, u32[]{:S(2)}) collective-permute-start(bf16[256,512]{1,0:T(8,128)(2,1)} %get-tuple-element.204), channel_id=1, source_target_pairs={{0,1},{1,0},{2,3},{3,2},{4,5},{5,4},{6,7},{7,6},{8,9},{9,8},{10,11... | collective-permute-start | bytes 786440 | tf_op jit(solution)/shard_map/retention_back_rows/ppermute | solution.py:91
  321.8 16.0 %collective-permute-start.65 = (bf16[128,2048]{1,0:T(8,128)(2,1)}, bf16[128,2048]{1,0:T(8,128)(2,1)}, u32[]{:S(2)}, u32[]{:S(2)}) collective-permute-start(bf16[128,2048]{1,0:T(8,128)(2,1)} %collective-permute-done.62), channel_id=1, source_target_pairs={{0,2},{1,3},{4,0},{5,1},{8,4},{9,5},{12,8},{13,9},{14,12},{15,13},... | collective-permute-start | bytes 1572872 | tf_op jit(solution)/shard_map/gather_branch/ppermute | solution.py:87
  323.6 15.9 %collective-permute-start.64 = (bf16[128,2048]{1,0:T(8,128)(2,1)}, bf16[128,2048]{1,0:T(8,128)(2,1)}, u32[]{:S(2)}, u32[]{:S(2)}) collective-permute-start(bf16[128,2048]{1,0:T(8,128)(2,1)} %collective-permute-done.61), channel_id=1, source_target_pairs={{0,4},{1,5},{4,8},{5,9},{8,12},{9,13},{12,14},{13,15},{14,10},{15,... | collective-permute-start | bytes 1572872 | tf_op jit(solution)/shard_map/gather_branch/ppermute | solution.py:87
  334.2 18.6 %collective-permute-start.54 = (bf16[128,2048]{1,0:T(8,128)(2,1)}, bf16[128,2048]{1,0:T(8,128)(2,1)}, u32[]{:S(2)}, u32[]{:S(2)}) collective-permute-start(bf16[128,2048]{1,0:T(8,128)(2,1)} %get-tuple-element.137), channel_id=1, source_target_pairs={{0,4},{1,5},{4,8},{5,9},{8,12},{9,13},{12,14},{13,15},{14,10},{15,... | collective-permute-start | bytes 1572872 | tf_op jit(solution)/shard_map/scatter_down/ppermute | solution.py:87
  335.8 16.9 %collective-permute-start.58 = (bf16[128,2048]{1,0:T(8,128)(2,1)}, bf16[128,2048]{1,0:T(8,128)(2,1)}, u32[]{:S(2)}, u32[]{:S(2)}) collective-permute-start(bf16[128,2048]{1,0:T(8,128)(2,1)} %get-tuple-element.138), channel_id=1, source_target_pairs={{0,2},{1,3},{4,0},{5,1},{8,4},{9,5},{12,8},{13,9},{14,12},{15,13},... | collective-permute-start | bytes 1572872 | tf_op jit(solution)/shard_map/scatter_down/ppermute | solution.py:87
  343.0 15.0 %collective-permute-start.66 = (bf16[256,512]{1,0:T(8,128)(2,1)}, bf16[256,512]{1,0:T(8,128)(2,1)}, u32[]{:S(2)}, u32[]{:S(2)}) collective-permute-start(bf16[256,512]{1,0:T(8,128)(2,1)} %get-tuple-element.202), channel_id=1, source_target_pairs={{0,1},{1,0},{2,3},{3,2},{4,5},{5,4},{6,7},{7,6},{8,9},{9,8},{10,11... | collective-permute-start | bytes 786440 | tf_op jit(solution)/shard_map/retention_back_rows/ppermute | solution.py:91
  343.0 19.1 %collective-permute-start.68 = (bf16[128,2048]{1,0:T(8,128)(2,1)}, bf16[128,2048]{1,0:T(8,128)(2,1)}, u32[]{:S(2)}, u32[]{:S(2)}) collective-permute-start(bf16[128,2048]{1,0:T(8,128)(2,1)} %collective-permute-done.65), channel_id=1, source_target_pairs={{0,2},{1,3},{4,0},{5,1},{8,4},{9,5},{12,8},{13,9},{14,12},{15,13},... | collective-permute-start | bytes 1572872 | tf_op jit(solution)/shard_map/gather_branch/ppermute | solution.py:87
  344.7 17.5 %collective-permute-start.67 = (bf16[128,2048]{1,0:T(8,128)(2,1)}, bf16[128,2048]{1,0:T(8,128)(2,1)}, u32[]{:S(2)}, u32[]{:S(2)}) collective-permute-start(bf16[128,2048]{1,0:T(8,128)(2,1)} %collective-permute-done.64), channel_id=1, source_target_pairs={{0,4},{1,5},{4,8},{5,9},{8,12},{9,13},{12,14},{13,15},{14,10},{15,... | collective-permute-start | bytes 1572872 | tf_op jit(solution)/shard_map/gather_branch/ppermute | solution.py:87
  356.1 55.2 %collective-permute-start.55 = (bf16[128,2048]{1,0:T(8,128)(2,1)}, bf16[128,2048]{1,0:T(8,128)(2,1)}, u32[]{:S(2)}, u32[]{:S(2)}) collective-permute-start(bf16[128,2048]{1,0:T(8,128)(2,1)} %get-tuple-element.135), channel_id=1, source_target_pairs={{0,4},{1,5},{4,8},{5,9},{8,12},{9,13},{12,14},{13,15},{14,10},{15,... | collective-permute-start | bytes 1572872 | tf_op jit(solution)/shard_map/scatter_down/ppermute | solution.py:87
  356.2 55.3 %collective-permute-start.59 = (bf16[128,2048]{1,0:T(8,128)(2,1)}, bf16[128,2048]{1,0:T(8,128)(2,1)}, u32[]{:S(2)}, u32[]{:S(2)}) collective-permute-start(bf16[128,2048]{1,0:T(8,128)(2,1)} %get-tuple-element.136), channel_id=1, source_target_pairs={{0,2},{1,3},{4,0},{5,1},{8,4},{9,5},{12,8},{13,9},{14,12},{15,13},... | collective-permute-start | bytes 1572872 | tf_op jit(solution)/shard_map/scatter_down/ppermute | solution.py:87
  369.5 13.9 %collective-permute-start.69 = (bf16[256,512]{1,0:T(8,128)(2,1)}, bf16[256,512]{1,0:T(8,128)(2,1)S(1)}, u32[]{:S(2)}, u32[]{:S(2)}) collective-permute-start(bf16[256,512]{1,0:T(8,128)(2,1)} %get-tuple-element.200), channel_id=1, source_target_pairs={{0,1},{1,0},{2,3},{3,2},{4,5},{5,4},{6,7},{7,6},{8,9},{9,8},{10,11... | collective-permute-start | bytes 786440 | tf_op jit(solution)/shard_map/retention_back_rows/ppermute | solution.py:91
  388.8 25.9 %collective-permute-start.72 = (bf16[128,512]{1,0:T(8,128)(2,1)}, bf16[128,512]{1,0:T(8,128)(2,1)S(1)}, u32[]{:S(2)}, u32[]{:S(2)}) collective-permute-start(bf16[128,512]{1,0:T(8,128)(2,1)} %get-tuple-element.220), channel_id=1, source_target_pairs={{0,1},{1,0},{2,3},{3,2},{4,5},{5,4},{6,7},{7,6},{8,9},{9,8},{10,11... | collective-permute-start | bytes 393224 | tf_op jit(solution)/shard_map/retention_back_rows/ppermute | solution.py:91
  401.0 102.9 %collective-permute-start.89 = (bf16[256,2048]{1,0:T(8,128)(2,1)}, bf16[256,2048]{1,0:T(8,128)(2,1)}, u32[]{:S(2)}, u32[]{:S(2)}) collective-permute-start(bf16[256,2048]{1,0:T(8,128)(2,1)} %convolution_convert_fusion.2), channel_id=1, source_target_pairs={{0,1},{1,0},{2,3},{3,2},{4,5},{5,4},{6,7},{7,6},{8,9},{9,8},{10,11... | collective-permute-start | bytes 3145736 | tf_op jit(solution)/shard_map/out_weight_grad/ppermute | solution.py:91
  405.9 93.6 %collective-permute-start.87 = (bf16[2048,256]{1,0:T(8,128)(2,1)}, bf16[2048,256]{1,0:T(8,128)(2,1)}, u32[]{:S(2)}, u32[]{:S(2)}) collective-permute-start(bf16[2048,256]{1,0:T(8,128)(2,1)} %convolution_convert_fusion.3), channel_id=1, source_target_pairs={{0,1},{1,0},{2,3},{3,2},{4,5},{5,4},{6,7},{7,6},{8,9},{9,8},{10,11... | collective-permute-start | bytes 3145736 | tf_op jit(solution)/shard_map/gate_grad/ppermute | solution.py:91
  411.3 71.5 %collective-permute-start.81 = (bf16[2048,128]{1,0:T(8,128)(2,1)}, bf16[2048,128]{1,0:T(8,128)(2,1)}, u32[]{:S(2)}, u32[]{:S(2)}) collective-permute-start(bf16[2048,128]{1,0:T(8,128)(2,1)} %convolution_convert_fusion.6), channel_id=1, source_target_pairs={{0,1},{1,0},{2,3},{3,2},{4,5},{5,4},{6,7},{7,6},{8,9},{9,8},{10,11... | collective-permute-start | bytes 1572872 | tf_op jit(solution)/shard_map/query_grad/ppermute | solution.py:91
  466.3 14.6 %collective-permute-start.73 = (bf16[128,1024]{1,0:T(8,128)(2,1)S(1)}, bf16[128,1024]{1,0:T(8,128)(2,1)S(1)}, u32[]{:S(2)}, u32[]{:S(2)}) collective-permute-start(bf16[128,1024]{1,0:T(8,128)(2,1)S(1)} %get-tuple-element.205), channel_id=1, source_target_pairs={{0,4},{1,5},{4,8},{5,9},{8,12},{9,13},{12,14},{13,15},{14,10},{15,... | collective-permute-start | bytes 786440 | tf_op jit(solution)/shard_map/scatter_in/ppermute | solution.py:87
  481.2 14.6 %collective-permute-start.78 = (bf16[128,2048]{1,0:T(8,128)(2,1)S(1)}, bf16[128,2048]{1,0:T(8,128)(2,1)S(1)}, u32[]{:S(2)}, u32[]{:S(2)}) collective-permute-start(bf16[128,2048]{1,0:T(8,128)(2,1)S(1)} %pad_maximum_fusion.16), channel_id=1, source_target_pairs={{0,2},{1,3},{4,0},{5,1},{8,4},{9,5},{12,8},{13,9},{14,12},{15,13},... | collective-permute-start | bytes 1572872 | tf_op jit(solution)/shard_map/scatter_in/ppermute | solution.py:87
  482.8 14.6 %collective-permute-start.74 = (bf16[128,2048]{1,0:T(8,128)(2,1)S(1)}, bf16[128,2048]{1,0:T(8,128)(2,1)S(1)}, u32[]{:S(2)}, u32[]{:S(2)}) collective-permute-start(bf16[128,2048]{1,0:T(8,128)(2,1)S(1)} %pad_maximum_fusion.15), channel_id=1, source_target_pairs={{0,4},{1,5},{4,8},{5,9},{8,12},{9,13},{12,14},{13,15},{14,10},{15,... | collective-permute-start | bytes 1572872 | tf_op jit(solution)/shard_map/scatter_in/ppermute | solution.py:87
  487.0 29.2 %collective-permute-start.85 = (bf16[2048,256]{1,0:T(8,128)(2,1)S(1)}, bf16[2048,256]{1,0:T(8,128)(2,1)S(1)}, u32[]{:S(2)}, u32[]{:S(2)}) collective-permute-start(bf16[2048,256]{1,0:T(8,128)(2,1)S(1)} %convolution_convert_fusion.4), channel_id=1, source_target_pairs={{0,1},{1,0},{2,3},{3,2},{4,5},{5,4},{6,7},{7,6},{8,9},{9,8},{10,11... | collective-permute-start | bytes 3145736 | tf_op jit(solution)/shard_map/value_grad/ppermute | solution.py:91
  495.8 19.0 %collective-permute-start.82 = (bf16[2048,128]{1,0:T(8,128)(2,1)S(1)}, bf16[2048,128]{1,0:T(8,128)(2,1)S(1)}, u32[]{:S(2)}, u32[]{:S(2)}) collective-permute-start(bf16[2048,128]{1,0:T(8,128)(2,1)S(1)} %add_convert_fusion.8), channel_id=1, source_target_pairs={{0,16},{16,0},{1,17},{17,1},{2,18},{18,2},{3,19},{19,3},{4,20},{20... | collective-permute-start | bytes 1572872 | tf_op jit(solution)/shard_map/query_grad/ppermute | solution.py:348
  497.8 13.4 %collective-permute-start.75 = (bf16[128,2048]{1,0:T(8,128)(2,1)S(1)}, bf16[128,2048]{1,0:T(8,128)(2,1)S(1)}, u32[]{:S(2)}, u32[]{:S(2)}) collective-permute-start(bf16[128,2048]{1,0:T(8,128)(2,1)S(1)} %get-tuple-element.131), channel_id=1, source_target_pairs={{0,4},{1,5},{4,8},{5,9},{8,12},{9,13},{12,14},{13,15},{14,10},{15,... | collective-permute-start | bytes 1572872 | tf_op jit(solution)/shard_map/scatter_in/ppermute | solution.py:87
  503.9 25.6 %collective-permute-start.84 = (bf16[2048,128]{1,0:T(8,128)(2,1)S(1)}, bf16[2048,128]{1,0:T(8,128)(2,1)S(1)}, u32[]{:S(2)}, u32[]{:S(2)}) collective-permute-start(bf16[2048,128]{1,0:T(8,128)(2,1)S(1)} %add_convert_fusion.7), channel_id=1, source_target_pairs={{0,16},{16,0},{1,17},{17,1},{2,18},{18,2},{3,19},{19,3},{4,20},{20... | collective-permute-start | bytes 1572872 | tf_op jit(solution)/shard_map/key_grad/ppermute | solution.py:348
  511.2 33.1 %collective-permute-start.90 = (bf16[256,2048]{1,0:T(8,128)(2,1)S(1)}, bf16[256,2048]{1,0:T(8,128)(2,1)S(1)}, u32[]{:S(2)}, u32[]{:S(2)}) collective-permute-start(bf16[256,2048]{1,0:T(8,128)(2,1)S(1)} %fusion.6), channel_id=1, source_target_pairs={{0,16},{16,0},{1,17},{17,1},{2,18},{18,2},{3,19},{19,3},{4,20},{20... | collective-permute-start | bytes 3145736 | tf_op jit(solution)/shard_map/out_weight_grad/ppermute | solution.py:348
  516.2 50.6 %collective-permute-start.88 = (bf16[2048,256]{1,0:T(8,128)(2,1)S(1)}, bf16[2048,256]{1,0:T(8,128)(2,1)S(1)}, u32[]{:S(2)}, u32[]{:S(2)}) collective-permute-start(bf16[2048,256]{1,0:T(8,128)(2,1)S(1)} %add_convert_fusion), channel_id=1, source_target_pairs={{0,16},{16,0},{1,17},{17,1},{2,18},{18,2},{3,19},{19,3},{4,20},{20... | collective-permute-start | bytes 3145736 | tf_op jit(solution)/shard_map/gate_grad/ppermute | solution.py:348
  525.1 63.6 %collective-permute-start.86 = (bf16[2048,256]{1,0:T(8,128)(2,1)S(1)}, bf16[2048,256]{1,0:T(8,128)(2,1)S(1)}, u32[]{:S(2)}, u32[]{:S(2)}) collective-permute-start(bf16[2048,256]{1,0:T(8,128)(2,1)S(1)} %add_convert_fusion.1), channel_id=1, source_target_pairs={{0,16},{16,0},{1,17},{17,1},{2,18},{18,2},{3,19},{19,3},{4,20},{20... | collective-permute-start | bytes 3145736 | tf_op jit(solution)/shard_map/value_grad/ppermute | solution.py:348
  543.6 44.5 %collective-permute-start.99 = (f32[4,128]{1,0:T(4,128)S(1)}, f32[4,128]{1,0:T(4,128)S(1)}, u32[]{:S(2)}, u32[]{:S(2)}) collective-permute-start(f32[4,128]{1,0:T(4,128)S(1)} %fusion.555), channel_id=1, source_target_pairs={{0,16},{16,0},{1,17},{17,1},{2,18},{18,2},{3,19},{19,3},{4,20},{20... | collective-permute-start | bytes 6152 | tf_op jit(solution)/shard_map/norm_grads/ppermute | solution.py:348
  (203 other events, 2735.8 us)

commit v2 on v1

v2 whole, which is shorter than its diff:
```python
import jax
import jax.numpy as jnp
import numpy as np
from jax import lax
from jax.experimental import pallas as pl
from jax.experimental.pallas import tpu as pltpu
from jax.sharding import PartitionSpec as P

HEADS = 8
KEY = 256
VAL = 512
QKV = 2 * KEY + VAL
VMEM_BYTES = 44 << 20

epsilon = 1e-05
group_epsilon = 0.25
key_scale = KEY ** (-0.5)
bf16, f32 = jnp.bfloat16, jnp.float32

RING = tuple(range(0, HEADS, 2)) + tuple(range(HEADS - 1, 0, -2))
BATCHES = ((0, -1, 1, -2, 2), (-3, 3), (4,))
OFFSETS = tuple(offset for batch in BATCHES for offset in batch)
FIRST = (0, 5, 7)


def contract(left_side, right_side, left_dim, right_dim):
    return lax.dot_general(
        left_side,
        right_side,
        (((left_dim,), (right_dim,)), ((), ())),
        preferred_element_type=f32,
    )


def after(value, *earlier):
    return lax.optimization_barrier((value, *earlier))[0]


def row_stats(values):
    average = jnp.mean(values, axis=-1, keepdims=True)
    centered = values - average
    variance = jnp.mean(centered * centered, axis=-1, keepdims=True)
    return average, lax.rsqrt(variance + epsilon)


def normalize_back(grad_normed, unit_rows, inverse, norm_gain):
    scaled = grad_normed * norm_gain
    plain_mean = jnp.mean(scaled, axis=-1, keepdims=True)
    cross_mean = jnp.mean(scaled * unit_rows, axis=-1, keepdims=True)
    return inverse * (scaled - plain_mean - unit_rows * cross_mean)


def turn(values, cosine, sine):
    half = values.shape[-1] // 2
    even, odd = values[:, :half], values[:, half:]
    return jnp.concatenate([even * cosine - odd * sine, even * sine + odd * cosine], axis=1)


def sigmoid(values):
    return 1.0 / (1.0 + jnp.exp(-values))


def run(body, name, outs, scratch, *groups, late=(), flops=0, free=False):
    lists = [list(group) if isinstance(group, (list, tuple)) else [group] for group in groups]
    sizes = [len(group) for group in lists]
    values = [value for group in lists for value in group]
    fixed = len(outs) + len(scratch)

    def kernel(*refs):
        split, at = [], 0
        for size in sizes:
            split.append(refs[at : at + size])
            at += size
        sources = refs[at : at + len(late)]
        at += len(late)
        results = refs[at : at + fixed]
        at += fixed
        copies = [
            pltpu.make_async_copy(source, refs[at + i], refs[at + len(late) + i])
            for i, source in enumerate(sources)
        ]
        for copy in copies:
            copy.start()

        def fetch(i):
            def wait():
                copies[i].wait()
                return refs[at + i]

            return wait

        body(*split, *results, *[fetch(i) for i in range(len(late))])

    whole = pl.BlockSpec(memory_space=pltpu.VMEM)
    moved = sum(value.size * value.dtype.itemsize for value in (*values, *late))
    moved += sum(int(np.prod(shape)) * jnp.dtype(dtype).itemsize for shape, dtype in outs)
    return pl.pallas_call(
        kernel,
        out_shape=[jax.ShapeDtypeStruct(shape, dtype) for shape, dtype in outs],
        in_specs=[whole] * len(values) + [pl.BlockSpec(memory_space=pl.ANY)] * len(late),
        out_specs=[whole] * len(outs),
        scratch_shapes=[pltpu.VMEM(shape, dtype) for shape, dtype in scratch]
        + [pltpu.VMEM(value.shape, value.dtype) for value in late]
        + [pltpu.SemaphoreType.DMA(())] * len(late),
        compiler_params=pltpu.CompilerParams(vmem_limit_bytes=VMEM_BYTES),
        cost_estimate=pl.CostEstimate(flops=flops, transcendentals=0, bytes_accessed=0 if free else moved),
        name=name,
    )(*values, *late)


def each_block(count, block, step):
    def body(i, unused):
        step(pl.multiple_of(i * block, block))
        return unused

    lax.fori_loop(0, count // block, body, 0)


def stage_rows(pieces, rows):
    width = rows.shape[1]
    half = pieces[0].shape[1]
    if half < width:
        rows[:, :half] = pieces[0][...]
        rows[:, half:] = pieces[1][...]
    else:
        chunk = rows.shape[0] // len(pieces)
        for at, piece in enumerate(pieces):
            rows[at * chunk : (at + 1) * chunk, :] = piece[...]


def project_body(pieces, norm, angles, tokens, normed, qkv, gate, stats, weights):
    (norm,), (angles,) = norm, angles
    stage_rows(pieces, tokens)
    count, width = normed.shape

    def normalize(first):
        span = pl.ds(first, 64)
        raw = tokens[span, :].astype(f32)
        average, inverse = row_stats(raw)
        stats[span, :] = jnp.concatenate([average, inverse], axis=1)
        value = (raw - average) * inverse * norm[0:1, :] + norm[1:2, :]
        normed[span, :] = value.astype(bf16)

    each_block(count, 64, normalize)
    weights = weights()
    half = KEY // 2
    cosine, sine = angles[:, :half], angles[:, half:]
    for part in range(2):
        raw = contract(normed[...], weights[:, part * KEY : (part + 1) * KEY], 1, 0)
        turned = turn(raw, cosine, sine)
        qkv[:, part * KEY : (part + 1) * KEY] = (turned * key_scale if part else turned).astype(bf16)
    qkv[:, 2 * KEY :] = contract(normed[...], weights[:, 2 * KEY : QKV], 1, 0).astype(bf16)
    gate[...] = contract(normed[...], weights[:, QKV:], 1, 0)


def decays(columns, rows, away, at, chunk, place, by_query):
    span = slice(at * chunk, (at + 1) * chunk)
    ids, begin = columns[span, 0:1], columns[span, 1:2]
    others, other_begin = rows[0:1, place], rows[1:2, place]
    if by_query:
        mask = (others <= ids) & (others >= begin)
        near = columns[span, 2:3]
    else:
        mask = (others >= ids) & (other_begin <= ids)
        near = columns[span, 3:4]
    return jnp.where(mask, near * away[at : at + 1, place], 0.0)


def spans_of(arrays):
    at = 0
    for array in arrays:
        yield array, slice(at, at + array.shape[0])
        at += array.shape[0]


def branch_body(own, every, gate, columns, rows, away, *refs):
    (own,), (gate,), (columns,), (rows,), (away,) = own, gate, columns, rows, away
    *parts, gated, grouped, inverse, intra, out_weight = refs
    count = own.shape[0]
    chunks = away.shape[0]
    chunk = count // chunks
    queries = own[:, :KEY]
    for array, place in spans_of(every):
        scores = contract(queries, array[:, KEY : 2 * KEY], 1, 1)
        for at in range(chunks):
            factor = decays(columns, rows, away, at, chunk, place, True)
            span = slice(at * chunk, (at + 1) * chunk)
            intra[span, place] = (scores[span] * factor).astype(bf16)
    retained = 0.0
    for array, place in spans_of(every):
        retained = retained + contract(intra[:, place], array[:, 2 * KEY :], 1, 0)
    grouped[...] = retained

    def finish(first):
        span = pl.ds(first, 64)
        value = grouped[span, :]
        average = jnp.mean(value, axis=1, keepdims=True)
        square = jnp.mean(value * value, axis=1, keepdims=True)
        scale = lax.rsqrt(square - average * average + group_epsilon)
        inverse[span, :] = scale
        value = (value - average) * scale
        grouped[span, :] = value
        pre = gate[span, :]
        gated[span, :] = (pre * sigmoid(pre) * value).astype(bf16)

    each_block(count, 64, finish)
    store_parts(parts, lambda place, weight=out_weight(): contract(gated[...], weight[:, place], 1, 0))


def store_parts(parts, product):
    first = 0
    for part in parts:
        width = part.shape[1]
        part[...] = product(slice(first, first + width)).astype(bf16)
        first += width


def feed_body(pieces, grad_pieces, rows, grad_rows, active, grad_hidden, *refs):
    *parts, work, up_weight, down_weight = refs
    stage_rows(pieces, rows)
    stage_rows(grad_pieces, grad_rows)
    up_weight = up_weight()
    work[0] = contract(rows[...], up_weight[...], 1, 0)
    work[1] = contract(grad_rows[...], down_weight()[...], 1, 1)

    def finish(first):
        span = pl.ds(first, 32)
        hidden, grad_active = work[0, span, :], work[1, span, :]
        cumulative = 0.5 * (1.0 + lax.erf(hidden * 0.7071067811865476))
        density = jnp.exp(-0.5 * hidden * hidden) * 0.3989422804014327
        active[span, :] = (hidden * cumulative).astype(bf16)
        grad_hidden[span, :] = (grad_active * (cumulative + hidden * density)).astype(bf16)

    each_block(rows.shape[0], 32, finish)
    store_parts(parts, lambda place: contract(grad_hidden[...], up_weight[place, :], 1, 1))


def down_body(active, down_weight, *parts):
    (down_weight,) = down_weight
    for value, targets in zip(active, (parts[:1], parts[1:2], parts[2:])):
        store_parts(targets, lambda place: contract(value[...], down_weight[:, place], 1, 0))


def gate_body(pieces, gate, grouped, inverse, rows, grad_gate, grad_retained, work, out_weight):
    (gate,), (grouped,), (inverse,) = gate, grouped, inverse
    stage_rows(pieces, rows)
    work[...] = contract(rows[...], out_weight()[...], 1, 1)

    def finish(first):
        span = pl.ds(first, 64)
        grad_gated, pre, value = work[span, :], gate[span, :], grouped[span, :]
        sigma = sigmoid(pre)
        grad_gate[span, :] = (grad_gated * value * (sigma * (1.0 + pre * (1.0 - sigma)))).astype(bf16)
        grads = grad_gated * (pre * sigma)
        plain = jnp.mean(grads, axis=1, keepdims=True)
        cross = jnp.mean(grads * value, axis=1, keepdims=True)
        grad_retained[span, :] = (inverse[span, :] * (grads - plain - value * cross)).astype(bf16)

    each_block(rows.shape[0], 64, finish)


def query_body(grads, every, columns, rows, away, angles, split, grad_query, plain_query):
    (grads,), (columns,), (rows,), (away,), (angles,), (split,) = grads, columns, rows, away, angles, split
    chunks = away.shape[0]
    chunk = grads.shape[0] // chunks
    total = 0.0
    for array, place in spans_of(every):
        scores = contract(grads[...], array[:, 2 * KEY :], 1, 1)
        scores = jnp.concatenate(
            [
                (
                    scores[at * chunk : (at + 1) * chunk]
                    * decays(columns, rows, away, at, chunk, place, True)
                ).astype(bf16)
                for at in range(chunks)
            ],
            axis=0,
        )
        total = total + contract(scores, array[:, KEY : 2 * KEY], 1, 0)
    half = KEY // 2
    value = turn(total, angles[:, :half], -angles[:, half:]).astype(bf16)
    grad_query[...] = value
    plain_query[...] = contract(value, split[...], 1, 1).astype(bf16)


def key_body(
    own, every, every_grad, columns, rows, away, angles, split, others, stats,
    grad_key, plain_key, grad_value, sums, *refs,
):
    (own,), (columns,), (rows,), (away,), (angles,), (split,) = own, columns, rows, away, angles, split
    (grad_query, grad_gate), (stats,) = others, stats
    *parts, work, weights, tokens = refs
    chunks = away.shape[0]
    count = own.shape[0]
    chunk = count // chunks
    total_key, total_value = 0.0, 0.0
    for (array, place), grads in zip(spans_of(every), every_grad):
        scores = contract(own[:, KEY : 2 * KEY], array[:, :KEY], 1, 1)
        grad_scores = contract(own[:, 2 * KEY :], grads[...], 1, 1)
        intra, grad_intra = [], []
        for at in range(chunks):
            factor = decays(columns, rows, away, at, chunk, place, False)
            span = slice(at * chunk, (at + 1) * chunk)
            intra.append((scores[span] * factor).astype(bf16))
            grad_intra.append((grad_scores[span] * factor).astype(bf16))
        total_value = total_value + contract(jnp.concatenate(intra, axis=0), grads[...], 1, 0)
        total_key = total_key + contract(jnp.concatenate(grad_intra, axis=0), array[:, :KEY], 1, 0)
    half = KEY // 2
    value = (turn(total_key, angles[:, :half], -angles[:, half:]) * key_scale).astype(bf16)
    grad_key[...] = value
    plain_key[...] = contract(value, split[...], 1, 1).astype(bf16)
    grad_value[...] = total_value.astype(bf16)
    work[:, :KEY] = grad_query[...]
    work[:, KEY : 2 * KEY] = value
    work[:, 2 * KEY : QKV] = grad_value[...]
    work[:, QKV:] = grad_gate[...]
    average, inverse = stats[:, 0:1], stats[:, 1:2]
    weights, tokens = weights(), tokens()
    tile = 512
    first = 0
    for part in parts:
        for at in range(0, part.shape[1], tile):
            place = slice(first + at, first + at + tile)
            value = contract(work[...], weights[place, :], 1, 1)
            part[:, at : at + tile] = value.astype(bf16)
            unit = (tokens[:, place].astype(f32) - average) * inverse
            sums[0:1, place] = jnp.sum(value * unit, axis=0, keepdims=True)
            sums[1:2, place] = jnp.sum(value, axis=0, keepdims=True)
        first += part.shape[1]


def local(
    tokens,
    lengths,
    norm_gains,
    norm_biases,
    w_query,
    w_key,
    w_value,
    w_gate,
    w_out,
    w_up,
    w_down,
    out_grad,
):
    mp_size = lax.axis_size("mp")
    seq_size = lax.axis_size("seq")
    ranks = mp_size // HEADS
    mp_index = lax.axis_index("mp")
    head = mp_index // ranks
    rank = mp_index % ranks
    chunk, width = tokens.shape
    half = width // 2
    own_rows = chunk * HEADS
    sizes = [chunk * len(batch) for batch in BATCHES]

    def ring_shift(value, step):
        pairs = [
            (RING[k] * ranks + r, RING[(k + step) % HEADS] * ranks + r)
            for k in range(HEADS)
            for r in range(ranks)
        ]
        return lax.ppermute(value, "mp", pairs)

    def rank_shift(value, by):
        pairs = [(h * ranks + r, h * ranks + (r + by) % ranks) for h in range(HEADS) for r in range(ranks)]
        return lax.ppermute(value, "mp", pairs)

    def gather_ring(block, work=None, ready=(), hook=None):
        results = []
        hook = hook or (lambda step, pieces: None)

        def use(at, pieces):
            if work:
                results.append(work(at, after(pieces, results[-1:])))

        forth, back = block, block
        near = [block]
        for _ in range(2):
            forth, back = lax.optimization_barrier((ring_shift(forth, 1), ring_shift(back, -1)))
            near += [forth, back]
            hook(len(near) // 2, (forth, back))
        forth, back = after((forth, back), ready)
        forth, back = lax.optimization_barrier((ring_shift(forth, 1), ring_shift(back, -1)))
        hook(3, (forth, back))
        use(0, near)
        far = [forth, back]
        left, right = after((forth[:, :half], back[:, half:]), results)
        left, right = ring_shift(left, 1), ring_shift(right, -1)
        use(1, far)
        ends = list(lax.optimization_barrier((left, right)))
        hook(4, ends)
        use(2, ends)
        return [near, far, ends], results

    def stack(values):
        return values[0] if len(values) == 1 else jnp.concatenate(values, axis=0)

    def scatter_ring(*part_of, hook=None):
        count = len(part_of)
        steps, sends = [], []

        def shift(forth, back):
            forth, back = lax.optimization_barrier((forth, back))
            sends.append((forth, back))
            forth, back = lax.optimization_barrier((ring_shift(forth, 1), ring_shift(back, -1)))
            steps.append((forth, back))
            tie = hook(len(steps), sends[-1], steps[-1]) if hook else None
            forth, back = after((forth, back), tie) if tie is not None else (forth, back)
            forth, back = (
                [value[i * chunk : (i + 1) * chunk].astype(f32) for i in range(count)] for value in (forth, back)
            )
            return forth, back

        far = [part(2, ()) for part in part_of]
        forth, back = shift(stack([value[0] for value in far]), stack([value[1] for value in far]))
        parts = [part(1, sends[0]) for part in part_of]
        forth = stack(
            [
                jnp.concatenate([p[chunk:, :half].astype(f32) + value, p[chunk:, half:].astype(f32)], axis=1)
                for (p,), value in zip(parts, forth)
            ]
        ).astype(bf16)
        back = stack(
            [
                jnp.concatenate([p[:chunk, :half].astype(f32), p[:chunk, half:].astype(f32) + value], axis=1)
                for (p,), value in zip(parts, back)
            ]
        ).astype(bf16)

        def of(value, at):
            return value[at * chunk : (at + 1) * chunk].astype(f32)

        near = None
        for at in (4, 2):
            forth, back = shift(forth, back)
            near = near or [part(0, sends[1])[0] for part in part_of]
            forth = stack([of(p, at) + value for p, value in zip(near, forth)]).astype(bf16)
            back = stack([of(p, at - 1) + value for p, value in zip(near, back)]).astype(bf16)
        forth, back = shift(forth, back)
        return [of(p, 0) + f + b for p, f, b in zip(near, forth, back)], steps

    def collect(shard):
        return [shard] + [rank_shift(shard, t) for t in range(1, ranks)]

    def assemble(pieces, axis):
        ordered = []
        for spot in range(ranks):
            value = pieces[0]
            for t in range(1, ranks):
                value = jnp.where((rank - t + ranks) % ranks == spot, pieces[t], value)
            ordered.append(value)
        return jnp.concatenate(ordered, axis=axis)

    def batch_of(array, at, axis=0):
        first = FIRST[at] * chunk
        return lax.slice_in_dim(array, first, first + sizes[at], axis=axis)

    with jax.named_scope("head_weights"):
        split = np.zeros((KEY, KEY), np.float32)
        for i in range(KEY // 2):
            split[2 * i, i] = 1.0
            split[2 * i + 1, KEY // 2 + i] = 1.0
        split = jnp.asarray(split, bf16)

        def separate(weight):
            return jnp.dot(weight, split, preferred_element_type=f32).astype(bf16)

        query_pieces, key_pieces = collect(w_query), collect(w_key)
        value_pieces = collect(after(w_value, query_pieces[1:]))
        gate_pieces = collect(after(w_gate, key_pieces[1:]))
        in_weights = jnp.concatenate(
            [
                separate(assemble(query_pieces, 1)),
                separate(assemble(key_pieces, 1)),
                assemble(value_pieces, 1),
                assemble(gate_pieces, 1),
            ],
            axis=1,
        )
        out_weight = assemble(collect(after(w_out, value_pieces[1:])), 0)

    with jax.named_scope("row_places"):
        table = np.zeros((HEADS, HEADS), np.int32)
        for k, h in enumerate(RING):
            for j, offset in enumerate(OFFSETS):
                table[h, j] = RING[(k + offset) % HEADS]
        sources = lax.dynamic_slice_in_dim(jnp.asarray(table), head, 1, 0)[0]
        inner = jnp.arange(chunk, dtype=jnp.int32)
        row_ids = jnp.concatenate(
            [
                (((sources * ranks + (rank - t + ranks) % ranks) * chunk)[:, None] + inner[None, :]).reshape(-1)
                for t in range(ranks)
            ]
        )
        ends = jnp.cumsum(lengths[0], dtype=jnp.int32)
        starts = ends - lengths[0]
        member = (row_ids[:, None] >= starts[None, :]) & (row_ids[:, None] < ends[None, :])
        begins = jnp.sum(jnp.where(member, starts[None, :], 0), axis=1, dtype=jnp.int32)
        position = (row_ids - begins)[:own_rows]
        frequencies = 10000.0 ** (-jnp.arange(KEY // 2).astype(f32) / (KEY // 2))
        angles = position.astype(f32)[:, None] * frequencies[None, :]
        angles = jnp.concatenate([jnp.cos(angles), jnp.sin(angles)], axis=1)
        log_decay = jnp.log(1.0 - 2.0 ** (-5.0 - head.astype(f32)))
        bases = row_ids[:own_rows:chunk]
        away = bases[:, None] - row_ids[None, :]
        away_query = jnp.exp(jnp.maximum(away, 1 - chunk).astype(f32) * log_decay)
        away_key = jnp.exp(jnp.maximum(-away, 0).astype(f32) * log_decay)
        near = jnp.tile(inner.astype(f32) * log_decay, HEADS)
        columns = jnp.stack(
            [row_ids[:own_rows].astype(f32), begins[:own_rows].astype(f32), jnp.exp(near), jnp.exp(-near)],
            axis=1,
        )
        rows = jnp.stack([row_ids.astype(f32), begins.astype(f32)])

    def away_of(array, at):
        return array[FIRST[at] : FIRST[at] + len(BATCHES[at])]

    normed_rows, own_qkv, gate_pre, stats_one = [None] * 3, [None] * 3, [None] * 3, [None] * 3
    token_rows = [None] * 3
    norm = jnp.stack([norm_gains[0], norm_biases[0]])

    batch_angles = [batch_of(angles, at) for at in range(3)]
    batch_columns = [batch_of(columns, at) for at in range(3)]
    batch_away = [away_of(away_query, at) for at in range(3)]
    batch_away_key = [away_of(away_key, at) for at in range(3)]
    ready = (in_weights, out_weight, batch_angles, batch_columns, rows, batch_away, batch_away_key, norm)
    ready = lax.optimization_barrier(ready)
    in_weights, out_weight, batch_angles, batch_columns, rows, batch_away, batch_away_key, norm = ready

    def project(at, pieces):
        token_rows[at], normed_rows[at], own_qkv[at], gate_pre[at], stats_one[at] = run(
            project_body,
            "project",
            [
                ((sizes[at], width), bf16),
                ((sizes[at], width), bf16),
                ((sizes[at], QKV), bf16),
                ((sizes[at], VAL), f32),
                ((sizes[at], 2), f32),
            ],
            [],
            pieces,
            norm,
            batch_angles[at],
            late=[in_weights],
            flops=2 * sizes[at] * width * (QKV + VAL),
        )
        return own_qkv[at]

    with jax.named_scope("project_in"):
        token_pieces, _ = gather_ring(tokens, project, ready)
        every_qkv = list(own_qkv)
        for t in range(1, ranks):
            every_qkv += [rank_shift(value, t) for value in own_qkv]
    with jax.named_scope("gather_out_grad"):
        grad_steps = {}
        grad_pieces, _ = gather_ring(after(out_grad, token_pieces[1]), hook=grad_steps.__setitem__)
    with jax.named_scope("feed_weights"):
        up_weight = assemble(collect(after(w_up, token_pieces[2])), 1)
        down_weight = assemble(collect(after(w_down, token_pieces[2])), 0)

    grouped, inverse_group, gated_rows = [None] * 3, [None] * 3, [None] * 3

    def part_shapes(at):
        return [((sizes[at], half), bf16)] * 2 if at == 2 else [((sizes[at], width), bf16)]

    def branch_part(at, earlier):
        *part, gated_rows[at], grouped[at], inverse_group[at] = run(
            branch_body,
            "branch",
            part_shapes(at)
            + [
                ((sizes[at], VAL), bf16),
                ((sizes[at], VAL), f32),
                ((sizes[at], 1), f32),
            ],
            [((sizes[at], ranks * own_rows), bf16)],
            after(own_qkv[at], earlier, grad_steps[2 - at if at < 2 else 1] if at != 1 else ()),
            every_qkv,
            gate_pre[at],
            batch_columns[at],
            rows,
            batch_away[at],
            late=[out_weight],
            flops=2 * sizes[at] * (ranks * own_rows * (KEY + VAL) + VAL * width),
        )
        return part

    with jax.named_scope("retention"):
        (total,), _ = scatter_ring(branch_part)
        middle = tokens.astype(f32) + total

    def shard(left, right, left_sharded, spot):
        cuts = left if left_sharded else right
        cut = cuts.shape[1] // ranks
        piece = lax.dynamic_slice_in_dim(cuts, spot * cut, cut, 1)
        return contract(piece, right, 0, 0) if left_sharded else contract(left, piece, 0, 0)

    def send_shards(left, right, left_sharded):
        others = [shard(left, right, left_sharded, (rank + t) % ranks).astype(bf16) for t in range(1, ranks)]
        return others, [rank_shift(value, t + 1) for t, value in enumerate(others)]

    def own_shard(left, right, left_sharded, arrived):
        result = shard(left, right, left_sharded, rank)
        for value in arrived:
            result = result + value.astype(f32)
        return result.astype(bf16)

    def swap_groups(value, late):
        total = value.astype(f32)
        for t in range(1, seq_size):
            pairs = [(i, (i + t) % seq_size) for i in range(seq_size)]
            total = total + after(lax.ppermute(value, "seq", pairs), late).astype(f32)
        return total

    def joined(batches):
        return jnp.concatenate(batches, axis=0)

    def by_rank(*values):
        cuts = [value.shape[1] // ranks for value in values]
        return jnp.concatenate(
            [value[:, r * cut : (r + 1) * cut] for r in range(ranks) for value, cut in zip(values, cuts)], axis=1
        )

    with jax.named_scope("norm_two"):
        average, inverse_two = row_stats(middle)
        unit_two = (middle - average) * inverse_two
        normed_two = (unit_two * norm_gains[1] + norm_biases[1]).astype(bf16)
    up_parts, two_rows, grad_rows = [None] * 3, [None] * 3, [None] * 3
    active_rows, grad_hidden_rows = [None] * 3, [None] * 3

    def feed(at, pieces):
        two_rows[at], grad_rows[at], active_rows[at], grad_hidden_rows[at], *up_parts[at] = run(
            feed_body,
            "feed",
            [
                ((sizes[at], width), bf16),
                ((sizes[at], width), bf16),
                ((sizes[at], VAL), bf16),
                ((sizes[at], VAL), bf16),
            ]
            + part_shapes(at),
            [((2, sizes[at], VAL), f32)],
            pieces,
            grad_pieces[at],
            late=[up_weight, down_weight],
            flops=6 * sizes[at] * width * VAL,
        )
        return active_rows[at]

    with jax.named_scope("feed_forward"):
        gather_ring(normed_two, feed)
    early = {}

    def up_hook(step, sends, arrived):
        if step == 1:
            with jax.named_scope("down_grad"):
                left, right = joined(after(active_rows, sends)), joined(after(grad_rows, sends))
                early["others"], got = send_shards(left, right, True)
                early["down"] = own_shard(left, right, True, got)
        if step == 2:
            with jax.named_scope("up_grad"):
                left, right = joined(after(two_rows, sends)), joined(after(grad_hidden_rows, sends))
                others, got = send_shards(left, right, False)
                early["up"] = own_shard(left, right, False, got)
        if step == 3:
            with jax.named_scope("down_parts"):
                *parts, left, right = run(
                    down_body,
                    "down",
                    [((size, width), bf16) for size in sizes[:2]] + [((sizes[2], half), bf16)] * 2,
                    [],
                    after(active_rows, sends),
                    down_weight,
                    flops=2 * own_rows * width * VAL,
                )
                early["parts"] = [[value] for value in parts] + [[left, right]]

    with jax.named_scope("scatter_up"):
        (grad_normed_two,), up_steps = scatter_ring(lambda at, earlier: up_parts[at], hook=up_hook)
    down_own, up_own, down_parts = early["down"], early["up"], early["parts"]
    with jax.named_scope("norm_two_back"):
        grad_middle = out_grad.astype(f32) + normalize_back(
            grad_normed_two, unit_two, inverse_two, norm_gains[1]
        )
        grad_branch = grad_middle.astype(bf16)
        gain_two = jnp.sum(grad_normed_two * unit_two, axis=0)
        bias_two = jnp.sum(grad_normed_two, axis=0)

    branch_rows, grad_gate, own_grad = [None] * 3, [None] * 3, [None] * 3
    grad_query, plain_query = [None] * 3, [None] * 3

    def gate_back(at, pieces):
        branch_rows[at], grad_gate[at], own_grad[at] = run(
            gate_body,
            "gate_back",
            [
                ((sizes[at], width), bf16),
                ((sizes[at], VAL), bf16),
                ((sizes[at], VAL), bf16),
            ],
            [((sizes[at], VAL), f32)],
            pieces,
            gate_pre[at],
            grouped[at],
            inverse_group[at],
            late=[out_weight],
            flops=2 * sizes[at] * width * VAL,
        )
        return own_grad[at]

    with jax.named_scope("gate_back"):
        branch_pieces, _ = gather_ring(after(grad_branch, down_own, up_own, down_parts), gate_back)
        every_grad = list(own_grad)
        for t in range(1, ranks):
            every_grad += [rank_shift(value, t) for value in own_grad]
    with jax.named_scope("down_grad"):
        down_grad = swap_groups(down_own, branch_pieces[2])

    def query_back(at, earlier):
        with jax.named_scope("query_back"):
            grad_query[at], plain_query[at] = run(
                query_body,
                "query_back",
                [((sizes[at], KEY), bf16)] * 2,
                [],
                after(own_grad[at], earlier),
                every_qkv,
                batch_columns[at],
                rows,
                batch_away[at],
                batch_angles[at],
                split,
                free=True,
            )

    with jax.named_scope("out_grad"):
        out_sides = joined(gated_rows), joined(branch_rows), True
        out_others, out_got = send_shards(*out_sides)
    late_own = {}
    grad_value, plain_key = [None] * 3, [None] * 3
    norm_sums = []

    def in_part(at, earlier):
        if at == 2:
            query_back(at, out_others)
        if at == 1:
            with jax.named_scope("out_grad"):
                left, right, _ = after(out_sides, earlier)
                late_own["out"] = own_shard(left, right, True, out_got)
            with jax.named_scope("gate_grad"):
                sides = joined(normed_rows), joined(after(grad_gate, late_own["out"])), False
                others, got = send_shards(*sides)
            query_back(at, others)
        if at == 0:
            query_back(at, earlier)
            with jax.named_scope("gate_grad"):
                left, right, _ = after(late_own["sides"], earlier)
                late_own["gate"] = own_shard(left, right, False, late_own["got"])
        if at == 1:
            late_own["sides"], late_own["got"] = sides, got
        _, plain_key[at], grad_value[at], sums, *part = run(
            key_body,
            "key_back",
            [
                ((sizes[at], KEY), bf16),
                ((sizes[at], KEY), bf16),
                ((sizes[at], VAL), bf16),
                ((2, width), f32),
            ]
            + part_shapes(at),
            [((sizes[at], QKV + VAL), bf16)],
            after(own_qkv[at], earlier),
            every_qkv,
            every_grad,
            batch_columns[at],
            rows,
            batch_away_key[at],
            batch_angles[at],
            split,
            [grad_query[at], grad_gate[at]],
            stats_one[at],
            late=[in_weights, token_rows[at]],
            free=True,
        )
        norm_sums.append(sums)
        return part

    with jax.named_scope("key_back"):
        def in_hook(step, sends, arrived):
            if step == 4:
                late_own["end"] = sends
            if step != 3:
                return None
            with jax.named_scope("query_key_value_grad"):
                columns_last = by_rank(joined(grad_value), joined(plain_query), joined(plain_key))
                sides = late_own["sides"][0], columns_last, False
                others, got = send_shards(*sides)
                late_own["last"] = own_shard(*sides, got)
            return late_own["last"]

        (grad_normed_one, total), in_steps = scatter_ring(
            in_part, lambda at, earlier: down_parts[at], hook=in_hook
        )
        layer_out = middle + total
    with jax.named_scope("norm_one_back"):
        tokens_grad = grad_middle + normalize_back(
            grad_normed_one,
            (tokens.astype(f32) - stats_one[0][:chunk, 0:1]) * stats_one[0][:chunk, 1:2],
            stats_one[0][:chunk, 1:2],
            norm_gains[0],
        )

    def sum_groups(value):
        result = value
        for t in range(1, seq_size):
            pairs = [(i, (i + t) % seq_size) for i in range(seq_size)]
            result = result + lax.ppermute(value, "seq", pairs)
        return result

    with jax.named_scope("norm_grads"):
        gain_one, bias_one = sum(norm_sums)
        total_sums = jnp.stack([gain_one, gain_two, bias_one, bias_two])
        total_sums = after(total_sums, late_own["end"])
        total = total_sums
        for t in range(1, ranks):
            total = total + rank_shift(total_sums, t)
        for bit in (1, 2, 4):
            pairs = [(h * ranks + r, (h ^ bit) * ranks + r) for h in range(HEADS) for r in range(ranks)]
            total = total + lax.ppermute(total, "mp", pairs)
        span = width // mp_size
        mine = sum_groups(lax.dynamic_slice_in_dim(total, mp_index * span, span, 1))

    with jax.named_scope("up_grad"):
        up_grad = swap_groups(up_own, in_steps[0])
    with jax.named_scope("out_grad"):
        out_weight_grad = swap_groups(late_own["out"], in_steps[2])
    with jax.named_scope("gate_grad"):
        gate_grad = swap_groups(late_own["gate"], late_own["end"])
    with jax.named_scope("query_key_value_grad"):
        last = swap_groups(late_own["last"], in_steps[3])
        value_end, query_end = VAL // ranks, (VAL + KEY) // ranks
        value_grad, query_grad, key_grad = last[:, :value_end], last[:, value_end:query_end], last[:, query_end:]
    return (
        layer_out,
        tokens_grad,
        query_grad,
        key_grad,
        value_grad,
        gate_grad,
        out_weight_grad,
        up_grad,
        down_grad,
        mine[:2],
        mine[2:],
    )


def solution(mesh):
    return jax.shard_map(
        local,
        mesh=mesh,
        in_specs=(
            P(("seq", "mp"), None),
            P("seq", None),
            P(),
            P(),
            P(None, "mp"),
            P(None, "mp"),
            P(None, "mp"),
            P(None, "mp"),
            P("mp", None),
            P(None, "mp"),
            P("mp", None),
            P(("seq", "mp"), None),
        ),
        out_specs=(
            P(("seq", "mp"), None),
            P(("seq", "mp"), None),
            P(None, "mp"),
            P(None, "mp"),
            P(None, "mp"),
            P(None, "mp"),
            P("mp", None),
            P(None, "mp"),
            P("mp", None),
            P(None, "mp"),
            P(None, "mp"),
        ),
        check_vma=False,
    )
```

time: 601 us -> 512 us (0.85)
  matrix products: 194 us -> 36.5 us
  Pallas kernels: 0 us -> 81.6 us
  waiting for transfers between devices: 177 us -> 243 us
  other arithmetic: 78.2 us -> 35.8 us
  local copies, waits for them, and re-layouts: 51.9 us -> 30.6 us
  starting transfers between devices: 84.3 us -> 72.6 us
    dot_general x40 -> x0, matrix products: 108 us -> none  [the longest x5 19.7 us: local(): jnp.dot(intra, all_grad, preferred_element_type=f32).astype(bf16)]
    pallas_call x0 -> x19, Pallas kernels: none -> 81.6 us  [run(): pl.pallas_call(kernel, out_shape=[jax.ShapeDtypeStruct(shape, dtype) for...]
    ppermute x64 -> x56, waiting for transfers between devices: 113 us -> 167 us  [ring_shift(): return lax.ppermute(value, 'mp', pairs)]
    dot_general x36 -> x10, matrix products: 82.3 us -> 32.8 us  [contract(): lax.dot_general(left_side, right_side, (((left_dim,), (right_dim,)), ((),...]
    ppermute x0 -> x5, waiting for transfers between devices: none -> 32.6 us  [swap_groups(): total = total + after(lax.ppermute(value, 'seq', pairs), late).astype(f32)]
    unnamed x27 -> x3, other arithmetic: 23.3 us -> 0.73 us
    dynamic_update_slice x13 -> x0, local copies, waits for them, and re-layouts: 16 us -> none  [place(): return lax.dynamic_update_slice(buffer, piece, (first, 0))]
    convert_element_type x18 -> x9, other arithmetic: 22 us -> 6.97 us  [the longest x4 4.91 us: scatter_ring(): stack([of(p, at - 1) + value for p, value in zip(near, back)]).astype(bf16)]
  transfers between devices with their start and end apart: 100 -> 84, of which waited for: 41 -> 44; matrix products, arithmetic and copies ran while one was open for 52% -> 16% of each run, Pallas kernels for 0% -> 16%
where the time goes in v2:
time: 512 us; the launch traced here: 504 us
  waiting for transfers between devices  243 us (47%)
  Pallas kernels  81.6 us (16%)
  starting transfers between devices  72.6 us (14%)
  matrix products  36.5 us (7%)
  other arithmetic  35.8 us (7%)
  local copies, waits for them, and re-layouts  30.6 us (6%)
    ppermute x56, waiting for transfers between devices, ring_shift(): return lax.ppermute(value, 'mp', pairs)  167 us
    pallas_call x19, Pallas kernels, run(): pl.pallas_call(kernel, out_shape=[jax.ShapeDtypeStruct(shape, dtype) for...  81.6 us
    ppermute x56, starting transfers between devices, ring_shift(): return lax.ppermute(value, 'mp', pairs)  60.3 us
    ppermute x1, waiting for transfers between devices, sum_groups(): result = result + lax.ppermute(value, 'seq', pairs)  41.3 us
    dot_general x10, matrix products, contract(): lax.dot_general(left_side, right_side, (((left_dim,), (right_dim,)), ((),...  32.8 us
    ppermute x5, waiting for transfers between devices, swap_groups(): total = total + after(lax.ppermute(value, 'seq', pairs), late).astype(f32)  32.6 us
    unnamed x287, local copies, waits for them, and re-layouts  19 us
  transfers between devices with their start and end apart: 84, of which 44 were waited for; matrix products, arithmetic and copies ran while one was open for 16% of the time, Pallas kernels for 16%

profile of v2, /device:TPU:0, one launch (start us, length us, event | category | flops | bytes accessed | tf_op | source)
XLA Modules:
  0.0 503.9 jit_solution(5119689646741998148)
XLA Ops:
  0.7 3.1 collective-permute-start
  9.5 1.9 multiply_sine_fusion
  24.3 5.5 %collective-permute-done.2.refs_3_ = bf16[128,2048]{1,0:T(8,128)(2,1)S(1)} collective-permute-done((bf16[128,2048]{1,0:T(8,128)(2,1)S(1)}, bf16[128,2048]{1,0:T(8,128)(2,1)S(1)}, u32[]{:S(2)}, u32[]{:S(2)}) %collective-permute-start.2) | collective-permute-done | bytes 524320 | tf_op jit(solution)/shard_map/project_in/ppermute | solution.py:363
  36.8 7.5 %project.3 = (bf16[640,2048]{1,0:T(8,128)(2,1)S(1)}, bf16[640,2048]{1,0:T(8,128)(2,1)}, bf16[640,1024]{1,0:T(8,128)(2,1)S(1)}, f32[640,512]{1,0:T(8,128)S(1)}, f32[640,2]{1,0:T(8,128)S(1)}) custom-call(bf16[128,2048]{1,0:T(8,128)(2,1)S(1)} %copy-done.11, bf16[128,2048]{1,0:T(8,128)(2,1)S(1)} %collective-permute-done.refs_1_, ...), custom_call_target="tpu_custom_call" | custom-call | flops 4026531840 | bytes 17454080 | tf_op jit(solution)/shard_map/project_in/project/pallas_call | solution.py:97
  46.5 2.6 collective-permute-done.9.refs_0_
  55.1 4.6 project.4
  61.7 8.9 %collective-permute-done.12.refs_1_ = bf16[128,1024]{1,0:T(8,128)(2,1)S(1)} collective-permute-done((bf16[128,1024]{1,0:T(8,128)(2,1)S(1)}, bf16[128,1024]{1,0:T(8,128)(2,1)S(1)}, u32[]{:S(2)}, u32[]{:S(2)}) %collective-permute-start.12) | collective-permute-done | bytes 262176 | tf_op jit(solution)/shard_map/project_in/ppermute | solution.py:363
  70.6 2.0 project.5
  80.8 2.8 branch.4
  83.6 9.2 %collective-permute-done.18 = bf16[128,1024]{1,0:T(8,128)(2,1)S(1)} collective-permute-done((bf16[128,1024]{1,0:T(8,128)(2,1)S(1)}, bf16[128,1024]{1,0:T(8,128)(2,1)S(1)}, u32[]{:S(2)}, u32[]{:S(2)}) %collective-permute-start.18) | collective-permute-done | bytes 262176 | tf_op jit(solution)/shard_map/retention/ppermute | solution.py:363
  96.0 7.4 %branch.5 = (bf16[640,2048]{1,0:T(8,128)(2,1)}, bf16[640,512]{1,0:T(8,128)(2,1)S(1)}, f32[640,512]{1,0:T(8,128)S(1)}, f32[640,1]{1,0:T(8,128)S(1)}) custom-call(bf16[640,1024]{1,0:T(8,128)(2,1)S(1)} %get-tuple-element.493.refs_1_.refs_0_, bf16[640,1024]{1,0:T(8,128)(2,1)S(1)} %get-tuple-element.493.refs_1_.refs_0_, ...), custom_call_target="tpu_custom_call" | custom-call | flops 3355443200 | bytes 13570560 | tf_op jit(solution)/shard_map/retention/branch/pallas_call | solution.py:97
  103.5 3.6 collective-permute-done.22
  111.1 10.0 %collective-permute-done.24 = bf16[128,2048]{1,0:T(8,128)(2,1)S(1)} collective-permute-done((bf16[128,2048]{1,0:T(8,128)(2,1)S(1)}, bf16[128,2048]{1,0:T(8,128)(2,1)S(1)}, u32[]{:S(2)}, u32[]{:S(2)}) %collective-permute-start.24) | collective-permute-done | bytes 524320 | tf_op jit(solution)/shard_map/retention/ppermute | solution.py:363
  121.5 2.6 add_convert_fusion.18
  127.4 12.1 %collective-permute-done.26 = bf16[128,2048]{1,0:T(8,128)(2,1)} collective-permute-done((bf16[128,2048]{1,0:T(8,128)(2,1)}, bf16[128,2048]{1,0:T(8,128)(2,1)}, u32[]{:S(2)}, u32[]{:S(2)}) %collective-permute-start.26) | collective-permute-done | bytes 524320 | tf_op jit(solution)/shard_map/retention/ppermute | solution.py:363
  140.8 2.0 fusion.78
  145.7 13.7 %collective-permute-done.29.refs_2_ = bf16[128,2048]{1,0:T(8,128)(2,1)S(1)} collective-permute-done((bf16[128,2048]{1,0:T(8,128)(2,1)S(1)}, bf16[128,2048]{1,0:T(8,128)(2,1)S(1)}, u32[]{:S(2)}, u32[]{:S(2)}) %collective-permute-start.29) | collective-permute-done | bytes 524320 | tf_op jit(solution)/shard_map/feed_forward/ppermute | solution.py:363
  163.8 10.5 %collective-permute-done.30.refs_3_ = bf16[128,2048]{1,0:T(8,128)(2,1)S(1)} collective-permute-done((bf16[128,2048]{1,0:T(8,128)(2,1)S(1)}, bf16[128,2048]{1,0:T(8,128)(2,1)S(1)}, u32[]{:S(2)}, u32[]{:S(2)}) %collective-permute-start.30) | collective-permute-done | bytes 524320 | tf_op jit(solution)/shard_map/feed_forward/ppermute | solution.py:363
  180.4 8.3 %feed.3 = (bf16[640,2048]{1,0:T(8,128)(2,1)}, bf16[640,2048]{1,0:T(8,128)(2,1)}, bf16[640,512]{1,0:T(8,128)(2,1)S(1)}, bf16[640,512]{1,0:T(8,128)(2,1)S(1)}, bf16[640,2048]{1,0:T(8,128)(2,1)}) custom-call(bf16[128,2048]{1,0:T(8,128)(2,1)S(1)} %add_convert_fusion.17.refs_0_, bf16[128,2048]{1,0:T(8,128)(2,1)S(1)} %collective-permute-done.28.refs_1_, ...), custom_call_target="tpu_custom_call" | custom-call | flops 4026531840 | bytes 18612224 | tf_op jit(solution)/shard_map/feed_forward/feed/pallas_call | solution.py:97
  190.9 3.0 feed.4
  193.9 2.1 collective-permute-done.38.refs_0_
  197.7 2.6 feed.5
  203.0 2.6 convolution_convert_fusion.4
  208.0 2.0 collective-permute-start.44
  210.8 9.5 %collective-permute-done.44 = bf16[128,2048]{1,0:T(8,128)(2,1)S(1)} collective-permute-done((bf16[128,2048]{1,0:T(8,128)(2,1)S(1)}, bf16[128,2048]{1,0:T(8,128)(2,1)S(1)}, u32[]{:S(2)}, u32[]{:S(2)}) %collective-permute-start.44) | collective-permute-done | bytes 524320 | tf_op jit(solution)/shard_map/scatter_up/ppermute | solution.py:363
  221.8 1.8 collective-permute-start.46
  223.9 2.3 convolution_convert_fusion.3
  226.2 2.3 down.1
  228.6 3.6 collective-permute-done.46
  232.2 2.1 collective-permute-done.47
  234.8 1.9 collective-permute-start.48
  236.9 4.7 add_convert_fusion.4
  241.6 3.6 add_convert_fusion.3
  247.5 1.8 fusion.77
  251.3 9.0 %collective-permute-done.53.refs_2_ = bf16[128,2048]{1,0:T(8,128)(2,1)} collective-permute-done((bf16[128,2048]{1,0:T(8,128)(2,1)}, bf16[128,2048]{1,0:T(8,128)(2,1)}, u32[]{:S(2)}, u32[]{:S(2)}) %collective-permute-start.53) | collective-permute-done | bytes 524320 | tf_op jit(solution)/shard_map/gate_back/ppermute | solution.py:363
  260.3 2.1 collective-permute-done.52.refs_1_
  264.5 2.1 constant_dynamic-update-slice_fusion.20
  268.4 8.3 %collective-permute-done.54.refs_3_ = bf16[128,2048]{1,0:T(8,128)(2,1)S(1)} collective-permute-done((bf16[128,2048]{1,0:T(8,128)(2,1)}, bf16[128,2048]{1,0:T(8,128)(2,1)S(1)}, u32[]{:S(2)}, u32[]{:S(2)}) %collective-permute-start.54) | collective-permute-done | bytes 524320 | tf_op jit(solution)/shard_map/gate_back/ppermute | solution.py:363
  276.7 1.8 collective-permute-done.55.refs_4_
  278.5 2.0 collective-permute-start.57
  282.0 6.5 %gate_back.3 = (bf16[640,2048]{1,0:T(8,128)(2,1)}, bf16[640,512]{1,0:T(8,128)(2,1)S(1)}, bf16[640,512]{1,0:T(8,128)(2,1)S(1)}) custom-call(bf16[128,2048]{1,0:T(8,128)(2,1)} %get-tuple-element.432.refs_0_, bf16[128,2048]{1,0:T(8,128)(2,1)} %collective-permute-done.52.refs_1_, bf16[128,2048]{1,0:T(8,128)(2,1)} %collective-permute-done.53.refs_2_, ...), custom_call_target="tpu_custom_call" | custom-call | flops 1342177280 | bytes 11274752 | tf_op jit(solution)/shard_map/gate_back/gate_back/pallas_call | solution.py:97
  288.7 3.6 constant_dynamic-update-slice_fusion.17
  292.6 2.2 collective-permute-start.59
  297.8 3.3 collective-permute-done.58.refs_0_
  303.9 4.6 convolution_convert_fusion.2
  310.6 5.0 key_back.3
  319.7 10.1 %collective-permute-done.64 = bf16[256,1024]{1,0:T(8,128)(2,1)S(1)} collective-permute-done((bf16[256,1024]{1,0:T(8,128)(2,1)S(1)}, bf16[256,1024]{1,0:T(8,128)(2,1)S(1)}, u32[]{:S(2)}, u32[]{:S(2)}) %collective-permute-start.64) | collective-permute-done | bytes 524320 | tf_op jit(solution)/shard_map/key_back/ppermute | solution.py:363
  330.7 4.9 add_convert_fusion.2
  335.7 2.3 convolution_convert_fusion.1
  339.7 4.7 key_back.4
  346.5 1.8 collective-permute-start.67
  348.4 3.1 query_back.5
  351.5 14.0 %key_back.5 = (bf16[640,256]{1,0:T(8,128)(2,1)}, bf16[640,256]{1,0:T(8,128)(2,1)S(1)}, bf16[640,512]{1,0:T(8,128)(2,1)S(1)}, f32[2,2048]{1,0:T(2,128)S(1)}, bf16[640,2048]{1,0:T(8,128)(2,1)}) custom-call(bf16[640,1024]{1,0:T(8,128)(2,1)S(1)} %get-tuple-element.493.refs_1_.refs_0_, bf16[640,1024]{1,0:T(8,128)(2,1)S(1)} %get-tuple-element.493.refs_1_.refs_0_, ...), custom_call_target="tpu_custom_call" | custom-call | tf_op jit(solution)/shard_map/key_back/key_back/pallas_call | solution.py:97
  366.3 2.7 convolution_convert_fusion
  370.7 2.0 add_convert_fusion.9
  375.2 21.8 %collective-permute-done.68 = bf16[256,2048]{1,0:T(8,128)(2,1)S(1)} collective-permute-done((bf16[256,2048]{1,0:T(8,128)(2,1)S(1)}, bf16[256,2048]{1,0:T(8,128)(2,1)S(1)}, u32[]{:S(2)}, u32[]{:S(2)}) %collective-permute-start.68) | collective-permute-done | bytes 1048608 | tf_op jit(solution)/shard_map/key_back/ppermute | solution.py:363
  397.1 2.5 add_convert_fusion
  401.6 2.9 convert_add_fusion.1
  406.8 2.6 add_convert_fusion.1
  412.0 2.7 convert_add_fusion.2
  417.1 13.5 %collective-permute-done.76 = bf16[256,2048]{1,0:T(8,128)(2,1)S(1)} collective-permute-done((bf16[256,2048]{1,0:T(8,128)(2,1)S(1)}, bf16[256,2048]{1,0:T(8,128)(2,1)S(1)}, u32[]{:S(2)}, u32[]{:S(2)}) %collective-permute-start.76) | collective-permute-done | bytes 1048608 | tf_op jit(solution)/shard_map/out_grad/ppermute | solution.py:614
  434.0 19.0 %collective-permute-done.75 = bf16[2048,256]{1,0:T(8,128)(2,1)S(1)} collective-permute-done((bf16[2048,256]{1,0:T(8,128)(2,1)S(1)}, bf16[2048,256]{1,0:T(8,128)(2,1)S(1)}, u32[]{:S(2)}, u32[]{:S(2)}) %collective-permute-start.75) | collective-permute-done | bytes 1048608 | tf_op jit(solution)/shard_map/gate_grad/ppermute | solution.py:614
  455.3 41.3 %collective-permute-done.83 = f32[4,128]{1,0:T(4,128)S(1)} collective-permute-done((f32[4,128]{1,0:T(4,128)S(1)}, f32[4,128]{1,0:T(4,128)S(1)}, u32[]{:S(2)}, u32[]{:S(2)}) %collective-permute-start.83) | collective-permute-done | bytes 2080 | tf_op jit(solution)/shard_map/norm_grads/ppermute | solution.py:819
  497.7 2.1 fusion.10
  (542 shorter events, 131.4 us)
Async XLA Ops:
  0.7 15.2 %collective-permute-start = (bf16[128,2048]{1,0:T(8,128)(2,1)}, bf16[128,2048]{1,0:T(8,128)(2,1)S(1)}, u32[]{:S(2)}, u32[]{:S(2)}) collective-permute-start(bf16[128,2048]{1,0:T(8,128)(2,1)} %refs_0_), channel_id=1, source_target_pairs={{0,4},{1,5},{4,8},{5,9},{8,12},{9,13},{12,14},{13,15},{14,10},{15,... | collective-permute-start | bytes 1572872 | tf_op jit(solution)/shard_map/project_in/ppermute | solution.py:363
  3.7 13.6 %collective-permute-start.1 = (bf16[128,2048]{1,0:T(8,128)(2,1)}, bf16[128,2048]{1,0:T(8,128)(2,1)S(1)}, u32[]{:S(2)}, u32[]{:S(2)}) collective-permute-start(bf16[128,2048]{1,0:T(8,128)(2,1)} %refs_0_), channel_id=1, source_target_pairs={{0,2},{1,3},{4,0},{5,1},{8,4},{9,5},{12,8},{13,9},{14,12},{15,13},... | collective-permute-start | bytes 1572872 | tf_op jit(solution)/shard_map/project_in/ppermute | solution.py:363
  17.3 12.5 %collective-permute-start.2 = (bf16[128,2048]{1,0:T(8,128)(2,1)S(1)}, bf16[128,2048]{1,0:T(8,128)(2,1)S(1)}, u32[]{:S(2)}, u32[]{:S(2)}) collective-permute-start(bf16[128,2048]{1,0:T(8,128)(2,1)S(1)} %collective-permute-done.refs_1_), channel_id=1, source_target_pairs={{0,4},{1,5},{4,8},{5,9},{8,12},{9,13},{12,14},{13,15},{14,10},{15,... | collective-permute-start | bytes 1572872 | tf_op jit(solution)/shard_map/project_in/ppermute | solution.py:363
  18.9 12.2 %collective-permute-start.3 = (bf16[128,2048]{1,0:T(8,128)(2,1)S(1)}, bf16[128,2048]{1,0:T(8,128)(2,1)S(1)}, u32[]{:S(2)}, u32[]{:S(2)}) collective-permute-start(bf16[128,2048]{1,0:T(8,128)(2,1)S(1)} %collective-permute-done.1.refs_2_), channel_id=1, source_target_pairs={{0,2},{1,3},{4,0},{5,1},{8,4},{9,5},{12,8},{13,9},{14,12},{15,13},... | collective-permute-start | bytes 1572872 | tf_op jit(solution)/shard_map/project_in/ppermute | solution.py:363
  19.4 12.3 %collective-permute-start.7 = (bf16[2048,256]{1,0:T(8,128)(2,1)}, bf16[2048,256]{1,0:T(8,128)(2,1)S(1)}, u32[]{:S(2)}, u32[]{:S(2)}) collective-permute-start(bf16[2048,256]{1,0:T(8,128)(2,1)} %param.21), channel_id=1, source_target_pairs={{0,1},{1,0},{2,3},{3,2},{4,5},{5,4},{6,7},{7,6},{8,9},{9,8},{10,11... | collective-permute-start | bytes 3145736 | tf_op jit(solution)/shard_map/head_weights/ppermute | solution.py:367
  19.4 11.7 %collective-permute-start.6 = (bf16[2048,256]{1,0:T(8,128)(2,1)}, bf16[2048,256]{1,0:T(8,128)(2,1)S(1)}, u32[]{:S(2)}, u32[]{:S(2)}) collective-permute-start(bf16[2048,256]{1,0:T(8,128)(2,1)} %param.20), channel_id=1, source_target_pairs={{0,1},{1,0},{2,3},{3,2},{4,5},{5,4},{6,7},{7,6},{8,9},{9,8},{10,11... | collective-permute-start | bytes 3145736 | tf_op jit(solution)/shard_map/head_weights/ppermute | solution.py:367
  34.8 14.3 %collective-permute-start.9 = (bf16[128,2048]{1,0:T(8,128)(2,1)S(1)}, bf16[128,2048]{1,0:T(8,128)(2,1)S(1)}, u32[]{:S(2)}, u32[]{:S(2)}) collective-permute-start(bf16[128,2048]{1,0:T(8,128)(2,1)S(1)} %collective-permute-done.2.refs_3_), channel_id=1, source_target_pairs={{0,4},{1,5},{4,8},{5,9},{8,12},{9,13},{12,14},{13,15},{14,10},{15,... | collective-permute-start | bytes 1572872 | tf_op jit(solution)/shard_map/project_in/ppermute | solution.py:363
  36.4 14.0 %collective-permute-start.10 = (bf16[128,2048]{1,0:T(8,128)(2,1)S(1)}, bf16[128,2048]{1,0:T(8,128)(2,1)S(1)}, u32[]{:S(2)}, u32[]{:S(2)}) collective-permute-start(bf16[128,2048]{1,0:T(8,128)(2,1)S(1)} %collective-permute-done.3.refs_4_), channel_id=1, source_target_pairs={{0,2},{1,3},{4,0},{5,1},{8,4},{9,5},{12,8},{13,9},{14,12},{15,13},... | collective-permute-start | bytes 1572872 | tf_op jit(solution)/shard_map/project_in/ppermute | solution.py:363
  46.5 28.4 %collective-permute-start.15 = (bf16[640,1024]{1,0:T(8,128)(2,1)S(1)}, bf16[640,1024]{1,0:T(8,128)(2,1)S(1)}, u32[]{:S(2)}, u32[]{:S(2)}) collective-permute-start(bf16[640,1024]{1,0:T(8,128)(2,1)S(1)} %get-tuple-element.493.refs_1_.refs_0_), channel_id=1, source_target_pairs={{0,1},{1,0},{2,3},{3,2},{4,5},{5,4},{6,7},{7,6},{8,9},{9,8},{10,11... | collective-permute-start | bytes 3932168 | tf_op jit(solution)/shard_map/project_in/ppermute | solution.py:367
  52.1 20.7 %collective-permute-start.14 = (bf16[128,2048]{1,0:T(8,128)(2,1)S(1)}, bf16[128,2048]{1,0:T(8,128)(2,1)S(1)}, u32[]{:S(2)}, u32[]{:S(2)}) collective-permute-start(bf16[128,2048]{1,0:T(8,128)(2,1)S(1)} %copy-done.42), channel_id=1, source_target_pairs={{0,2},{1,3},{4,0},{5,1},{8,4},{9,5},{12,8},{13,9},{14,12},{15,13},... | collective-permute-start | bytes 1572872 | tf_op jit(solution)/shard_map/gather_out_grad/ppermute | solution.py:363
  52.6 20.3 %collective-permute-start.13 = (bf16[128,2048]{1,0:T(8,128)(2,1)S(1)}, bf16[128,2048]{1,0:T(8,128)(2,1)S(1)}, u32[]{:S(2)}, u32[]{:S(2)}) collective-permute-start(bf16[128,2048]{1,0:T(8,128)(2,1)S(1)} %copy-done.42), channel_id=1, source_target_pairs={{0,4},{1,5},{4,8},{5,9},{8,12},{9,13},{12,14},{13,15},{14,10},{15,... | collective-permute-start | bytes 1572872 | tf_op jit(solution)/shard_map/gather_out_grad/ppermute | solution.py:363
  54.1 16.5 %collective-permute-start.12 = (bf16[128,1024]{1,0:T(8,128)(2,1)S(1)}, bf16[128,1024]{1,0:T(8,128)(2,1)S(1)}, u32[]{:S(2)}, u32[]{:S(2)}) collective-permute-start(bf16[128,1024]{1,0:T(8,128)(2,1)S(1)} %slice.297), channel_id=1, source_target_pairs={{0,2},{1,3},{4,0},{5,1},{8,4},{9,5},{12,8},{13,9},{14,12},{15,13},... | collective-permute-start | bytes 786440 | tf_op jit(solution)/shard_map/project_in/ppermute | solution.py:363
  61.7 13.3 %collective-permute-start.16 = (bf16[256,1024]{1,0:T(8,128)(2,1)S(1)}, bf16[256,1024]{1,0:T(8,128)(2,1)S(1)}, u32[]{:S(2)}, u32[]{:S(2)}) collective-permute-start(bf16[256,1024]{1,0:T(8,128)(2,1)S(1)} %get-tuple-element.473.refs_2_.refs_0_), channel_id=1, source_target_pairs={{0,1},{1,0},{2,3},{3,2},{4,5},{5,4},{6,7},{7,6},{8,9},{9,8},{10,11... | collective-permute-start | bytes 1572872 | tf_op jit(solution)/shard_map/project_in/ppermute | solution.py:367
  72.8 23.1 %collective-permute-start.20 = (bf16[128,2048]{1,0:T(8,128)(2,1)S(1)}, bf16[128,2048]{1,0:T(8,128)(2,1)S(1)}, u32[]{:S(2)}, u32[]{:S(2)}) collective-permute-start(bf16[128,2048]{1,0:T(8,128)(2,1)S(1)} %collective-permute-done.13.refs_6_), channel_id=1, source_target_pairs={{0,4},{1,5},{4,8},{5,9},{8,12},{9,13},{12,14},{13,15},{14,10},{15,... | collective-permute-start | bytes 1572872 | tf_op jit(solution)/shard_map/gather_out_grad/ppermute | solution.py:363
  73.9 22.0 %collective-permute-start.21 = (bf16[128,2048]{1,0:T(8,128)(2,1)S(1)}, bf16[128,2048]{1,0:T(8,128)(2,1)S(1)}, u32[]{:S(2)}, u32[]{:S(2)}) collective-permute-start(bf16[128,2048]{1,0:T(8,128)(2,1)S(1)} %collective-permute-done.14.refs_7_), channel_id=1, source_target_pairs={{0,2},{1,3},{4,0},{5,1},{8,4},{9,5},{12,8},{13,9},{14,12},{15,13},... | collective-permute-start | bytes 1572872 | tf_op jit(solution)/shard_map/gather_out_grad/ppermute | solution.py:363
  78.7 14.1 %collective-permute-start.18 = (bf16[128,1024]{1,0:T(8,128)(2,1)S(1)}, bf16[128,1024]{1,0:T(8,128)(2,1)S(1)}, u32[]{:S(2)}, u32[]{:S(2)}) collective-permute-start(bf16[128,1024]{1,0:T(8,128)(2,1)S(1)} %get-tuple-element.321), channel_id=1, source_target_pairs={{0,4},{1,5},{4,8},{5,9},{8,12},{9,13},{12,14},{13,15},{14,10},{15,... | collective-permute-start | bytes 786440 | tf_op jit(solution)/shard_map/retention/ppermute | solution.py:363
  79.7 13.8 %collective-permute-start.19 = (bf16[128,1024]{1,0:T(8,128)(2,1)S(1)}, bf16[128,1024]{1,0:T(8,128)(2,1)S(1)}, u32[]{:S(2)}, u32[]{:S(2)}) collective-permute-start(bf16[128,1024]{1,0:T(8,128)(2,1)S(1)} %get-tuple-element.322), channel_id=1, source_target_pairs={{0,2},{1,3},{4,0},{5,1},{8,4},{9,5},{12,8},{13,9},{14,12},{15,13},... | collective-permute-start | bytes 786440 | tf_op jit(solution)/shard_map/retention/ppermute | solution.py:363
  93.8 13.3 %collective-permute-start.22 = (bf16[128,2048]{1,0:T(8,128)(2,1)S(1)}, bf16[128,2048]{1,0:T(8,128)(2,1)S(1)}, u32[]{:S(2)}, u32[]{:S(2)}) collective-permute-start(bf16[128,2048]{1,0:T(8,128)(2,1)S(1)} %pad_maximum_fusion.7), channel_id=1, source_target_pairs={{0,4},{1,5},{4,8},{5,9},{8,12},{9,13},{12,14},{13,15},{14,10},{15,... | collective-permute-start | bytes 1572872 | tf_op jit(solution)/shard_map/retention/ppermute | solution.py:363
  94.5 12.9 %collective-permute-start.23 = (bf16[128,2048]{1,0:T(8,128)(2,1)S(1)}, bf16[128,2048]{1,0:T(8,128)(2,1)S(1)}, u32[]{:S(2)}, u32[]{:S(2)}) collective-permute-start(bf16[128,2048]{1,0:T(8,128)(2,1)S(1)} %pad_maximum_fusion.8), channel_id=1, source_target_pairs={{0,2},{1,3},{4,0},{5,1},{8,4},{9,5},{12,8},{13,9},{14,12},{15,13},... | collective-permute-start | bytes 1572872 | tf_op jit(solution)/shard_map/retention/ppermute | solution.py:363
  109.0 12.1 %collective-permute-start.24 = (bf16[128,2048]{1,0:T(8,128)(2,1)S(1)}, bf16[128,2048]{1,0:T(8,128)(2,1)S(1)}, u32[]{:S(2)}, u32[]{:S(2)}) collective-permute-start(bf16[128,2048]{1,0:T(8,128)(2,1)S(1)} %get-tuple-element.337), channel_id=1, source_target_pairs={{0,4},{1,5},{4,8},{5,9},{8,12},{9,13},{12,14},{13,15},{14,10},{15,... | collective-permute-start | bytes 1572872 | tf_op jit(solution)/shard_map/retention/ppermute | solution.py:363
  109.6 11.9 %collective-permute-start.25 = (bf16[128,2048]{1,0:T(8,128)(2,1)S(1)}, bf16[128,2048]{1,0:T(8,128)(2,1)S(1)}, u32[]{:S(2)}, u32[]{:S(2)}) collective-permute-start(bf16[128,2048]{1,0:T(8,128)(2,1)S(1)} %get-tuple-element.338), channel_id=1, source_target_pairs={{0,2},{1,3},{4,0},{5,1},{8,4},{9,5},{12,8},{13,9},{14,12},{15,13},... | collective-permute-start | bytes 1572872 | tf_op jit(solution)/shard_map/retention/ppermute | solution.py:363
  124.1 15.4 %collective-permute-start.26 = (bf16[128,2048]{1,0:T(8,128)(2,1)}, bf16[128,2048]{1,0:T(8,128)(2,1)}, u32[]{:S(2)}, u32[]{:S(2)}) collective-permute-start(bf16[128,2048]{1,0:T(8,128)(2,1)} %get-tuple-element.341), channel_id=1, source_target_pairs={{0,4},{1,5},{4,8},{5,9},{8,12},{9,13},{12,14},{13,15},{14,10},{15,... | collective-permute-start | bytes 1572872 | tf_op jit(solution)/shard_map/retention/ppermute | solution.py:363
  124.9 15.9 %collective-permute-start.27 = (bf16[128,2048]{1,0:T(8,128)(2,1)}, bf16[128,2048]{1,0:T(8,128)(2,1)}, u32[]{:S(2)}, u32[]{:S(2)}) collective-permute-start(bf16[128,2048]{1,0:T(8,128)(2,1)} %get-tuple-element.342), channel_id=1, source_target_pairs={{0,2},{1,3},{4,0},{5,1},{8,4},{9,5},{12,8},{13,9},{14,12},{15,13},... | collective-permute-start | bytes 1572872 | tf_op jit(solution)/shard_map/retention/ppermute | solution.py:363
  126.3 18.4 %collective-permute-start.32 = (bf16[2048,256]{1,0:T(8,128)(2,1)}, bf16[2048,256]{1,0:T(8,128)(2,1)S(1)}, u32[]{:S(2)}, u32[]{:S(2)}) collective-permute-start(bf16[2048,256]{1,0:T(8,128)(2,1)} %param.23), channel_id=1, source_target_pairs={{0,1},{1,0},{2,3},{3,2},{4,5},{5,4},{6,7},{7,6},{8,9},{9,8},{10,11... | collective-permute-start | bytes 3145736 | tf_op jit(solution)/shard_map/feed_weights/ppermute | solution.py:367
  126.4 35.1 %collective-permute-start.33 = (bf16[256,2048]{1,0:T(8,128)(2,1)}, bf16[256,2048]{1,0:T(8,128)(2,1)S(1)}, u32[]{:S(2)}, u32[]{:S(2)}) collective-permute-start(bf16[256,2048]{1,0:T(8,128)(2,1)} %param.24), channel_id=1, source_target_pairs={{0,1},{1,0},{2,3},{3,2},{4,5},{5,4},{6,7},{7,6},{8,9},{9,8},{10,11... | collective-permute-start | bytes 3145736 | tf_op jit(solution)/shard_map/feed_weights/ppermute | solution.py:367
  126.9 34.8 %collective-permute-start.36 = (bf16[128,2048]{1,0:T(8,128)(2,1)}, bf16[128,2048]{1,0:T(8,128)(2,1)S(1)}, u32[]{:S(2)}, u32[]{:S(2)}) collective-permute-start(bf16[128,2048]{1,0:T(8,128)(2,1)} %copy-done.85), channel_id=1, source_target_pairs={{0,4},{1,5},{4,8},{5,9},{8,12},{9,13},{12,14},{13,15},{14,10},{15,... | collective-permute-start | bytes 1572872 | tf_op jit(solution)/shard_map/gather_out_grad/ppermute | solution.py:363
  139.5 22.1 %collective-permute-start.37 = (bf16[128,2048]{1,0:T(8,128)(2,1)}, bf16[128,2048]{1,0:T(8,128)(2,1)S(1)}, u32[]{:S(2)}, u32[]{:S(2)}) collective-permute-start(bf16[128,2048]{1,0:T(8,128)(2,1)} %copy-done.87), channel_id=1, source_target_pairs={{0,2},{1,3},{4,0},{5,1},{8,4},{9,5},{12,8},{13,9},{14,12},{15,13},... | collective-permute-start | bytes 1572872 | tf_op jit(solution)/shard_map/gather_out_grad/ppermute | solution.py:363
  143.3 16.1 %collective-permute-start.29 = (bf16[128,2048]{1,0:T(8,128)(2,1)S(1)}, bf16[128,2048]{1,0:T(8,128)(2,1)S(1)}, u32[]{:S(2)}, u32[]{:S(2)}) collective-permute-start(bf16[128,2048]{1,0:T(8,128)(2,1)S(1)} %add_convert_fusion.17.refs_0_), channel_id=1, source_target_pairs={{0,2},{1,3},{4,0},{5,1},{8,4},{9,5},{12,8},{13,9},{14,12},{15,13},... | collective-permute-start | bytes 1572872 | tf_op jit(solution)/shard_map/feed_forward/ppermute | solution.py:363
  144.8 14.6 %collective-permute-start.28 = (bf16[128,2048]{1,0:T(8,128)(2,1)S(1)}, bf16[128,2048]{1,0:T(8,128)(2,1)S(1)}, u32[]{:S(2)}, u32[]{:S(2)}) collective-permute-start(bf16[128,2048]{1,0:T(8,128)(2,1)S(1)} %add_convert_fusion.17.refs_0_), channel_id=1, source_target_pairs={{0,4},{1,5},{4,8},{5,9},{8,12},{9,13},{12,14},{13,15},{14,10},{15,... | collective-permute-start | bytes 1572872 | tf_op jit(solution)/shard_map/feed_forward/ppermute | solution.py:363
  159.4 14.9 %collective-permute-start.30 = (bf16[128,2048]{1,0:T(8,128)(2,1)S(1)}, bf16[128,2048]{1,0:T(8,128)(2,1)S(1)}, u32[]{:S(2)}, u32[]{:S(2)}) collective-permute-start(bf16[128,2048]{1,0:T(8,128)(2,1)S(1)} %collective-permute-done.28.refs_1_), channel_id=1, source_target_pairs={{0,4},{1,5},{4,8},{5,9},{8,12},{9,13},{12,14},{13,15},{14,10},{15,... | collective-permute-start | bytes 1572872 | tf_op jit(solution)/shard_map/feed_forward/ppermute | solution.py:363
  159.9 14.9 %collective-permute-start.31 = (bf16[128,2048]{1,0:T(8,128)(2,1)S(1)}, bf16[128,2048]{1,0:T(8,128)(2,1)S(1)}, u32[]{:S(2)}, u32[]{:S(2)}) collective-permute-start(bf16[128,2048]{1,0:T(8,128)(2,1)S(1)} %collective-permute-done.29.refs_2_), channel_id=1, source_target_pairs={{0,2},{1,3},{4,0},{5,1},{8,4},{9,5},{12,8},{13,9},{14,12},{15,13},... | collective-permute-start | bytes 1572872 | tf_op jit(solution)/shard_map/feed_forward/ppermute | solution.py:363
  161.7 18.2 %collective-permute-start.40 = (bf16[128,1024]{1,0:T(8,128)(2,1)S(1)}, bf16[128,1024]{1,0:T(8,128)(2,1)S(1)}, u32[]{:S(2)}, u32[]{:S(2)}) collective-permute-start(bf16[128,1024]{1,0:T(8,128)(2,1)S(1)} %slice.311), channel_id=1, source_target_pairs={{0,4},{1,5},{4,8},{5,9},{8,12},{9,13},{12,14},{13,15},{14,10},{15,... | collective-permute-start | bytes 786440 | tf_op jit(solution)/shard_map/gather_out_grad/ppermute | solution.py:363
  162.2 18.1 %collective-permute-start.41 = (bf16[128,1024]{1,0:T(8,128)(2,1)S(1)}, bf16[128,1024]{1,0:T(8,128)(2,1)S(1)}, u32[]{:S(2)}, u32[]{:S(2)}) collective-permute-start(bf16[128,1024]{1,0:T(8,128)(2,1)S(1)} %slice.312), channel_id=1, source_target_pairs={{0,2},{1,3},{4,0},{5,1},{8,4},{9,5},{12,8},{13,9},{14,12},{15,13},... | collective-permute-start | bytes 786440 | tf_op jit(solution)/shard_map/gather_out_grad/ppermute | solution.py:363
  174.8 13.9 %collective-permute-start.34 = (bf16[128,2048]{1,0:T(8,128)(2,1)S(1)}, bf16[128,2048]{1,0:T(8,128)(2,1)S(1)}, u32[]{:S(2)}, u32[]{:S(2)}) collective-permute-start(bf16[128,2048]{1,0:T(8,128)(2,1)S(1)} %collective-permute-done.30.refs_3_), channel_id=1, source_target_pairs={{0,4},{1,5},{4,8},{5,9},{8,12},{9,13},{12,14},{13,15},{14,10},{15,... | collective-permute-start | bytes 1572872 | tf_op jit(solution)/shard_map/feed_forward/ppermute | solution.py:363
  176.3 12.4 %collective-permute-start.35 = (bf16[128,2048]{1,0:T(8,128)(2,1)S(1)}, bf16[128,2048]{1,0:T(8,128)(2,1)S(1)}, u32[]{:S(2)}, u32[]{:S(2)}) collective-permute-start(bf16[128,2048]{1,0:T(8,128)(2,1)S(1)} %collective-permute-done.31.refs_4_), channel_id=1, source_target_pairs={{0,2},{1,3},{4,0},{5,1},{8,4},{9,5},{12,8},{13,9},{14,12},{15,13},... | collective-permute-start | bytes 1572872 | tf_op jit(solution)/shard_map/feed_forward/ppermute | solution.py:363
  205.7 31.2 %collective-permute-start.50 = (bf16[256,2048]{1,0:T(8,128)(2,1)}, bf16[256,2048]{1,0:T(8,128)(2,1)}, u32[]{:S(2)}, u32[]{:S(2)}) collective-permute-start(bf16[256,2048]{1,0:T(8,128)(2,1)} %convolution_convert_fusion.4), channel_id=1, source_target_pairs={{0,1},{1,0},{2,3},{3,2},{4,5},{5,4},{6,7},{7,6},{8,9},{9,8},{10,11... | collective-permute-start | bytes 3145736 | tf_op jit(solution)/shard_map/scatter_up/down_grad/ppermute | solution.py:367
  208.0 12.4 %collective-permute-start.44 = (bf16[128,2048]{1,0:T(8,128)(2,1)S(1)}, bf16[128,2048]{1,0:T(8,128)(2,1)S(1)}, u32[]{:S(2)}, u32[]{:S(2)}) collective-permute-start(bf16[128,2048]{1,0:T(8,128)(2,1)S(1)} %pad_maximum_fusion.9), channel_id=1, source_target_pairs={{0,4},{1,5},{4,8},{5,9},{8,12},{9,13},{12,14},{13,15},{14,10},{15,... | collective-permute-start | bytes 1572872 | tf_op jit(solution)/shard_map/scatter_up/ppermute | solution.py:363
  226.2 15.4 %collective-permute-start.51 = (bf16[2048,256]{1,0:T(8,128)(2,1)}, bf16[2048,256]{1,0:T(8,128)(2,1)}, u32[]{:S(2)}, u32[]{:S(2)}) collective-permute-start(bf16[2048,256]{1,0:T(8,128)(2,1)} %convolution_convert_fusion.3), channel_id=1, source_target_pairs={{0,1},{1,0},{2,3},{3,2},{4,5},{5,4},{6,7},{7,6},{8,9},{9,8},{10,11... | collective-permute-start | bytes 3145736 | tf_op jit(solution)/shard_map/scatter_up/up_grad/ppermute | solution.py:367
  249.6 12.9 %collective-permute-start.52 = (bf16[128,2048]{1,0:T(8,128)(2,1)}, bf16[128,2048]{1,0:T(8,128)(2,1)}, u32[]{:S(2)}, u32[]{:S(2)}) collective-permute-start(bf16[128,2048]{1,0:T(8,128)(2,1)} %get-tuple-element.432.refs_0_), channel_id=1, source_target_pairs={{0,4},{1,5},{4,8},{5,9},{8,12},{9,13},{12,14},{13,15},{14,10},{15,... | collective-permute-start | bytes 1572872 | tf_op jit(solution)/shard_map/gate_back/ppermute | solution.py:363
  262.5 14.3 %collective-permute-start.54 = (bf16[128,2048]{1,0:T(8,128)(2,1)}, bf16[128,2048]{1,0:T(8,128)(2,1)S(1)}, u32[]{:S(2)}, u32[]{:S(2)}) collective-permute-start(bf16[128,2048]{1,0:T(8,128)(2,1)} %collective-permute-done.52.refs_1_), channel_id=1, source_target_pairs={{0,4},{1,5},{4,8},{5,9},{8,12},{9,13},{12,14},{13,15},{14,10},{15,... | collective-permute-start | bytes 1572872 | tf_op jit(solution)/shard_map/gate_back/ppermute | solution.py:363
  264.1 14.4 %collective-permute-start.55 = (bf16[128,2048]{1,0:T(8,128)(2,1)}, bf16[128,2048]{1,0:T(8,128)(2,1)S(1)}, u32[]{:S(2)}, u32[]{:S(2)}) collective-permute-start(bf16[128,2048]{1,0:T(8,128)(2,1)} %collective-permute-done.53.refs_2_), channel_id=1, source_target_pairs={{0,2},{1,3},{4,0},{5,1},{8,4},{9,5},{12,8},{13,9},{14,12},{15,13},... | collective-permute-start | bytes 1572872 | tf_op jit(solution)/shard_map/gate_back/ppermute | solution.py:363
  278.5 13.8 %collective-permute-start.56 = (bf16[128,2048]{1,0:T(8,128)(2,1)S(1)}, bf16[128,2048]{1,0:T(8,128)(2,1)S(1)}, u32[]{:S(2)}, u32[]{:S(2)}) collective-permute-start(bf16[128,2048]{1,0:T(8,128)(2,1)S(1)} %collective-permute-done.54.refs_3_), channel_id=1, source_target_pairs={{0,4},{1,5},{4,8},{5,9},{8,12},{9,13},{12,14},{13,15},{14,10},{15,... | collective-permute-start | bytes 1572872 | tf_op jit(solution)/shard_map/gate_back/ppermute | solution.py:363
  278.5 13.8 %collective-permute-start.57 = (bf16[128,2048]{1,0:T(8,128)(2,1)S(1)}, bf16[128,2048]{1,0:T(8,128)(2,1)S(1)}, u32[]{:S(2)}, u32[]{:S(2)}) collective-permute-start(bf16[128,2048]{1,0:T(8,128)(2,1)S(1)} %collective-permute-done.55.refs_4_), channel_id=1, source_target_pairs={{0,2},{1,3},{4,0},{5,1},{8,4},{9,5},{12,8},{13,9},{14,12},{15,13},... | collective-permute-start | bytes 1572872 | tf_op jit(solution)/shard_map/gate_back/ppermute | solution.py:363
  280.6 39.1 %collective-permute-start.78 = (bf16[256,2048]{1,0:T(8,128)(2,1)S(1)}, bf16[256,2048]{1,0:T(8,128)(2,1)}, u32[]{:S(2)}, u32[]{:S(2)}) collective-permute-start(bf16[256,2048]{1,0:T(8,128)(2,1)S(1)} %copy-done.107), channel_id=1, source_target_pairs={{0,16},{16,0},{1,17},{17,1},{2,18},{18,2},{3,19},{19,3},{4,20},{20... | collective-permute-start | bytes 3145736 | tf_op jit(solution)/shard_map/down_grad/ppermute | solution.py:614
  288.6 22.0 %collective-permute-start.60 = (bf16[640,512]{1,0:T(8,128)(2,1)S(1)}, bf16[640,512]{1,0:T(8,128)(2,1)S(1)}, u32[]{:S(2)}, u32[]{:S(2)}) collective-permute-start(bf16[640,512]{1,0:T(8,128)(2,1)S(1)} %get-tuple-element.494.refs_7_.refs_0_), channel_id=1, source_target_pairs={{0,1},{1,0},{2,3},{3,2},{4,5},{5,4},{6,7},{7,6},{8,9},{9,8},{10,11... | collective-permute-start | bytes 1966088 | tf_op jit(solution)/shard_map/gate_back/ppermute | solution.py:367
  296.6 14.0 %collective-permute-start.61 = (bf16[256,512]{1,0:T(8,128)(2,1)S(1)}, bf16[256,512]{1,0:T(8,128)(2,1)S(1)}, u32[]{:S(2)}, u32[]{:S(2)}) collective-permute-start(bf16[256,512]{1,0:T(8,128)(2,1)S(1)} %get-tuple-element.484.refs_8_.refs_0_), channel_id=1, source_target_pairs={{0,1},{1,0},{2,3},{3,2},{4,5},{5,4},{6,7},{7,6},{8,9},{9,8},{10,11... | collective-permute-start | bytes 786440 | tf_op jit(solution)/shard_map/gate_back/ppermute | solution.py:367
  308.5 22.2 %collective-permute-start.63 = (bf16[256,2048]{1,0:T(8,128)(2,1)}, bf16[256,2048]{1,0:T(8,128)(2,1)}, u32[]{:S(2)}, u32[]{:S(2)}) collective-permute-start(bf16[256,2048]{1,0:T(8,128)(2,1)} %convolution_convert_fusion.2), channel_id=1, source_target_pairs={{0,1},{1,0},{2,3},{3,2},{4,5},{5,4},{6,7},{7,6},{8,9},{9,8},{10,11... | collective-permute-start | bytes 3145736 | tf_op jit(solution)/shard_map/out_grad/ppermute | solution.py:367
  315.8 13.9 %collective-permute-start.64 = (bf16[256,1024]{1,0:T(8,128)(2,1)S(1)}, bf16[256,1024]{1,0:T(8,128)(2,1)S(1)}, u32[]{:S(2)}, u32[]{:S(2)}) collective-permute-start(bf16[256,1024]{1,0:T(8,128)(2,1)S(1)} %pad_maximum_fusion.11), channel_id=1, source_target_pairs={{0,4},{1,5},{4,8},{5,9},{8,12},{9,13},{12,14},{13,15},{14,10},{15,... | collective-permute-start | bytes 1572872 | tf_op jit(solution)/shard_map/key_back/ppermute | solution.py:363
  316.9 13.7 %collective-permute-start.65 = (bf16[256,1024]{1,0:T(8,128)(2,1)S(1)}, bf16[256,1024]{1,0:T(8,128)(2,1)S(1)}, u32[]{:S(2)}, u32[]{:S(2)}) collective-permute-start(bf16[256,1024]{1,0:T(8,128)(2,1)S(1)} %pad_maximum_fusion.12), channel_id=1, source_target_pairs={{0,2},{1,3},{4,0},{5,1},{8,4},{9,5},{12,8},{13,9},{14,12},{15,13},... | collective-permute-start | bytes 1572872 | tf_op jit(solution)/shard_map/key_back/ppermute | solution.py:363
  319.0 85.5 %collective-permute-start.77 = (bf16[2048,256]{1,0:T(8,128)(2,1)S(1)}, bf16[2048,256]{1,0:T(8,128)(2,1)}, u32[]{:S(2)}, u32[]{:S(2)}) collective-permute-start(bf16[2048,256]{1,0:T(8,128)(2,1)S(1)} %copy-done.106), channel_id=1, source_target_pairs={{0,16},{16,0},{1,17},{17,1},{2,18},{18,2},{3,19},{19,3},{4,20},{20... | collective-permute-start | bytes 3145736 | tf_op jit(solution)/shard_map/up_grad/ppermute | solution.py:614
  346.1 24.1 %collective-permute-start.66 = (bf16[256,2048]{1,0:T(8,128)(2,1)S(1)}, bf16[256,2048]{1,0:T(8,128)(2,1)S(1)}, u32[]{:S(2)}, u32[]{:S(2)}) collective-permute-start(bf16[256,2048]{1,0:T(8,128)(2,1)S(1)} %maximum_maximum_fusion), channel_id=1, source_target_pairs={{0,4},{1,5},{4,8},{5,9},{8,12},{9,13},{12,14},{13,15},{14,10},{15,... | collective-permute-start | bytes 3145736 | tf_op jit(solution)/shard_map/key_back/ppermute | solution.py:363
  346.5 24.2 %collective-permute-start.67 = (bf16[256,2048]{1,0:T(8,128)(2,1)S(1)}, bf16[256,2048]{1,0:T(8,128)(2,1)}, u32[]{:S(2)}, u32[]{:S(2)}) collective-permute-start(bf16[256,2048]{1,0:T(8,128)(2,1)S(1)} %maximum_maximum_fusion.1), channel_id=1, source_target_pairs={{0,2},{1,3},{4,0},{5,1},{8,4},{9,5},{12,8},{13,9},{14,12},{15,13},... | collective-permute-start | bytes 3145736 | tf_op jit(solution)/shard_map/key_back/ppermute | solution.py:363
  348.4 58.4 %collective-permute-start.74 = (bf16[2048,256]{1,0:T(8,128)(2,1)}, bf16[2048,256]{1,0:T(8,128)(2,1)}, u32[]{:S(2)}, u32[]{:S(2)}) collective-permute-start(bf16[2048,256]{1,0:T(8,128)(2,1)} %convolution_convert_fusion.1), channel_id=1, source_target_pairs={{0,1},{1,0},{2,3},{3,2},{4,5},{5,4},{6,7},{7,6},{8,9},{9,8},{10,11... | collective-permute-start | bytes 3145736 | tf_op jit(solution)/shard_map/key_back/gate_grad/ppermute | solution.py:367
  369.0 28.1 %collective-permute-start.70 = (bf16[2048,512]{1,0:T(8,128)(2,1)S(1)}, bf16[2048,512]{1,0:T(8,128)(2,1)S(1)}, u32[]{:S(2)}, u32[]{:S(2)}) collective-permute-start(bf16[2048,512]{1,0:T(8,128)(2,1)S(1)} %convolution_convert_fusion), channel_id=1, source_target_pairs={{0,1},{1,0},{2,3},{3,2},{4,5},{5,4},{6,7},{7,6},{8,9},{9,8},{10,11... | collective-permute-start | bytes 6291464 | tf_op jit(solution)/shard_map/key_back/query_key_value_grad/ppermute | solution.py:367
  373.0 24.0 %collective-permute-start.68 = (bf16[256,2048]{1,0:T(8,128)(2,1)S(1)}, bf16[256,2048]{1,0:T(8,128)(2,1)S(1)}, u32[]{:S(2)}, u32[]{:S(2)}) collective-permute-start(bf16[256,2048]{1,0:T(8,128)(2,1)S(1)} %pad_maximum_fusion.3), channel_id=1, source_target_pairs={{0,4},{1,5},{4,8},{5,9},{8,12},{9,13},{12,14},{13,15},{14,10},{15,... | collective-permute-start | bytes 3145736 | tf_op jit(solution)/shard_map/key_back/ppermute | solution.py:363
  373.4 23.7 %collective-permute-start.69 = (bf16[256,2048]{1,0:T(8,128)(2,1)S(1)}, bf16[256,2048]{1,0:T(8,128)(2,1)S(1)}, u32[]{:S(2)}, u32[]{:S(2)}) collective-permute-start(bf16[256,2048]{1,0:T(8,128)(2,1)S(1)} %pad_maximum_fusion.4), channel_id=1, source_target_pairs={{0,2},{1,3},{4,0},{5,1},{8,4},{9,5},{12,8},{13,9},{14,12},{15,13},... | collective-permute-start | bytes 3145736 | tf_op jit(solution)/shard_map/key_back/ppermute | solution.py:363
  404.5 26.1 %collective-permute-start.76 = (bf16[256,2048]{1,0:T(8,128)(2,1)S(1)}, bf16[256,2048]{1,0:T(8,128)(2,1)S(1)}, u32[]{:S(2)}, u32[]{:S(2)}) collective-permute-start(bf16[256,2048]{1,0:T(8,128)(2,1)S(1)} %copy-done.109), channel_id=1, source_target_pairs={{0,16},{16,0},{1,17},{17,1},{2,18},{18,2},{3,19},{19,3},{4,20},{20... | collective-permute-start | bytes 3145736 | tf_op jit(solution)/shard_map/out_grad/ppermute | solution.py:614
  409.4 43.7 %collective-permute-start.75 = (bf16[2048,256]{1,0:T(8,128)(2,1)S(1)}, bf16[2048,256]{1,0:T(8,128)(2,1)S(1)}, u32[]{:S(2)}, u32[]{:S(2)}) collective-permute-start(bf16[2048,256]{1,0:T(8,128)(2,1)S(1)} %add_convert_fusion.1), channel_id=1, source_target_pairs={{0,16},{16,0},{1,17},{17,1},{2,18},{18,2},{3,19},{19,3},{4,20},{20... | collective-permute-start | bytes 3145736 | tf_op jit(solution)/shard_map/gate_grad/ppermute | solution.py:614
  410.9 20.2 %collective-permute-start.81 = (f32[4,2048]{1,0:T(4,128)S(1)}, f32[4,2048]{1,0:T(4,128)S(1)}, u32[]{:S(2)}, u32[]{:S(2)}) collective-permute-start(f32[4,2048]{1,0:T(4,128)S(1)} %add.414), channel_id=1, source_target_pairs={{0,4},{1,5},{2,6},{3,7},{4,0},{5,1},{6,2},{7,3},{8,12},{9,13},{10,... | collective-permute-start | bytes 98312 | tf_op jit(solution)/shard_map/norm_grads/ppermute | solution.py:831
  414.8 82.4 %collective-permute-start.71 = (bf16[256,2048]{1,0:T(8,128)(2,1)S(1)}, bf16[256,2048]{1,0:T(8,128)(2,1)S(1)}, u32[]{:S(2)}, u32[]{:S(2)}) collective-permute-start(bf16[256,2048]{1,0:T(8,128)(2,1)S(1)} %pad_maximum_fusion.5), channel_id=1, source_target_pairs={{0,4},{1,5},{4,8},{5,9},{8,12},{9,13},{12,14},{13,15},{14,10},{15,... | collective-permute-start | bytes 3145736 | tf_op jit(solution)/shard_map/key_back/ppermute | solution.py:363
  415.8 81.4 %collective-permute-start.72 = (bf16[256,2048]{1,0:T(8,128)(2,1)S(1)}, bf16[256,2048]{1,0:T(8,128)(2,1)S(1)}, u32[]{:S(2)}, u32[]{:S(2)}) collective-permute-start(bf16[256,2048]{1,0:T(8,128)(2,1)S(1)} %pad_maximum_fusion.6), channel_id=1, source_target_pairs={{0,2},{1,3},{4,0},{5,1},{8,4},{9,5},{12,8},{13,9},{14,12},{15,13},... | collective-permute-start | bytes 3145736 | tf_op jit(solution)/shard_map/key_back/ppermute | solution.py:363
  430.6 69.2 %collective-permute-start.73 = (bf16[2048,512]{1,0:T(8,128)(2,1)S(1)}, bf16[2048,512]{1,0:T(8,128)(2,1)S(1)}, u32[]{:S(2)}, u32[]{:S(2)}) collective-permute-start(bf16[2048,512]{1,0:T(8,128)(2,1)S(1)} %add_convert_fusion), channel_id=1, source_target_pairs={{0,16},{16,0},{1,17},{17,1},{2,18},{18,2},{3,19},{19,3},{4,20},{20... | collective-permute-start | bytes 6291464 | tf_op jit(solution)/shard_map/query_key_value_grad/ppermute | solution.py:614
  431.2 21.9 %collective-permute-start.82 = (f32[4,2048]{1,0:T(4,128)S(1)}, f32[4,2048]{1,0:T(4,128)S(1)}, u32[]{:S(2)}, u32[]{:S(2)}) collective-permute-start(f32[4,2048]{1,0:T(4,128)S(1)} %add.415), channel_id=1, source_target_pairs={{0,8},{1,9},{2,10},{3,11},{4,12},{5,13},{6,14},{7,15},{8,0},{9,1},... | collective-permute-start | bytes 98312 | tf_op jit(solution)/shard_map/norm_grads/ppermute | solution.py:831
  453.1 43.5 %collective-permute-start.83 = (f32[4,128]{1,0:T(4,128)S(1)}, f32[4,128]{1,0:T(4,128)S(1)}, u32[]{:S(2)}, u32[]{:S(2)}) collective-permute-start(f32[4,128]{1,0:T(4,128)S(1)} %fusion.70), channel_id=1, source_target_pairs={{0,16},{16,0},{1,17},{17,1},{2,18},{18,2},{3,19},{19,3},{4,20},{20... | collective-permute-start | bytes 6152 | tf_op jit(solution)/shard_map/norm_grads/ppermute | solution.py:819
  (150 other events, 1703.7 us)
